TPU v7x, 32 devices: a whole 2x2x4 slice. The times are simulated.
32 devices in a mesh: grp: 2 (over y), seq: 4 (over z), head: 4 (over x, core).
Axes of the slice: x: 2, y: 2, z: 4, core: 2. Of those that a mesh axis runs over, the one named last changes fastest.
Arguments:
- queries: bfloat16 [8192, 2048], P(('grp', 'seq'), 'head'), parts along dimension 0, may hold values from -16.5 to 16.5
- keys: bfloat16 [8192, 2048], P(('grp', 'seq'), 'head'), parts along dimension 0, may hold values from -16.5 to 16.5
- values: bfloat16 [8192, 2048], P(('grp', 'seq'), 'head'), parts along dimension 0, may hold values from -6 to 6
- pattern: int32 [64, 15], P(('grp', 'seq')), parts along dimension 0, may hold values from 0 to 31, as said below
- out_weight: bfloat16 [2048, 2048], P('head'), may hold values from -0.5 to 0.5
Outputs:
- output: bfloat16 [8192, 2048], P(('grp', 'seq', 'head')), parts along dimension 0
There are 2 independent parts, one for each index of `grp`. A program takes and returns all parts, laid end to end along the dimension named above; an argument that names none is the same for every part. Nothing has to cross between parts.
Inputs may be any that keep to these rules, and one draw needn't show every extreme that they name: `pattern`: row b lists first 7 distinct local blocks (b + o) mod 32 with -8 <= o <= 8, o = 0 always among them, then 8 distinct global blocks that are the same in every row.
All inputs are finite; a program needn't handle non-finite values.
Results may differ from a plain program's by a relative error of at most 0.0057.
Values may be sent and summed in bfloat16 or wider, within the bound.
No kernel may reach another device: no remote copies, remote signals or barrier semaphores. Data moves between devices by JAX's collectives and lax.ppermute only.
A program may use at most 128 MiB of HBM per device.

v0:
```python
import functools
import math

import jax
import jax.numpy as jnp
from jax import lax
from jax.experimental import pallas as pl
from jax.experimental.pallas import tpu as pltpu
from jax.sharding import PartitionSpec as P


DH = 128
BLK = 128
LOC = 7


def shifted(value, axis, steps):
    count = lax.axis_size(axis)
    return lax.ppermute(value, axis, [(i, (i + steps) % count) for i in range(count)])


def swapped(value, axis, mask):
    count = lax.axis_size(axis)
    return lax.ppermute(value, axis, [(i, i ^ mask) for i in range(count)])


def chained(*values):
    return lax.optimization_barrier(values)


def attend_body(count, slots, q_ref, *refs):
    pieces, (o_ref, kv, sems) = refs[:count], refs[count:]
    copies, first = [], 0
    for at, piece in enumerate(pieces):
        rows = pl.ds(first, piece.shape[1])
        copies.append(pltpu.make_async_copy(piece, kv.at[:, rows], sems.at[at]))
        first += piece.shape[1]
    for copy in copies:
        copy.start()
    for copy in copies:
        copy.wait()
    nsel = slots.shape[1]
    factor = math.log2(math.e) / math.sqrt(DH)

    def one_block(i):
        rows = pl.ds(pl.multiple_of(i * BLK, BLK), BLK)
        picked = [
            pl.ds(pl.multiple_of(slots[i, j] * BLK, BLK), BLK) for j in range(nsel)
        ]
        key_set = jnp.concatenate([kv[0, p, :] for p in picked], axis=0)
        scores = lax.dot_general(
            q_ref[rows, :],
            key_set,
            (((1,), (1,)), ((), ())),
            preferred_element_type=jnp.float32,
        )
        peak = jnp.max(scores, axis=1, keepdims=True)
        expo = jnp.exp2(scores * factor - peak * factor).astype(jnp.bfloat16)
        ones = jnp.ones((BLK, DH), jnp.bfloat16)
        value_set = jnp.concatenate(
            [jnp.concatenate([kv[1, p, :], ones], axis=1) for p in picked], axis=0
        )
        mixed = jnp.dot(expo, value_set, preferred_element_type=jnp.float32)
        o_ref[rows, :] = (mixed[:, :DH] / mixed[:, DH:]).astype(o_ref.dtype)

    blocks = q_ref.shape[0] // BLK
    together = math.gcd(blocks, 8)

    def some_blocks(g, carry):
        for u in range(together):
            one_block(g * together + u)
        return carry

    lax.fori_loop(0, blocks // together, some_blocks, 0)


def attend(queries, pieces, slots):
    total = sum(piece.shape[1] for piece in pieces)
    whole = pl.BlockSpec(queries.shape, lambda i, s: (0, 0))
    return pl.pallas_call(
        functools.partial(attend_body, len(pieces)),
        out_shape=jax.ShapeDtypeStruct(queries.shape, queries.dtype),
        grid_spec=pltpu.PrefetchScalarGridSpec(
            num_scalar_prefetch=1,
            grid=(1,),
            in_specs=[whole] + [pl.BlockSpec(memory_space=pl.ANY)] * len(pieces),
            out_specs=whole,
            scratch_shapes=[
                pltpu.VMEM((2, total, DH), queries.dtype),
                pltpu.SemaphoreType.DMA((len(pieces),)),
            ],
        ),
        compiler_params=pltpu.CompilerParams(vmem_limit_bytes=32 << 20),
        name="attend",
    )(slots, queries, *pieces)


def project_body(groups, count, has_part, at, *refs):
    lefts = refs[:groups]
    weights = refs[groups : groups + groups * count]
    rest = refs[groups + groups * count :]
    o_ref = rest[-1]
    total = rest[0][...] if has_part else None
    for g in range(groups):
        left = jnp.concatenate([lefts[g][j] for j in range(count)], axis=1)
        right = jnp.concatenate(
            [weights[g * count + j][...] for j in range(count)], axis=0
        )
        term = jnp.dot(left, right, preferred_element_type=jnp.float32)
        total = term if total is None else total + term
    o_ref[...] = total.astype(o_ref.dtype)


def project(lefts, weights, origins, part, dtype):
    groups, count = len(lefts), len(weights)
    _, rows, width = lefts[0].shape
    columns = weights[0].shape[1]
    tile = min(512, columns)

    def weight_spec(g):
        return pl.BlockSpec((width, tile), lambda n, at: (at[g], n))

    in_specs = [pl.BlockSpec((count, rows, width), lambda n, at: (0, 0, 0))] * groups
    operands = list(lefts)
    for g in range(groups):
        for weight in weights:
            in_specs.append(weight_spec(g))
            operands.append(weight)
    tile_spec = pl.BlockSpec((rows, tile), lambda n, at: (0, n))
    if part is not None:
        in_specs.append(tile_spec)
        operands.append(part)
    return pl.pallas_call(
        functools.partial(project_body, groups, count, part is not None),
        out_shape=jax.ShapeDtypeStruct((rows, columns), dtype),
        grid_spec=pltpu.PrefetchScalarGridSpec(
            num_scalar_prefetch=1,
            grid=(columns // tile,),
            in_specs=in_specs,
            out_specs=tile_spec,
        ),
        compiler_params=pltpu.CompilerParams(vmem_limit_bytes=32 << 20),
        name="project",
    )(jnp.stack(origins), *operands)


def by_heads(queries, keys, values, pattern, out_weight):
    qblocks = pattern.shape[0]
    rows, feat = queries.shape
    seq, heads = lax.axis_size("seq"), lax.axis_size("head")
    me, head = lax.axis_index("seq"), lax.axis_index("head")
    width = feat // seq
    share = rows // heads
    order = plan_of(seq)

    def columns_for(array, mask):
        return lax.dynamic_slice_in_dim(array, (me ^ mask) * width, width, axis=1)

    def pair_for(mask):
        return jnp.stack([columns_for(keys, mask), columns_for(values, mask)])

    pairs = {0: pair_for(0)}
    patterns, asked = {0: pattern}, {0: columns_for(queries, 0)}
    for mask in order:
        pairs[mask] = swapped(pair_for(mask), "seq", mask)
        patterns[mask] = swapped(pattern, "seq", mask)
        asked[mask] = swapped(columns_for(queries, mask), "seq", mask)
    weights = {0: out_weight}
    for hop in far_first(heads):
        for other in list(weights):
            weights[other ^ hop] = swapped(weights[other], "head", hop)

    pieces = [pairs[mask] for mask in range(seq)]
    ready, before = {}, None
    for mask in order + [0]:
        ids = patterns[mask]
        slots = ((ids // qblocks) ^ me) * qblocks + ids % qblocks
        if before is not None:
            slots, before = chained(slots, before)
        mixed = before = attend(asked[mask], pieces, slots)
        mine = []
        for hop in range(heads):
            block = lax.dynamic_slice_in_dim(mixed, (head ^ hop) * share, share, axis=0)
            mine.append(swapped(block, "head", hop) if hop else block)
        stacked = jnp.stack(mine)
        ready[mask] = swapped(stacked, "seq", mask) if mask else stacked
    tail = order[-1]
    early = [mask for mask in [0] + order if mask != tail]
    ordered = [weights[hop] for hop in range(heads)]
    part = project(
        [ready[mask] for mask in early],
        ordered,
        [me ^ mask for mask in early],
        None,
        jnp.float32,
    )
    return project([ready[tail]], ordered, [me ^ tail], part, queries.dtype)


def plan_of(seq):
    return [seq - 1] + list(range(1, seq - 1))


def far_first(heads):
    hop = 1
    while hop < heads:
        hop *= 2
    hops = []
    while hop > 1:
        hop //= 2
        hops.append(hop)
    return hops


def by_rows(queries, keys, values, pattern, out_weight):
    qblocks = pattern.shape[0]
    _, feat = queries.shape
    total = qblocks * lax.axis_size("seq")
    me = lax.axis_index("seq")
    own = jnp.stack([keys, values])
    nearby = [shifted(own, "seq", 1), own, shifted(own, "seq", -1)]
    ids = pattern[0, LOC:]
    local = ids - me * qblocks
    owned = (local >= 0) & (local < qblocks)
    blocks = own.reshape(2, qblocks, BLK, feat)
    picked = jnp.take(blocks, jnp.clip(local, 0, qblocks - 1), axis=1)
    picked = jnp.where(owned[None, :, None, None], picked, jnp.zeros((), picked.dtype))
    distant = lax.psum(picked, "seq").reshape(2, -1, feat)
    near_slots = (pattern[:, :LOC] - (me - 1) * qblocks) % total
    far_slots = jnp.broadcast_to(
        3 * qblocks + jnp.arange(ids.shape[0], dtype=jnp.int32), (qblocks, ids.shape[0])
    )
    slots = jnp.concatenate([near_slots, far_slots], axis=1)
    mixed = []
    for first in range(0, feat, DH):
        columns = slice(first, first + DH)
        pieces = [piece[:, :, columns] for piece in nearby + [distant]]
        mixed.append(attend(queries[:, columns], pieces, slots))
    attended = jnp.concatenate(mixed, axis=1)
    regrouped = lax.all_to_all(attended, "head", split_axis=0, concat_axis=1, tiled=True)
    result = jnp.dot(
        regrouped,
        lax.all_gather(out_weight, "head", axis=0, tiled=True),
        preferred_element_type=jnp.float32,
    )
    return result.astype(queries.dtype)


def heads_split(feat, seq):
    return feat == seq * DH and seq & (seq - 1) == 0


def per_device(queries, keys, values, pattern, out_weight):
    if heads_split(queries.shape[1], lax.axis_size("seq")):
        return by_heads(queries, keys, values, pattern, out_weight)
    return by_rows(queries, keys, values, pattern, out_weight)


def solution(mesh):
    placed = (
        P(("grp", "seq"), "head"),
        P(("grp", "seq"), "head"),
        P(("grp", "seq"), "head"),
        P(("grp", "seq"), None),
        P("head", None),
    )
    step = jax.shard_map(
        per_device,
        mesh=mesh,
        in_specs=placed,
        out_specs=P(("grp", "seq", "head"), None),
        check_vma=False,
    )

    def run(queries, keys, values, pattern, out_weight):
        feat = queries.shape[1] // mesh.shape["head"]
        whole = step
        if heads_split(feat, mesh.shape["seq"]):
            whole = step
        return whole(queries, keys, values, pattern, out_weight)

    return run
```

profile of v0, /device:TPU:0, one launch (start us, length us, event | category | flops | bytes accessed | tf_op | source)
XLA Modules:
  0.0 144.1 jit_solution(14338061477807066851)
XLA Ops:
  0.0 3.0 %collective-permute-start.14 = (bf16[512,2048]{1,0:T(8,128)(2,1)}, bf16[512,2048]{1,0:T(8,128)(2,1)S(1)}, u32[]{:S(2)}, u32[]{:S(2)}) collective-permute-start(bf16[512,2048]{1,0:T(8,128)(2,1)} %refs_1_.1), channel_id=1, source_target_pairs={{0,2},{1,3},{2,0},{3,1},{4,6},{5,7},{6,4},{7,5},{8,10},{9,11},{10,... | collective-permute-start | bytes 6291464 | tf_op jit(solution)/shard_map/ppermute | solution.py:24
  3.0 1.6 %collective-permute-start.1 = (s32[8,15]{1,0:T(8,128)}, s32[8,15]{1,0:T(8,128)S(1)}, u32[]{:S(2)}, u32[]{:S(2)}) collective-permute-start(s32[8,15]{1,0:T(8,128)} %param.8), channel_id=1, source_target_pairs={{0,4},{4,0},{8,12},{12,8},{1,5},{5,1},{9,13},{13,9},{2,6},{6,2},{1... | collective-permute-start | bytes 1448 | tf_op jit(solution)/shard_map/ppermute | solution.py:24
  4.5 2.6 %collective-permute-start = (s32[8,15]{1,0:T(8,128)}, s32[8,15]{1,0:T(8,128)S(1)}, u32[]{:S(2)}, u32[]{:S(2)}) collective-permute-start(s32[8,15]{1,0:T(8,128)} %param.8), channel_id=1, source_target_pairs={{0,8},{4,12},{8,0},{12,4},{1,9},{5,13},{9,1},{13,5},{2,10},{6,14},... | collective-permute-start | bytes 1448 | tf_op jit(solution)/shard_map/ppermute | solution.py:24
  7.1 0.2 collective-permute-start.2
  7.4 0.0 collective-permute-start.13
  7.4 1.7 %dynamic-slice_bitcast_fusion = (bf16[1,1024,128]{2,1,0:T(8,128)(2,1)S(1)}, bf16[1,1024,128]{2,1,0:T(8,128)(2,1)S(1)}, bf16[1,1024,128]{2,1,0:T(8,128)(2,1)S(1)}...) fusion(bf16[1024,512]{1,0:T(8,128)(2,1)} %param.7, ...), kind=kLoop, calls=%fused_computation.8 | loop fusion | bytes 4194320 | tf_op jit(solution)/shard_map/stack | solution.py:160
  9.1 0.0 copy-start.1
  9.1 0.9 pad_maximum_fusion.3
  10.0 0.8 pad_maximum_fusion.1
  10.8 1.0 constant_dynamic-slice_fusion.9
  11.8 0.8 pad_maximum_fusion.2
  12.6 0.0 collective-permute-done.1
  12.6 3.6 %collective-permute-start.3 = (bf16[1024,128]{1,0:T(8,128)(2,1)}, bf16[1024,128]{1,0:T(8,128)(2,1)}, u32[]{:S(2)}, u32[]{:S(2)}) collective-permute-start(bf16[1024,128]{1,0:T(8,128)(2,1)} %get-tuple-element.13), channel_id=1, source_target_pairs={{0,12},{4,8},{8,4},{12,0},{1,13},{5,9},{9,5},{13,1},{2,14},{6,10},... | collective-permute-start | bytes 786440 | tf_op jit(solution)/shard_map/ppermute | solution.py:24
  16.2 0.0 collective-permute-done
  16.2 0.0 collective-permute-start.5
  16.2 0.0 collective-permute-done.2
  16.2 0.8 collective-permute-start.4
  17.0 31.8 %collective-permute-done.14.refs_5_.refs_9_.refs_13_.refs_3_ = bf16[512,2048]{1,0:T(8,128)(2,1)S(1)} collective-permute-done((bf16[512,2048]{1,0:T(8,128)(2,1)}, bf16[512,2048]{1,0:T(8,128)(2,1)S(1)}, u32[]{:S(2)}, u32[]{:S(2)}) %collective-permute-start.14) | collective-permute-done | bytes 2097184 | tf_op jit(solution)/shard_map/ppermute | solution.py:24
  48.8 0.0 collective-permute-start.15
  48.8 0.1 pad_maximum_fusion.refs_0_
  48.9 0.0 collective-permute-done.3.q_ref
  48.9 3.9 %collective-permute-start.6 = (bf16[2,1024,128]{2,1,0:T(8,128)(2,1)}, bf16[2,1024,128]{2,1,0:T(8,128)(2,1)S(1)}, u32[]{:S(2)}, u32[]{:S(2)}) collective-permute-start(bf16[2,1024,128]{2,1,0:T(8,128)(2,1)} %pad_maximum_fusion.3), channel_id=1, source_target_pairs={{0,12},{4,8},{8,4},{12,0},{1,13},{5,9},{9,5},{13,1},{2,14},{6,10},... | collective-permute-start | bytes 1572872 | tf_op jit(solution)/shard_map/ppermute | solution.py:24
  52.9 0.0 collective-permute-done.5.refs_2_
  52.9 0.1 collective-permute-start.7
  53.0 0.6 collective-permute-start.8
  53.6 12.4 %collective-permute-done.6.refs_3_ = bf16[2,1024,128]{2,1,0:T(8,128)(2,1)S(1)} collective-permute-done((bf16[2,1024,128]{2,1,0:T(8,128)(2,1)}, bf16[2,1024,128]{2,1,0:T(8,128)(2,1)S(1)}, u32[]{:S(2)}, u32[]{:S(2)}) %collective-permute-start.6) | collective-permute-done | bytes 524320 | tf_op jit(solution)/shard_map/ppermute | solution.py:24
  65.9 5.8 %attend.4 = bf16[1024,128]{1,0:T(8,128)(2,1)S(1)} custom-call(s32[8,15]{1,0:T(8,128)S(1)} %fusion.8.slots, bf16[1024,128]{1,0:T(8,128)(2,1)} %collective-permute-done.3.q_ref, bf16[2,1024,128]{2,1,0:T(8,128)(2,1)S(1)} %pad_maximum_fusion.refs_0_, bf16[2,1024,128]{2,1,0:T(8,128)(2,1)} %collective-permute-done.4.refs_1_, ...), custom_call_target="tpu_custom_call" | custom-call | tf_op jit(solution)/shard_map/attend/pallas_call | solution.py:80
  71.7 0.0 collective-permute-done.7.q_ref
  71.7 4.8 %attend.5 = bf16[1024,128]{1,0:T(8,128)(2,1)S(1)} custom-call(s32[8,15]{1,0:T(8,128)S(1)} %fusion.5.slots, bf16[1024,128]{1,0:T(8,128)(2,1)S(1)} %collective-permute-done.7.q_ref, bf16[2,1024,128]{2,1,0:T(8,128)(2,1)S(1)} %pad_maximum_fusion.refs_0_, bf16[2,1024,128]{2,1,0:T(8,128)(2,1)} %collective-permute-done.4.refs_1_, ...), custom_call_target="tpu_custom_call" | custom-call | tf_op jit(solution)/shard_map/attend/pallas_call | solution.py:80
  76.5 10.7 %collective-permute-done.8.q_ref = bf16[1024,128]{1,0:T(8,128)(2,1)S(1)} collective-permute-done((bf16[1024,128]{1,0:T(8,128)(2,1)}, bf16[1024,128]{1,0:T(8,128)(2,1)S(1)}, u32[]{:S(2)}, u32[]{:S(2)}) %collective-permute-start.8) | collective-permute-done | bytes 262176 | tf_op jit(solution)/shard_map/ppermute | solution.py:24
  87.3 4.9 %attend.6 = bf16[1024,128]{1,0:T(8,128)(2,1)S(1)} custom-call(s32[8,15]{1,0:T(8,128)S(1)} %fusion.2.slots, bf16[1024,128]{1,0:T(8,128)(2,1)S(1)} %collective-permute-done.8.q_ref, bf16[2,1024,128]{2,1,0:T(8,128)(2,1)S(1)} %pad_maximum_fusion.refs_0_, bf16[2,1024,128]{2,1,0:T(8,128)(2,1)} %collective-permute-done.4.refs_1_, ...), custom_call_target="tpu_custom_call" | custom-call | tf_op jit(solution)/shard_map/attend/pallas_call | solution.py:80
  92.1 4.8 %attend.7 = bf16[1024,128]{1,0:T(8,128)(2,1)S(1)} custom-call(s32[8,15]{1,0:T(8,128)S(1)} %fusion.11.slots, bf16[1024,128]{1,0:T(8,128)(2,1)S(1)} %get-tuple-element.11.q_ref, bf16[2,1024,128]{2,1,0:T(8,128)(2,1)S(1)} %pad_maximum_fusion.refs_0_, bf16[2,1024,128]{2,1,0:T(8,128)(2,1)} %collective-permute-done.4.refs_1_, ...), custom_call_target="tpu_custom_call" | custom-call | tf_op jit(solution)/shard_map/attend/pallas_call | solution.py:80
  97.0 0.0 copy-start
  97.0 0.8 collective-permute-start.18
  97.8 0.8 collective-permute-start.17
  98.7 1.5 %collective-permute-start.25 = (bf16[256,128]{1,0:T(8,128)(2,1)S(1)}, bf16[256,128]{1,0:T(8,128)(2,1)S(1)}, u32[]{:S(2)}, u32[]{:S(2)}) collective-permute-start(bf16[256,128]{1,0:T(8,128)(2,1)S(1)} %get-tuple-element.24), channel_id=1, source_target_pairs={{0,3},{1,2},{2,1},{3,0},{4,7},{5,6},{6,5},{7,4},{8,11},{9,10},{10,... | collective-permute-start | bytes 196616 | tf_op jit(solution)/shard_map/ppermute | solution.py:24
  100.2 1.3 collective-permute-done.18
  101.4 1.5 %collective-permute-start.24 = (bf16[256,128]{1,0:T(8,128)(2,1)S(1)}, bf16[256,128]{1,0:T(8,128)(2,1)S(1)}, u32[]{:S(2)}, u32[]{:S(2)}) collective-permute-start(bf16[256,128]{1,0:T(8,128)(2,1)S(1)} %get-tuple-element.25), channel_id=1, source_target_pairs={{0,2},{1,3},{2,0},{3,1},{4,6},{5,7},{6,4},{7,5},{8,10},{9,11},{10,... | collective-permute-start | bytes 196616 | tf_op jit(solution)/shard_map/ppermute | solution.py:24
  103.0 0.0 collective-permute-done.17
  103.0 1.2 collective-permute-done.25
  104.2 0.9 collective-permute-start.21
  105.2 0.5 collective-permute-done.24
  105.7 1.5 %collective-permute-start.20 = (bf16[256,128]{1,0:T(8,128)(2,1)S(1)}, bf16[256,128]{1,0:T(8,128)(2,1)S(1)}, u32[]{:S(2)}, u32[]{:S(2)}) collective-permute-start(bf16[256,128]{1,0:T(8,128)(2,1)S(1)} %get-tuple-element.29), channel_id=1, source_target_pairs={{0,2},{1,3},{2,0},{3,1},{4,6},{5,7},{6,4},{7,5},{8,10},{9,11},{10,... | collective-permute-start | bytes 196616 | tf_op jit(solution)/shard_map/ppermute | solution.py:24
  107.3 1.1 collective-permute-done.21
  108.3 1.3 collective-permute-start.11
  109.6 0.4 collective-permute-done.20
  110.0 1.5 %collective-permute-start.10 = (bf16[256,128]{1,0:T(8,128)(2,1)S(1)}, bf16[256,128]{1,0:T(8,128)(2,1)S(1)}, u32[]{:S(2)}, u32[]{:S(2)}) collective-permute-start(bf16[256,128]{1,0:T(8,128)(2,1)S(1)} %get-tuple-element.37), channel_id=1, source_target_pairs={{0,2},{1,3},{2,0},{3,1},{4,6},{5,7},{6,4},{7,5},{8,10},{9,11},{10,... | collective-permute-start | bytes 196616 | tf_op jit(solution)/shard_map/ppermute | solution.py:24
  111.5 0.0 collective-permute-start.9
  111.6 0.6 collective-permute-done.11
  112.1 0.5 collective-permute-start.16
  112.7 1.6 %collective-permute-done.10 = bf16[256,128]{1,0:T(8,128)(2,1)S(1)} collective-permute-done((bf16[256,128]{1,0:T(8,128)(2,1)S(1)}, bf16[256,128]{1,0:T(8,128)(2,1)S(1)}, u32[]{:S(2)}, u32[]{:S(2)}) %collective-permute-start.10) | collective-permute-done | bytes 65568 | tf_op jit(solution)/shard_map/ppermute | solution.py:24
  114.3 2.5 %collective-permute-start.22 = (bf16[4,256,128]{2,1,0:T(8,128)(2,1)S(1)}, bf16[4,256,128]{2,1,0:T(8,128)(2,1)S(1)}, u32[]{:S(2)}, u32[]{:S(2)}) collective-permute-start(bf16[4,256,128]{2,1,0:T(8,128)(2,1)S(1)} %pad_maximum_fusion.6), channel_id=1, source_target_pairs={{0,12},{4,8},{8,4},{12,0},{1,13},{5,9},{9,5},{13,1},{2,14},{6,10},... | collective-permute-start | bytes 786440 | tf_op jit(solution)/shard_map/ppermute | solution.py:24
  116.8 0.0 collective-permute-done.9
  116.8 5.1 %collective-permute-start.26 = (bf16[4,256,128]{2,1,0:T(8,128)(2,1)S(1)}, bf16[4,256,128]{2,1,0:T(8,128)(2,1)S(1)}, u32[]{:S(2)}, u32[]{:S(2)}) collective-permute-start(bf16[4,256,128]{2,1,0:T(8,128)(2,1)S(1)} %pad_maximum_fusion.7), channel_id=1, source_target_pairs={{0,4},{4,0},{8,12},{12,8},{1,5},{5,1},{9,13},{13,9},{2,6},{6,2},{1... | collective-permute-start | bytes 786440 | tf_op jit(solution)/shard_map/ppermute | solution.py:24
  122.0 0.0 collective-permute-done.16
  122.0 0.1 collective-permute-start.12
  122.1 0.1 pad_add_fusion.at
  122.2 1.8 %collective-permute-done.22.refs_1_ = bf16[4,256,128]{2,1,0:T(8,128)(2,1)S(1)} collective-permute-done((bf16[4,256,128]{2,1,0:T(8,128)(2,1)S(1)}, bf16[4,256,128]{2,1,0:T(8,128)(2,1)S(1)}, u32[]{:S(2)}, u32[]{:S(2)}) %collective-permute-start.22) | collective-permute-done | bytes 262176 | tf_op jit(solution)/shard_map/ppermute | solution.py:24
  124.0 4.9 %collective-permute-done.26.refs_2_ = bf16[4,256,128]{2,1,0:T(8,128)(2,1)S(1)} collective-permute-done((bf16[4,256,128]{2,1,0:T(8,128)(2,1)S(1)}, bf16[4,256,128]{2,1,0:T(8,128)(2,1)S(1)}, u32[]{:S(2)}, u32[]{:S(2)}) %collective-permute-start.26) | collective-permute-done | bytes 262176 | tf_op jit(solution)/shard_map/ppermute | solution.py:24
  128.9 0.0 collective-permute-done.13.refs_4_.refs_8_.refs_12_.refs_2_
  128.9 0.0 collective-permute-done.15.refs_6_.refs_10_.refs_14_.refs_4_
  128.9 5.2 %project.2.refs_5_ = f32[256,2048]{1,0:T(8,128)S(1)} custom-call(s32[3]{0:T(128)S(1)} %pad_add_fusion.at, bf16[4,256,128]{2,1,0:T(8,128)(2,1)S(1)} %pad_maximum_fusion.5.refs_0_, bf16[4,256,128]{2,1,0:T(8,128)(2,1)S(1)} %collective-permute-done.22.refs_1_, bf16[4,256,128]{2,1,0:T(8,128)(2,1)S(1)} %collective-permute-done.26.refs_2_, ...), custom_call_target="tpu_custom_call" | custom-call | tf_op jit(solution)/shard_map/project/pallas_call | solution.py:133
  134.1 6.0 %collective-permute-done.12.refs_0_ = bf16[4,256,128]{2,1,0:T(8,128)(2,1)S(1)} collective-permute-done((bf16[4,256,128]{2,1,0:T(8,128)(2,1)S(1)}, bf16[4,256,128]{2,1,0:T(8,128)(2,1)S(1)}, u32[]{:S(2)}, u32[]{:S(2)}) %collective-permute-start.12) | collective-permute-done | bytes 262176 | tf_op jit(solution)/shard_map/ppermute | solution.py:24
  140.1 4.0 %project.3 = bf16[256,2048]{1,0:T(8,128)(2,1)} custom-call(s32[1]{0:T(128)} %bitcast.at, bf16[4,256,128]{2,1,0:T(8,128)(2,1)S(1)} %collective-permute-done.12.refs_0_, bf16[512,2048]{1,0:T(8,128)(2,1)S(1)} %copy-done, bf16[512,2048]{1,0:T(8,128)(2,1)} %collective-permute-done.13.refs_4_.refs_8_.refs_12_.refs_2_, ...), custom_call_target="tpu_custom_call" | custom-call | tf_op jit(solution)/shard_map/project/pallas_call | solution.py:133
  (21 shorter events, 0.3 us)
Async XLA Ops:
  0.0 48.8 %collective-permute-start.14 = (bf16[512,2048]{1,0:T(8,128)(2,1)}, bf16[512,2048]{1,0:T(8,128)(2,1)S(1)}, u32[]{:S(2)}, u32[]{:S(2)}) collective-permute-start(bf16[512,2048]{1,0:T(8,128)(2,1)} %refs_1_.1), channel_id=1, source_target_pairs={{0,2},{1,3},{2,0},{3,1},{4,6},{5,7},{6,4},{7,5},{8,10},{9,11},{10,... | collective-permute-start | bytes 6291464 | tf_op jit(solution)/shard_map/ppermute | solution.py:24
  3.0 9.6 %collective-permute-start.1 = (s32[8,15]{1,0:T(8,128)}, s32[8,15]{1,0:T(8,128)S(1)}, u32[]{:S(2)}, u32[]{:S(2)}) collective-permute-start(s32[8,15]{1,0:T(8,128)} %param.8), channel_id=1, source_target_pairs={{0,4},{4,0},{8,12},{12,8},{1,5},{5,1},{9,13},{13,9},{2,6},{6,2},{1... | collective-permute-start | bytes 1448 | tf_op jit(solution)/shard_map/ppermute | solution.py:24
  4.5 11.7 %collective-permute-start = (s32[8,15]{1,0:T(8,128)}, s32[8,15]{1,0:T(8,128)S(1)}, u32[]{:S(2)}, u32[]{:S(2)}) collective-permute-start(s32[8,15]{1,0:T(8,128)} %param.8), channel_id=1, source_target_pairs={{0,8},{4,12},{8,0},{12,4},{1,9},{5,13},{9,1},{13,5},{2,10},{6,14},... | collective-permute-start | bytes 1448 | tf_op jit(solution)/shard_map/ppermute | solution.py:24
  7.1 9.1 %collective-permute-start.2 = (s32[8,15]{1,0:T(8,128)}, s32[8,15]{1,0:T(8,128)S(1)}, u32[]{:S(2)}, u32[]{:S(2)}) collective-permute-start(s32[8,15]{1,0:T(8,128)} %param.8), channel_id=1, source_target_pairs={{0,12},{4,8},{8,4},{12,0},{1,13},{5,9},{9,5},{13,1},{2,14},{6,10},... | collective-permute-start | bytes 1448 | tf_op jit(solution)/shard_map/ppermute | solution.py:24
  7.4 121.5 %collective-permute-start.13 = (bf16[512,2048]{1,0:T(8,128)(2,1)}, bf16[512,2048]{1,0:T(8,128)(2,1)}, u32[]{:S(2)}, u32[]{:S(2)}) collective-permute-start(bf16[512,2048]{1,0:T(8,128)(2,1)} %refs_1_.1), channel_id=1, source_target_pairs={{0,1},{1,0},{2,3},{3,2},{4,5},{5,4},{6,7},{7,6},{8,9},{9,8},{10,11... | collective-permute-start | bytes 6291464 | tf_op jit(solution)/shard_map/ppermute | solution.py:24
  9.1 1.7 %copy-start.1 = (bf16[1024,512]{1,0:T(8,128)(2,1)S(1)}, bf16[1024,512]{1,0:T(8,128)(2,1)}, u32[]{:S(2)}) copy-start(bf16[1024,512]{1,0:T(8,128)(2,1)} %param.5) | copy-start | bytes 3145732
  10.8 38.1 %copy-start.2 = (s32[8,15]{1,0:T(8,128)S(1)}, s32[8,15]{1,0:T(8,128)}, u32[]{:S(2)}) copy-start(s32[8,15]{1,0:T(8,128)} %param.8) | copy-start | bytes 1444
  12.6 36.3 %collective-permute-start.3 = (bf16[1024,128]{1,0:T(8,128)(2,1)}, bf16[1024,128]{1,0:T(8,128)(2,1)}, u32[]{:S(2)}, u32[]{:S(2)}) collective-permute-start(bf16[1024,128]{1,0:T(8,128)(2,1)} %get-tuple-element.13), channel_id=1, source_target_pairs={{0,12},{4,8},{8,4},{12,0},{1,13},{5,9},{9,5},{13,1},{2,14},{6,10},... | collective-permute-start | bytes 786440 | tf_op jit(solution)/shard_map/ppermute | solution.py:24
  16.2 36.6 %collective-permute-start.5 = (bf16[2,1024,128]{2,1,0:T(8,128)(2,1)}, bf16[2,1024,128]{2,1,0:T(8,128)(2,1)S(1)}, u32[]{:S(2)}, u32[]{:S(2)}) collective-permute-start(bf16[2,1024,128]{2,1,0:T(8,128)(2,1)} %pad_maximum_fusion.2), channel_id=1, source_target_pairs={{0,8},{4,12},{8,0},{12,4},{1,9},{5,13},{9,1},{13,5},{2,10},{6,14},... | collective-permute-start | bytes 1572872 | tf_op jit(solution)/shard_map/ppermute | solution.py:24
  16.2 36.7 %collective-permute-start.4 = (bf16[2,1024,128]{2,1,0:T(8,128)(2,1)}, bf16[2,1024,128]{2,1,0:T(8,128)(2,1)}, u32[]{:S(2)}, u32[]{:S(2)}) collective-permute-start(bf16[2,1024,128]{2,1,0:T(8,128)(2,1)} %pad_maximum_fusion.1), channel_id=1, source_target_pairs={{0,4},{4,0},{8,12},{12,8},{1,5},{5,1},{9,13},{13,9},{2,6},{6,2},{1... | collective-permute-start | bytes 1572872 | tf_op jit(solution)/shard_map/ppermute | solution.py:24
  48.8 80.1 %collective-permute-start.15 = (bf16[512,2048]{1,0:T(8,128)(2,1)S(1)}, bf16[512,2048]{1,0:T(8,128)(2,1)}, u32[]{:S(2)}, u32[]{:S(2)}) collective-permute-start(bf16[512,2048]{1,0:T(8,128)(2,1)S(1)} %collective-permute-done.14.refs_5_.refs_9_.refs_13_.refs_3_), channel_id=1, source_target_pairs={{0,1},{1,0},{2,3},{3,2},{4,5},{5,4},{6,7},{7,6},{8,9},{9,8},{10,11... | collective-permute-start | bytes 6291464 | tf_op jit(solution)/shard_map/ppermute | solution.py:24
  48.9 17.0 %collective-permute-start.6 = (bf16[2,1024,128]{2,1,0:T(8,128)(2,1)}, bf16[2,1024,128]{2,1,0:T(8,128)(2,1)S(1)}, u32[]{:S(2)}, u32[]{:S(2)}) collective-permute-start(bf16[2,1024,128]{2,1,0:T(8,128)(2,1)} %pad_maximum_fusion.3), channel_id=1, source_target_pairs={{0,12},{4,8},{8,4},{12,0},{1,13},{5,9},{9,5},{13,1},{2,14},{6,10},... | collective-permute-start | bytes 1572872 | tf_op jit(solution)/shard_map/ppermute | solution.py:24
  52.9 18.8 %collective-permute-start.7 = (bf16[1024,128]{1,0:T(8,128)(2,1)}, bf16[1024,128]{1,0:T(8,128)(2,1)S(1)}, u32[]{:S(2)}, u32[]{:S(2)}) collective-permute-start(bf16[1024,128]{1,0:T(8,128)(2,1)} %get-tuple-element.12), channel_id=1, source_target_pairs={{0,4},{4,0},{8,12},{12,8},{1,5},{5,1},{9,13},{13,9},{2,6},{6,2},{1... | collective-permute-start | bytes 786440 | tf_op jit(solution)/shard_map/ppermute | solution.py:24
  53.0 34.3 %collective-permute-start.8 = (bf16[1024,128]{1,0:T(8,128)(2,1)}, bf16[1024,128]{1,0:T(8,128)(2,1)S(1)}, u32[]{:S(2)}, u32[]{:S(2)}) collective-permute-start(bf16[1024,128]{1,0:T(8,128)(2,1)} %get-tuple-element.14), channel_id=1, source_target_pairs={{0,8},{4,12},{8,0},{12,4},{1,9},{5,13},{9,1},{13,5},{2,10},{6,14},... | collective-permute-start | bytes 786440 | tf_op jit(solution)/shard_map/ppermute | solution.py:24
  97.0 31.9 %copy-start = (bf16[512,2048]{1,0:T(8,128)(2,1)S(1)}, bf16[512,2048]{1,0:T(8,128)(2,1)}, u32[]{:S(2)}) copy-start(bf16[512,2048]{1,0:T(8,128)(2,1)} %refs_1_.1) | copy-start | bytes 6291460
  97.0 4.4 %collective-permute-start.18 = (bf16[256,128]{1,0:T(8,128)(2,1)S(1)}, bf16[256,128]{1,0:T(8,128)(2,1)S(1)}, u32[]{:S(2)}, u32[]{:S(2)}) collective-permute-start(bf16[256,128]{1,0:T(8,128)(2,1)S(1)} %get-tuple-element.32), channel_id=1, source_target_pairs={{0,3},{1,2},{2,1},{3,0},{4,7},{5,6},{6,5},{7,4},{8,11},{9,10},{10,... | collective-permute-start | bytes 196616 | tf_op jit(solution)/shard_map/ppermute | solution.py:24
  97.8 5.1 %collective-permute-start.17 = (bf16[256,128]{1,0:T(8,128)(2,1)S(1)}, bf16[256,128]{1,0:T(8,128)(2,1)S(1)}, u32[]{:S(2)}, u32[]{:S(2)}) collective-permute-start(bf16[256,128]{1,0:T(8,128)(2,1)S(1)} %get-tuple-element.33), channel_id=1, source_target_pairs={{0,2},{1,3},{2,0},{3,1},{4,6},{5,7},{6,4},{7,5},{8,10},{9,11},{10,... | collective-permute-start | bytes 196616 | tf_op jit(solution)/shard_map/ppermute | solution.py:24
  98.7 5.6 %collective-permute-start.25 = (bf16[256,128]{1,0:T(8,128)(2,1)S(1)}, bf16[256,128]{1,0:T(8,128)(2,1)S(1)}, u32[]{:S(2)}, u32[]{:S(2)}) collective-permute-start(bf16[256,128]{1,0:T(8,128)(2,1)S(1)} %get-tuple-element.24), channel_id=1, source_target_pairs={{0,3},{1,2},{2,1},{3,0},{4,7},{5,6},{6,5},{7,4},{8,11},{9,10},{10,... | collective-permute-start | bytes 196616 | tf_op jit(solution)/shard_map/ppermute | solution.py:24
  101.4 4.3 %collective-permute-start.24 = (bf16[256,128]{1,0:T(8,128)(2,1)S(1)}, bf16[256,128]{1,0:T(8,128)(2,1)S(1)}, u32[]{:S(2)}, u32[]{:S(2)}) collective-permute-start(bf16[256,128]{1,0:T(8,128)(2,1)S(1)} %get-tuple-element.25), channel_id=1, source_target_pairs={{0,2},{1,3},{2,0},{3,1},{4,6},{5,7},{6,4},{7,5},{8,10},{9,11},{10,... | collective-permute-start | bytes 196616 | tf_op jit(solution)/shard_map/ppermute | solution.py:24
  103.0 4.3 %collective-permute-start.23 = (bf16[256,128]{1,0:T(8,128)(2,1)S(1)}, bf16[256,128]{1,0:T(8,128)(2,1)S(1)}, u32[]{:S(2)}, u32[]{:S(2)}) collective-permute-start(bf16[256,128]{1,0:T(8,128)(2,1)S(1)} %get-tuple-element.26), channel_id=1, source_target_pairs={{0,1},{1,0},{2,3},{3,2},{4,5},{5,4},{6,7},{7,6},{8,9},{9,8},{10,11... | collective-permute-start | bytes 196616 | tf_op jit(solution)/shard_map/ppermute | solution.py:24
  104.2 4.1 %collective-permute-start.21 = (bf16[256,128]{1,0:T(8,128)(2,1)S(1)}, bf16[256,128]{1,0:T(8,128)(2,1)S(1)}, u32[]{:S(2)}, u32[]{:S(2)}) collective-permute-start(bf16[256,128]{1,0:T(8,128)(2,1)S(1)} %get-tuple-element.28), channel_id=1, source_target_pairs={{0,3},{1,2},{2,1},{3,0},{4,7},{5,6},{6,5},{7,4},{8,11},{9,10},{10,... | collective-permute-start | bytes 196616 | tf_op jit(solution)/shard_map/ppermute | solution.py:24
  105.7 4.3 %collective-permute-start.20 = (bf16[256,128]{1,0:T(8,128)(2,1)S(1)}, bf16[256,128]{1,0:T(8,128)(2,1)S(1)}, u32[]{:S(2)}, u32[]{:S(2)}) collective-permute-start(bf16[256,128]{1,0:T(8,128)(2,1)S(1)} %get-tuple-element.29), channel_id=1, source_target_pairs={{0,2},{1,3},{2,0},{3,1},{4,6},{5,7},{6,4},{7,5},{8,10},{9,11},{10,... | collective-permute-start | bytes 196616 | tf_op jit(solution)/shard_map/ppermute | solution.py:24
  107.2 4.3 %collective-permute-start.19 = (bf16[256,128]{1,0:T(8,128)(2,1)S(1)}, bf16[256,128]{1,0:T(8,128)(2,1)S(1)}, u32[]{:S(2)}, u32[]{:S(2)}) collective-permute-start(bf16[256,128]{1,0:T(8,128)(2,1)S(1)} %get-tuple-element.30), channel_id=1, source_target_pairs={{0,1},{1,0},{2,3},{3,2},{4,5},{5,4},{6,7},{7,6},{8,9},{9,8},{10,11... | collective-permute-start | bytes 196616 | tf_op jit(solution)/shard_map/ppermute | solution.py:24
  108.3 3.8 %collective-permute-start.11 = (bf16[256,128]{1,0:T(8,128)(2,1)S(1)}, bf16[256,128]{1,0:T(8,128)(2,1)S(1)}, u32[]{:S(2)}, u32[]{:S(2)}) collective-permute-start(bf16[256,128]{1,0:T(8,128)(2,1)S(1)} %get-tuple-element.36), channel_id=1, source_target_pairs={{0,3},{1,2},{2,1},{3,0},{4,7},{5,6},{6,5},{7,4},{8,11},{9,10},{10,... | collective-permute-start | bytes 196616 | tf_op jit(solution)/shard_map/ppermute | solution.py:24
  110.0 4.3 %collective-permute-start.10 = (bf16[256,128]{1,0:T(8,128)(2,1)S(1)}, bf16[256,128]{1,0:T(8,128)(2,1)S(1)}, u32[]{:S(2)}, u32[]{:S(2)}) collective-permute-start(bf16[256,128]{1,0:T(8,128)(2,1)S(1)} %get-tuple-element.37), channel_id=1, source_target_pairs={{0,2},{1,3},{2,0},{3,1},{4,6},{5,7},{6,4},{7,5},{8,10},{9,11},{10,... | collective-permute-start | bytes 196616 | tf_op jit(solution)/shard_map/ppermute | solution.py:24
  111.5 5.3 %collective-permute-start.9 = (bf16[256,128]{1,0:T(8,128)(2,1)S(1)}, bf16[256,128]{1,0:T(8,128)(2,1)S(1)}, u32[]{:S(2)}, u32[]{:S(2)}) collective-permute-start(bf16[256,128]{1,0:T(8,128)(2,1)S(1)} %get-tuple-element.38), channel_id=1, source_target_pairs={{0,1},{1,0},{2,3},{3,2},{4,5},{5,4},{6,7},{7,6},{8,9},{9,8},{10,11... | collective-permute-start | bytes 196616 | tf_op jit(solution)/shard_map/ppermute | solution.py:24
  112.1 9.8 %collective-permute-start.16 = (bf16[256,128]{1,0:T(8,128)(2,1)S(1)}, bf16[256,128]{1,0:T(8,128)(2,1)S(1)}, u32[]{:S(2)}, u32[]{:S(2)}) collective-permute-start(bf16[256,128]{1,0:T(8,128)(2,1)S(1)} %get-tuple-element.34), channel_id=1, source_target_pairs={{0,1},{1,0},{2,3},{3,2},{4,5},{5,4},{6,7},{7,6},{8,9},{9,8},{10,11... | collective-permute-start | bytes 196616 | tf_op jit(solution)/shard_map/ppermute | solution.py:24
  114.3 9.7 %collective-permute-start.22 = (bf16[4,256,128]{2,1,0:T(8,128)(2,1)S(1)}, bf16[4,256,128]{2,1,0:T(8,128)(2,1)S(1)}, u32[]{:S(2)}, u32[]{:S(2)}) collective-permute-start(bf16[4,256,128]{2,1,0:T(8,128)(2,1)S(1)} %pad_maximum_fusion.6), channel_id=1, source_target_pairs={{0,12},{4,8},{8,4},{12,0},{1,13},{5,9},{9,5},{13,1},{2,14},{6,10},... | collective-permute-start | bytes 786440 | tf_op jit(solution)/shard_map/ppermute | solution.py:24
  116.8 12.1 %collective-permute-start.26 = (bf16[4,256,128]{2,1,0:T(8,128)(2,1)S(1)}, bf16[4,256,128]{2,1,0:T(8,128)(2,1)S(1)}, u32[]{:S(2)}, u32[]{:S(2)}) collective-permute-start(bf16[4,256,128]{2,1,0:T(8,128)(2,1)S(1)} %pad_maximum_fusion.7), channel_id=1, source_target_pairs={{0,4},{4,0},{8,12},{12,8},{1,5},{5,1},{9,13},{13,9},{2,6},{6,2},{1... | collective-permute-start | bytes 786440 | tf_op jit(solution)/shard_map/ppermute | solution.py:24
  122.0 18.1 %collective-permute-start.12 = (bf16[4,256,128]{2,1,0:T(8,128)(2,1)S(1)}, bf16[4,256,128]{2,1,0:T(8,128)(2,1)S(1)}, u32[]{:S(2)}, u32[]{:S(2)}) collective-permute-start(bf16[4,256,128]{2,1,0:T(8,128)(2,1)S(1)} %pad_maximum_fusion.4), channel_id=1, source_target_pairs={{0,8},{4,12},{8,0},{12,4},{1,9},{5,13},{9,1},{13,5},{2,10},{6,14},... | collective-permute-start | bytes 786440 | tf_op jit(solution)/shard_map/ppermute | solution.py:24
where the time goes:
time: 145 us; the launch traced here: 144 us
  waiting for transfers between devices  74.4 us (51%)
  starting transfers between devices  34.3 us (24%)
  Pallas kernels  29.5 us (20%)
  other arithmetic  2.86 us (2%)
  local copies, waits for them, and re-layouts  2.79 us (2%)
    ppermute x27, waiting for transfers between devices, swapped(): return lax.ppermute(value, axis, [(i, i ^ mask) for i in range(count)])  74.4 us
    ppermute x27, starting transfers between devices, swapped(): return lax.ppermute(value, axis, [(i, i ^ mask) for i in range(count)])  34.3 us
    pallas_call x4, Pallas kernels, attend(): pl.pallas_call(functools.partial(attend_body, len(pieces)), out_shape=jax...  20.3 us
    pallas_call x2, Pallas kernels, project(): pl.pallas_call(functools.partial(project_body, groups, count, part is not...  9.23 us
  transfers between devices with their start and end apart: 27, of which 13 were waited for; matrix products, arithmetic and copies ran while one was open for 4% of the time, Pallas kernels for 18%

commit v1 on v0

v1 whole, which is shorter than its diff:
```python
import functools
import math

import jax
import jax.numpy as jnp
from jax import lax
from jax.experimental import pallas as pl
from jax.experimental.pallas import tpu as pltpu
from jax.sharding import PartitionSpec as P


DH = 128
BLK = 128
LOC = 7


def shifted(value, axis, steps):
    count = lax.axis_size(axis)
    return lax.ppermute(value, axis, [(i, (i + steps) % count) for i in range(count)])


def swapped(value, axis, mask):
    count = lax.axis_size(axis)
    return lax.ppermute(value, axis, [(i, i ^ mask) for i in range(count)])


def swapped_by_parity(value, masks):
    seq, heads = lax.axis_size("seq"), lax.axis_size("head")
    moves = [
        (s * heads + h, (s ^ masks[h % 2]) * heads + h)
        for s in range(seq)
        for h in range(heads)
    ]
    return lax.ppermute(value, ("seq", "head"), moves)


def in_hbm(array):
    return pltpu.with_memory_space_constraint(array, pltpu.HBM)


def chained(*values):
    return lax.optimization_barrier(values)


def cut_body(plan, width, *refs):
    sources, rest = refs[:3], refs[3:]
    outs, sems = rest[:-1], rest[-1]
    me, even = lax.axis_index("seq"), lax.axis_index("head") % 2 == 0
    rows = sources[0].shape[0]
    part = math.gcd(rows, 256)
    copies = []
    for out, (which, masks) in zip(outs, plan):
        place = me ^ jnp.where(even, masks[0], masks[1])
        columns = pl.ds(pl.multiple_of(place * width, width), width)
        for at, source in enumerate(which):
            target = out if len(which) == 1 else out.at[at]
            for first in range(0, rows, part):
                strip = pl.ds(first, part)
                copies.append(
                    pltpu.make_async_copy(
                        sources[source].at[strip, columns],
                        target.at[strip],
                        sems.at[len(copies)],
                    )
                )
    for copy in copies:
        copy.start()
    for copy in copies:
        copy.wait()


def cut(arrays, plan, width):
    rows = arrays[0].shape[0]
    shapes = [
        (rows, width) if len(which) == 1 else (len(which), rows, width)
        for which, _ in plan
    ]
    strips = rows // math.gcd(rows, 256)
    count = sum(len(which) for which, _ in plan) * strips
    return pl.pallas_call(
        functools.partial(cut_body, plan, width),
        out_shape=[pltpu.VMEM(shape, arrays[0].dtype) for shape in shapes],
        in_specs=[pl.BlockSpec(memory_space=pl.ANY)] * len(arrays),
        out_specs=[pl.BlockSpec(memory_space=pltpu.VMEM)] * len(plan),
        scratch_shapes=[pltpu.SemaphoreType.DMA((count,))],
        compiler_params=pltpu.CompilerParams(vmem_limit_bytes=4 << 20),
        name="cut",
    )(*arrays)


def pool_body(count, *refs):
    pieces, kv, sems = refs[:count], refs[count], refs[count + 1]
    copies, first = [], 0
    for at, piece in enumerate(pieces):
        rows = pl.ds(first, piece.shape[1])
        copies.append(pltpu.make_async_copy(piece, kv.at[:, rows], sems.at[at]))
        first += piece.shape[1]
    for copy in copies:
        copy.start()
    for copy in copies:
        copy.wait()


def pool(pieces):
    total = sum(piece.shape[1] for piece in pieces)
    return pl.pallas_call(
        functools.partial(pool_body, len(pieces)),
        out_shape=pltpu.VMEM((2, total, DH), pieces[0].dtype),
        in_specs=[pl.BlockSpec(memory_space=pl.ANY)] * len(pieces),
        out_specs=pl.BlockSpec(memory_space=pltpu.VMEM),
        scratch_shapes=[pltpu.SemaphoreType.DMA((len(pieces),))],
        compiler_params=pltpu.CompilerParams(vmem_limit_bytes=4 << 20),
        name="pool",
    )(*[in_hbm(piece) for piece in pieces])


def attend_body(slots, q_ref, kv, o_ref):
    nsel = slots.shape[1]
    factor = math.log2(math.e) / math.sqrt(DH)

    def one_block(i):
        rows = pl.ds(pl.multiple_of(i * BLK, BLK), BLK)
        picked = [
            pl.ds(pl.multiple_of(slots[i, j] * BLK, BLK), BLK) for j in range(nsel)
        ]
        key_set = jnp.concatenate([kv[0, p, :] for p in picked], axis=0)
        scores = lax.dot_general(
            q_ref[rows, :],
            key_set,
            (((1,), (1,)), ((), ())),
            preferred_element_type=jnp.float32,
        )
        peak = jnp.max(scores, axis=1, keepdims=True)
        expo = jnp.exp2(scores * factor - peak * factor).astype(jnp.bfloat16)
        ones = jnp.ones((BLK, DH), jnp.bfloat16)
        value_set = jnp.concatenate(
            [jnp.concatenate([kv[1, p, :], ones], axis=1) for p in picked], axis=0
        )
        mixed = jnp.dot(expo, value_set, preferred_element_type=jnp.float32)
        o_ref[rows, :] = (mixed[:, :DH] / mixed[:, DH:]).astype(o_ref.dtype)

    blocks = q_ref.shape[0] // BLK
    together = math.gcd(blocks, 8)

    def some_blocks(g, carry):
        for u in range(together):
            one_block(g * together + u)
        return carry

    lax.fori_loop(0, blocks // together, some_blocks, 0)


def attend(queries, pooled, slots):
    return pl.pallas_call(
        attend_body,
        out_shape=jax.ShapeDtypeStruct(queries.shape, queries.dtype),
        in_specs=[
            pl.BlockSpec(memory_space=pltpu.SMEM),
            pl.BlockSpec(memory_space=pltpu.VMEM),
            pl.BlockSpec(memory_space=pltpu.VMEM),
        ],
        out_specs=pl.BlockSpec(memory_space=pltpu.VMEM),
        compiler_params=pltpu.CompilerParams(vmem_limit_bytes=24 << 20),
        name="attend",
    )(slots, queries, pooled)


def sheaf_body(count, width, *refs):
    sources, out, sems = refs[:count], refs[count], refs[count + 1]
    copies = []
    for origin in range(sources[0].shape[0] // width):
        for j, source in enumerate(sources):
            target = out.at[pl.ds((origin * count + j) * width, width)]
            copies.append(
                pltpu.make_async_copy(
                    source.at[pl.ds(origin * width, width)], target, sems.at[len(copies)]
                )
            )
    for copy in copies:
        copy.start()
    for copy in copies:
        copy.wait()


def sheaf(weights, width):
    count = len(weights)
    rows, columns = weights[0].shape
    return pl.pallas_call(
        functools.partial(sheaf_body, count, width),
        out_shape=pltpu.VMEM((count * rows, columns), weights[0].dtype),
        in_specs=[pl.BlockSpec(memory_space=pl.ANY)] * count,
        out_specs=pl.BlockSpec(memory_space=pltpu.VMEM),
        scratch_shapes=[pltpu.SemaphoreType.DMA((count * (rows // width),))],
        compiler_params=pltpu.CompilerParams(vmem_limit_bytes=4 << 20),
        name="sheaf",
    )(*[in_hbm(weight) for weight in weights])


def product(left_ref, rights_ref, mask, columns):
    count, _, width = left_ref.shape
    origin = lax.axis_index("seq") ^ mask
    depth = count * width
    left = jnp.concatenate([left_ref[j] for j in range(count)], axis=1)
    right = rights_ref[pl.ds(pl.multiple_of(origin * depth, depth), depth), columns]
    return jnp.dot(left, right, preferred_element_type=jnp.float32)


def project_body(masks, tile, rights_ref, *refs):
    lefts, o_ref = refs[:-1], refs[-1]
    for first in range(0, o_ref.shape[1], tile):
        columns = pl.ds(first, tile)
        total = None
        for left_ref, mask in zip(lefts, masks):
            term = product(left_ref, rights_ref, mask, columns)
            total = term if total is None else total + term
        o_ref[:, columns] = total


def project(lefts, masks, rights):
    rows, columns = lefts[0].shape[1], rights.shape[1]
    inside = pl.BlockSpec(memory_space=pltpu.VMEM)
    return pl.pallas_call(
        functools.partial(project_body, masks, math.gcd(512, columns)),
        out_shape=pltpu.VMEM((rows, columns), jnp.float32),
        in_specs=[inside] * (1 + len(lefts)),
        out_specs=inside,
        compiler_params=pltpu.CompilerParams(vmem_limit_bytes=24 << 20),
        name="project",
    )(rights, *lefts)


def finish_body(mask, tile, left_ref, rights_ref, part_ref, o_ref, held, sems):
    copies = []
    for n in range(part_ref.shape[1] // tile):
        columns = pl.ds(n * tile, tile)
        term = product(left_ref, rights_ref, mask, columns)
        held[:, columns] = (part_ref[:, columns] + term).astype(held.dtype)
        copies.append(
            pltpu.make_async_copy(held.at[:, columns], o_ref.at[:, columns], sems.at[n])
        )
        copies[-1].start()
    for copy in copies:
        copy.wait()


def finish(left, mask, rights, part, dtype):
    tile = math.gcd(512, part.shape[1])
    inside = pl.BlockSpec(memory_space=pltpu.VMEM)
    return pl.pallas_call(
        functools.partial(finish_body, mask, tile),
        out_shape=jax.ShapeDtypeStruct(part.shape, dtype),
        in_specs=[inside] * 3,
        out_specs=pl.BlockSpec(memory_space=pl.ANY),
        scratch_shapes=[
            pltpu.VMEM(part.shape, dtype),
            pltpu.SemaphoreType.DMA((part.shape[1] // tile,)),
        ],
        compiler_params=pltpu.CompilerParams(vmem_limit_bytes=24 << 20),
        name="finish",
    )(left, rights, part)


def rounds_of(seq):
    even = list(range(1, seq))
    odd = even[:2][::-1] + even[2:]
    return list(zip(even, odd))


def served_by(seq):
    far = list(range(seq - 1, 1, -1))
    return far[:1] + [1] + far[1:]


def far_first(heads):
    hops = [1]
    while 2 * hops[0] < heads:
        hops = [2 * hops[0]] + hops
    return hops


def by_heads(queries, keys, values, pattern, out_weight):
    qblocks = pattern.shape[0]
    rows, feat = queries.shape
    seq, heads = lax.axis_size("seq"), lax.axis_size("head")
    me, head = lax.axis_index("seq"), lax.axis_index("head")
    width = feat // seq
    share = rows // heads
    rounds, order = rounds_of(seq), served_by(seq)
    even = head % 2 == 0
    arrays = tuple(in_hbm(array) for array in (keys, values, queries))

    pairs = []
    for masks in rounds:
        (outgoing,) = cut(arrays, [((0, 1), masks)], width)
        pairs.append(swapped_by_parity(outgoing, masks))
    kept = [((0, 1), (0, 0)), ((2,), (0, 0))] + [((2,), (m, m)) for m in order]
    own_pair, own_queries, *queries_for = cut(arrays, kept, width)
    pairs = [own_pair] + pairs
    patterns, asked = {0: pattern}, {0: own_queries}
    for at, mask in enumerate(order):
        patterns[mask] = swapped(pattern, "seq", mask)
        asked[mask] = swapped(queries_for[at], "seq", mask)
    weights = {0: out_weight}
    for hop in far_first(heads):
        for other in list(weights):
            weights[other ^ hop] = swapped(weights[other], "head", hop)

    pooled = pool(pairs)

    def slots_of(ids):
        apart = (ids // qblocks) ^ me
        slot = jnp.zeros_like(ids)
        for r, (a, b) in enumerate(rounds):
            slot = jnp.where(apart == jnp.where(even, a, b), r + 1, slot)
        return slot * qblocks + ids % qblocks

    def split(block):
        got = []
        for hop in range(heads):
            mine = lax.dynamic_slice_in_dim(block, (head ^ hop) * share, share, axis=0)
            got.append(swapped(mine, "head", hop) if hop else mine)
        return jnp.stack(got)

    ready, before = {}, None
    for mask in [0] + order:
        slots = slots_of(patterns[mask])
        if before is not None:
            slots, before = chained(slots, before)
        mixed = before = attend(asked[mask], pooled, slots)
        if mask and mask != 1 and mask != order[-1]:
            ready[mask] = split(swapped(mixed, "seq", mask))
        elif mask:
            ready[mask] = swapped(split(mixed), "seq", mask)
        else:
            ready[mask] = split(mixed)
    tail = order[-1]
    early = [mask for mask in [0] + order if mask != tail]
    rights = sheaf([weights[hop] for hop in range(heads)], width)
    part = project([ready[mask] for mask in early], early, rights)
    return finish(ready[tail], tail, rights, part, queries.dtype)


def by_rows(queries, keys, values, pattern, out_weight):
    qblocks = pattern.shape[0]
    _, feat = queries.shape
    total = qblocks * lax.axis_size("seq")
    me = lax.axis_index("seq")
    own = jnp.stack([keys, values])
    nearby = [shifted(own, "seq", 1), own, shifted(own, "seq", -1)]
    ids = pattern[0, LOC:]
    local = ids - me * qblocks
    owned = (local >= 0) & (local < qblocks)
    blocks = own.reshape(2, qblocks, BLK, feat)
    picked = jnp.take(blocks, jnp.clip(local, 0, qblocks - 1), axis=1)
    picked = jnp.where(owned[None, :, None, None], picked, jnp.zeros((), picked.dtype))
    distant = lax.psum(picked, "seq").reshape(2, -1, feat)
    near_slots = (pattern[:, :LOC] - (me - 1) * qblocks) % total
    far_slots = jnp.broadcast_to(
        3 * qblocks + jnp.arange(ids.shape[0], dtype=jnp.int32), (qblocks, ids.shape[0])
    )
    slots = jnp.concatenate([near_slots, far_slots], axis=1)
    mixed = []
    for first in range(0, feat, DH):
        columns = slice(first, first + DH)
        pooled = pool([piece[:, :, columns] for piece in nearby + [distant]])
        mixed.append(attend(queries[:, columns], pooled, slots))
    attended = jnp.concatenate(mixed, axis=1)
    regrouped = lax.all_to_all(attended, "head", split_axis=0, concat_axis=1, tiled=True)
    result = jnp.dot(
        regrouped,
        lax.all_gather(out_weight, "head", axis=0, tiled=True),
        preferred_element_type=jnp.float32,
    )
    return result.astype(queries.dtype)


def heads_split(feat, seq):
    return feat == seq * DH and seq & (seq - 1) == 0


def per_device(queries, keys, values, pattern, out_weight):
    if heads_split(queries.shape[1], lax.axis_size("seq")):
        return by_heads(queries, keys, values, pattern, out_weight)
    return by_rows(queries, keys, values, pattern, out_weight)


def solution(mesh):
    placed = (
        P(("grp", "seq"), "head"),
        P(("grp", "seq"), "head"),
        P(("grp", "seq"), "head"),
        P(("grp", "seq"), None),
        P("head", None),
    )
    step = jax.shard_map(
        per_device,
        mesh=mesh,
        in_specs=placed,
        out_specs=P(("grp", "seq", "head"), None),
        check_vma=False,
    )

    def run(queries, keys, values, pattern, out_weight):
        feat = queries.shape[1] // mesh.shape["head"]
        whole = step
        if heads_split(feat, mesh.shape["seq"]):
            whole = step
        return whole(queries, keys, values, pattern, out_weight)

    return run
```

time: 145 us -> 173 us (1.19)
  waiting for transfers between devices: 74.4 us -> 93.7 us
  starting transfers between devices: 34.3 us -> 48.3 us
  other arithmetic: 2.86 us -> 0.2 us
  local copies, waits for them, and re-layouts: 2.79 us -> 0.88 us
    ppermute x0 -> x3, waiting for transfers between devices: none -> 27.5 us  [swapped_by_parity(): return lax.ppermute(value, ('seq', 'head'), moves)]
    ppermute x27 -> x24, starting transfers between devices: 34.3 us -> 43.7 us  [swapped(): return lax.ppermute(value, axis, [(i, i ^ mask) for i in range(count)])]
    ppermute x27 -> x24, waiting for transfers between devices: 74.4 us -> 66.2 us  [swapped(): return lax.ppermute(value, axis, [(i, i ^ mask) for i in range(count)])]
    ppermute x0 -> x3, starting transfers between devices: none -> 4.61 us  [swapped_by_parity(): return lax.ppermute(value, ('seq', 'head'), moves)]
    another operation x9 -> x4, other arithmetic: 2.81 us -> 0.14 us  [split(): return jnp.stack(got)]
    pallas_call x6 -> x12, Pallas kernels: 29.5 us -> 29.2 us  [the longest x4 15.8 us: attend(): pl.pallas_call(attend_body, out_shape=jax.ShapeDtypeStruct(queries.shape,...]
  transfers between devices with their start and end apart: 27 -> 27, of which waited for: 13 -> 13; matrix products, arithmetic and copies ran while one was open for 4% -> 0% of each run, Pallas kernels for 18% -> 16%
where the time goes in v1:
time: 173 us
  waiting for transfers between devices  93.7 us (54%)
  starting transfers between devices  48.3 us (28%)
  Pallas kernels  29.2 us (17%)
    ppermute x24, waiting for transfers between devices, swapped(): return lax.ppermute(value, axis, [(i, i ^ mask) for i in range(count)])  66.2 us
    ppermute x24, starting transfers between devices, swapped(): return lax.ppermute(value, axis, [(i, i ^ mask) for i in range(count)])  43.7 us
    ppermute x3, waiting for transfers between devices, swapped_by_parity(): return lax.ppermute(value, ('seq', 'head'), moves)  27.5 us
    pallas_call x4, Pallas kernels, attend(): pl.pallas_call(attend_body, out_shape=jax.ShapeDtypeStruct(queries.shape,...  15.8 us
    pallas_call x4, Pallas kernels, cut(): pl.pallas_call(functools.partial(cut_body, plan, width), out_shape=[pltpu...  5.07 us
    ppermute x3, starting transfers between devices, swapped_by_parity(): return lax.ppermute(value, ('seq', 'head'), moves)  4.61 us
    pallas_call x1, Pallas kernels, sheaf(): pl.pallas_call(functools.partial(sheaf_body, count, width), out_shape=plt...  3.52 us
  transfers between devices with their start and end apart: 27, of which 13 were waited for; matrix products, arithmetic and copies ran while one was open for 0% of the time, Pallas kernels for 16%

profile of v1, /device:TPU:0, one launch (start us, length us, event | category | flops | bytes accessed | tf_op | source)
XLA Modules:
  0.0 172.6 jit_solution(11664214926628152442)
XLA Ops:
  0.0 3.0 %collective-permute-start.14 = (bf16[512,2048]{1,0:T(8,128)(2,1)}, bf16[512,2048]{1,0:T(8,128)(2,1)}, u32[]{:S(2)}, u32[]{:S(2)}) collective-permute-start(bf16[512,2048]{1,0:T(8,128)(2,1)} %refs_0_.9), channel_id=1, source_target_pairs={{0,2},{1,3},{2,0},{3,1},{4,6},{5,7},{6,4},{7,5},{8,10},{9,11},{10,... | collective-permute-start | bytes 6291464 | tf_op jit(solution)/shard_map/ppermute | solution.py:24
  3.0 0.0 collective-permute-start.13
  3.0 45.9 %collective-permute-done.14.refs_2_ = bf16[512,2048]{1,0:T(8,128)(2,1)} collective-permute-done((bf16[512,2048]{1,0:T(8,128)(2,1)}, bf16[512,2048]{1,0:T(8,128)(2,1)}, u32[]{:S(2)}, u32[]{:S(2)}) %collective-permute-start.14) | collective-permute-done | bytes 2097184 | tf_op jit(solution)/shard_map/ppermute | solution.py:24
  48.9 0.0 collective-permute-start.15
  48.9 1.8 %collective-permute-start.1 = (s32[8,15]{1,0:T(8,128)}, s32[8,15]{1,0:T(8,128)S(1)}, u32[]{:S(2)}, u32[]{:S(2)}) collective-permute-start(s32[8,15]{1,0:T(8,128)} %param.8), channel_id=1, source_target_pairs={{0,4},{4,0},{8,12},{12,8},{1,5},{5,1},{9,13},{13,9},{2,6},{6,2},{1... | collective-permute-start | bytes 1448 | tf_op jit(solution)/shard_map/ppermute | solution.py:24
  50.7 2.6 %collective-permute-start = (s32[8,15]{1,0:T(8,128)}, s32[8,15]{1,0:T(8,128)S(1)}, u32[]{:S(2)}, u32[]{:S(2)}) collective-permute-start(s32[8,15]{1,0:T(8,128)} %param.8), channel_id=1, source_target_pairs={{0,8},{4,12},{8,0},{12,4},{1,9},{5,13},{9,1},{13,5},{2,10},{6,14},... | collective-permute-start | bytes 1448 | tf_op jit(solution)/shard_map/ppermute | solution.py:24
  53.3 0.0 collective-permute-start.2
  53.3 1.1 cut.6
  54.5 0.0 collective-permute-done.1
  54.5 2.0 %collective-permute-start.4 = (bf16[2,1024,128]{2,1,0:T(8,128)(2,1)S(1)}, bf16[2,1024,128]{2,1,0:T(8,128)(2,1)S(1)}, u32[]{:S(2)}, u32[]{:S(2)}) collective-permute-start(bf16[2,1024,128]{2,1,0:T(8,128)(2,1)S(1)} %cut.6), channel_id=1, source_target_pairs={{0,8},{1,5},{2,10},{3,7},{4,12},{5,1},{6,14},{7,3},{8,0},{9,13},{1... | collective-permute-start | bytes 1572872 | tf_op jit(solution)/shard_map/ppermute | solution.py:34
  56.5 1.1 cut.7
  57.6 0.0 collective-permute-done
  57.6 2.0 %collective-permute-start.5 = (bf16[2,1024,128]{2,1,0:T(8,128)(2,1)S(1)}, bf16[2,1024,128]{2,1,0:T(8,128)(2,1)}, u32[]{:S(2)}, u32[]{:S(2)}) collective-permute-start(bf16[2,1024,128]{2,1,0:T(8,128)(2,1)S(1)} %cut.7), channel_id=1, source_target_pairs={{0,12},{1,13},{2,14},{3,15},{4,8},{5,9},{6,10},{7,11},{8,4},{9,5},... | collective-permute-start | bytes 1572872 | tf_op jit(solution)/shard_map/ppermute | solution.py:34
  59.6 1.1 cut.5
  60.8 0.0 copy-start.2
  60.8 0.6 collective-permute-start.3
  61.4 1.6 cut.4
  63.1 0.0 copy-start
  63.1 0.8 copy-done
  63.9 27.5 %collective-permute-done.4.refs_2_ = bf16[2,1024,128]{2,1,0:T(8,128)(2,1)S(1)} collective-permute-done((bf16[2,1024,128]{2,1,0:T(8,128)(2,1)S(1)}, bf16[2,1024,128]{2,1,0:T(8,128)(2,1)S(1)}, u32[]{:S(2)}, u32[]{:S(2)}) %collective-permute-start.4) | collective-permute-done | bytes 524320 | tf_op jit(solution)/shard_map/ppermute | solution.py:34
  91.4 7.3 %collective-permute-start.6 = (bf16[1024,128]{1,0:T(8,128)(2,1)S(1)}, bf16[1024,128]{1,0:T(8,128)(2,1)S(1)}, u32[]{:S(2)}, u32[]{:S(2)}) collective-permute-start(bf16[1024,128]{1,0:T(8,128)(2,1)S(1)} %get-tuple-element.16), channel_id=1, source_target_pairs={{0,12},{4,8},{8,4},{12,0},{1,13},{5,9},{9,5},{13,1},{2,14},{6,10},... | collective-permute-start | bytes 786440 | tf_op jit(solution)/shard_map/ppermute | solution.py:24
  98.8 0.0 collective-permute-done.5.refs_3_
  98.8 11.2 %collective-permute-start.7 = (bf16[1024,128]{1,0:T(8,128)(2,1)S(1)}, bf16[1024,128]{1,0:T(8,128)(2,1)S(1)}, u32[]{:S(2)}, u32[]{:S(2)}) collective-permute-start(bf16[1024,128]{1,0:T(8,128)(2,1)S(1)} %get-tuple-element.18), channel_id=1, source_target_pairs={{0,4},{4,0},{8,12},{12,8},{1,5},{5,1},{9,13},{13,9},{2,6},{6,2},{1... | collective-permute-start | bytes 786440 | tf_op jit(solution)/shard_map/ppermute | solution.py:24
  110.0 0.0 collective-permute-done.3.refs_1_
  110.0 2.0 %collective-permute-start.8 = (bf16[1024,128]{1,0:T(8,128)(2,1)S(1)}, bf16[1024,128]{1,0:T(8,128)(2,1)S(1)}, u32[]{:S(2)}, u32[]{:S(2)}) collective-permute-start(bf16[1024,128]{1,0:T(8,128)(2,1)S(1)} %get-tuple-element.20), channel_id=1, source_target_pairs={{0,8},{4,12},{8,0},{12,4},{1,9},{5,13},{9,1},{13,5},{2,10},{6,14},... | collective-permute-start | bytes 786440 | tf_op jit(solution)/shard_map/ppermute | solution.py:24
  112.1 1.6 pool.1.kv
  113.6 3.9 %attend.4 = bf16[1024,128]{1,0:T(8,128)(2,1)S(1)} custom-call(s32[8,15]{1,0:T(8,128)S(1)} %fusion.7.slots, bf16[1024,128]{1,0:T(8,128)(2,1)S(1)} %get-tuple-element.13.q_ref, bf16[2,4096,128]{2,1,0:T(8,128)(2,1)S(1)} %pool.1.kv), custom_call_target="tpu_custom_call" | custom-call | tf_op jit(solution)/shard_map/attend/pallas_call | solution.py:154
  117.5 3.9 %attend.5 = bf16[1024,128]{1,0:T(8,128)(2,1)S(1)} custom-call(s32[8,15]{1,0:T(8,128)S(1)} %fusion.5.slots, bf16[1024,128]{1,0:T(8,128)(2,1)S(1)} %collective-permute-done.6.q_ref, bf16[2,4096,128]{2,1,0:T(8,128)(2,1)S(1)} %pool.1.kv), custom_call_target="tpu_custom_call" | custom-call | tf_op jit(solution)/shard_map/attend/pallas_call | solution.py:154
  121.4 1.5 collective-permute-start.19
  123.0 0.0 collective-permute-done.7.q_ref
  123.0 3.9 %attend.6 = bf16[1024,128]{1,0:T(8,128)(2,1)S(1)} custom-call(s32[8,15]{1,0:T(8,128)S(1)} %fusion.3.slots, bf16[1024,128]{1,0:T(8,128)(2,1)S(1)} %collective-permute-done.7.q_ref, bf16[2,4096,128]{2,1,0:T(8,128)(2,1)S(1)} %pool.1.kv), custom_call_target="tpu_custom_call" | custom-call | tf_op jit(solution)/shard_map/attend/pallas_call | solution.py:154
  126.9 4.0 %collective-permute-done.8.q_ref = bf16[1024,128]{1,0:T(8,128)(2,1)S(1)} collective-permute-done((bf16[1024,128]{1,0:T(8,128)(2,1)S(1)}, bf16[1024,128]{1,0:T(8,128)(2,1)S(1)}, u32[]{:S(2)}, u32[]{:S(2)}) %collective-permute-start.8) | collective-permute-done | bytes 262176 | tf_op jit(solution)/shard_map/ppermute | solution.py:24
  130.9 4.1 %attend.7 = bf16[1024,128]{1,0:T(8,128)(2,1)S(1)} custom-call(s32[8,15]{1,0:T(8,128)S(1)} %fusion.1.slots, bf16[1024,128]{1,0:T(8,128)(2,1)S(1)} %collective-permute-done.8.q_ref, bf16[2,4096,128]{2,1,0:T(8,128)(2,1)S(1)} %pool.1.kv), custom_call_target="tpu_custom_call" | custom-call | tf_op jit(solution)/shard_map/attend/pallas_call | solution.py:154
  135.0 3.3 %collective-permute-start.11 = (bf16[256,128]{1,0:T(8,128)(2,1)S(1)}, bf16[256,128]{1,0:T(8,128)(2,1)S(1)}, u32[]{:S(2)}, u32[]{:S(2)}) collective-permute-start(bf16[256,128]{1,0:T(8,128)(2,1)S(1)} %get-tuple-element.34), channel_id=1, source_target_pairs={{0,3},{1,2},{2,1},{3,0},{4,7},{5,6},{6,5},{7,4},{8,11},{9,10},{10,... | collective-permute-start | bytes 196616 | tf_op jit(solution)/shard_map/ppermute | solution.py:24
  138.3 0.6 collective-permute-start.10
  138.9 1.4 collective-permute-done.11
  140.3 1.1 collective-permute-start.9
  141.5 1.2 collective-permute-done.10
  142.7 0.0 collective-permute-done.9
  142.7 0.9 collective-permute-start.24
  143.6 3.1 %collective-permute-done.25 = bf16[256,128]{1,0:T(8,128)(2,1)S(1)} collective-permute-done((bf16[256,128]{1,0:T(8,128)(2,1)S(1)}, bf16[256,128]{1,0:T(8,128)(2,1)S(1)}, u32[]{:S(2)}, u32[]{:S(2)}) %collective-permute-start.25) | collective-permute-done | bytes 65568 | tf_op jit(solution)/shard_map/ppermute | solution.py:24
  146.7 0.0 collective-permute-start.23
  146.7 0.9 collective-permute-done.24
  147.6 0.8 collective-permute-start.18
  148.5 0.0 collective-permute-done.19
  148.5 0.9 collective-permute-start.17
  149.4 0.0 collective-permute-done.23
  149.4 0.2 collective-permute-start.16
  149.6 2.1 %collective-permute-done.18 = bf16[256,128]{1,0:T(8,128)(2,1)S(1)} collective-permute-done((bf16[256,128]{1,0:T(8,128)(2,1)S(1)}, bf16[256,128]{1,0:T(8,128)(2,1)S(1)}, u32[]{:S(2)}, u32[]{:S(2)}) %collective-permute-start.18) | collective-permute-done | bytes 65568 | tf_op jit(solution)/shard_map/ppermute | solution.py:24
  151.7 1.1 collective-permute-start.22
  152.9 0.6 collective-permute-done.17
  153.4 1.1 collective-permute-start.21
  154.6 0.0 collective-permute-done.16
  154.6 0.6 collective-permute-start.26
  155.2 0.3 collective-permute-done.22
  155.5 3.5 %collective-permute-start.12 = (bf16[4,256,128]{2,1,0:T(8,128)(2,1)S(1)}, bf16[4,256,128]{2,1,0:T(8,128)(2,1)S(1)}, u32[]{:S(2)}, u32[]{:S(2)}) collective-permute-start(bf16[4,256,128]{2,1,0:T(8,128)(2,1)S(1)} %pad_maximum_fusion), channel_id=1, source_target_pairs={{0,8},{4,12},{8,0},{12,4},{1,9},{5,13},{9,1},{13,5},{2,10},{6,14},... | collective-permute-start | bytes 786440 | tf_op jit(solution)/shard_map/ppermute | solution.py:24
  159.0 0.0 collective-permute-done.21
  159.1 1.2 collective-permute-done.20
  160.3 0.0 collective-permute-done.15.refs_3_
  160.3 3.5 %sheaf.1.rights_ref = bf16[2048,2048]{1,0:T(8,128)(2,1)S(1)} custom-call(bf16[512,2048]{1,0:T(8,128)(2,1)} %refs_0_.9, bf16[512,2048]{1,0:T(8,128)(2,1)} %collective-permute-done.13.refs_1_, bf16[512,2048]{1,0:T(8,128)(2,1)} %collective-permute-done.14.refs_2_, bf16[512,2048]{1,0:T(8,128)(2,1)} %collective-permute-done.15.refs_3_), custom_call_target="tpu_custom_call" | custom-call | tf_op jit(solution)/shard_map/sheaf/pallas_call | solution.py:188
  163.9 3.4 %collective-permute-done.26.refs_2_ = bf16[4,256,128]{2,1,0:T(8,128)(2,1)S(1)} collective-permute-done((bf16[4,256,128]{2,1,0:T(8,128)(2,1)S(1)}, bf16[4,256,128]{2,1,0:T(8,128)(2,1)S(1)}, u32[]{:S(2)}, u32[]{:S(2)}) %collective-permute-start.26) | collective-permute-done | bytes 262176 | tf_op jit(solution)/shard_map/ppermute | solution.py:24
  167.2 1.8 %project.1.part_ref = f32[256,2048]{1,0:T(8,128)S(1)} custom-call(bf16[2048,2048]{1,0:T(8,128)(2,1)S(1)} %sheaf.1.rights_ref, bf16[4,256,128]{2,1,0:T(8,128)(2,1)S(1)} %pad_maximum_fusion.1.refs_0_, bf16[4,256,128]{2,1,0:T(8,128)(2,1)S(1)} %pad_maximum_fusion.2.refs_1_, bf16[4,256,128]{2,1,0:T(8,128)(2,1)S(1)} %collective-permute-done.26.refs_2_), custom_call_target="tpu_custom_call" | custom-call | tf_op jit(solution)/shard_map/project/pallas_call | solution.py:222
  169.0 2.0 %collective-permute-done.12.left_ref = bf16[4,256,128]{2,1,0:T(8,128)(2,1)S(1)} collective-permute-done((bf16[4,256,128]{2,1,0:T(8,128)(2,1)S(1)}, bf16[4,256,128]{2,1,0:T(8,128)(2,1)S(1)}, u32[]{:S(2)}, u32[]{:S(2)}) %collective-permute-start.12) | collective-permute-done | bytes 262176 | tf_op jit(solution)/shard_map/ppermute | solution.py:24
  171.0 1.5 finish.1
  (20 shorter events, 0.3 us)
Async XLA Ops:
  0.0 48.9 %collective-permute-start.14 = (bf16[512,2048]{1,0:T(8,128)(2,1)}, bf16[512,2048]{1,0:T(8,128)(2,1)}, u32[]{:S(2)}, u32[]{:S(2)}) collective-permute-start(bf16[512,2048]{1,0:T(8,128)(2,1)} %refs_0_.9), channel_id=1, source_target_pairs={{0,2},{1,3},{2,0},{3,1},{4,6},{5,7},{6,4},{7,5},{8,10},{9,11},{10,... | collective-permute-start | bytes 6291464 | tf_op jit(solution)/shard_map/ppermute | solution.py:24
  3.0 157.4 %collective-permute-start.13 = (bf16[512,2048]{1,0:T(8,128)(2,1)}, bf16[512,2048]{1,0:T(8,128)(2,1)}, u32[]{:S(2)}, u32[]{:S(2)}) collective-permute-start(bf16[512,2048]{1,0:T(8,128)(2,1)} %refs_0_.9), channel_id=1, source_target_pairs={{0,1},{1,0},{2,3},{3,2},{4,5},{5,4},{6,7},{7,6},{8,9},{9,8},{10,11... | collective-permute-start | bytes 6291464 | tf_op jit(solution)/shard_map/ppermute | solution.py:24
  48.9 111.4 %collective-permute-start.15 = (bf16[512,2048]{1,0:T(8,128)(2,1)}, bf16[512,2048]{1,0:T(8,128)(2,1)}, u32[]{:S(2)}, u32[]{:S(2)}) collective-permute-start(bf16[512,2048]{1,0:T(8,128)(2,1)} %collective-permute-done.14.refs_2_), channel_id=1, source_target_pairs={{0,1},{1,0},{2,3},{3,2},{4,5},{5,4},{6,7},{7,6},{8,9},{9,8},{10,11... | collective-permute-start | bytes 6291464 | tf_op jit(solution)/shard_map/ppermute | solution.py:24
  48.9 5.6 %collective-permute-start.1 = (s32[8,15]{1,0:T(8,128)}, s32[8,15]{1,0:T(8,128)S(1)}, u32[]{:S(2)}, u32[]{:S(2)}) collective-permute-start(s32[8,15]{1,0:T(8,128)} %param.8), channel_id=1, source_target_pairs={{0,4},{4,0},{8,12},{12,8},{1,5},{5,1},{9,13},{13,9},{2,6},{6,2},{1... | collective-permute-start | bytes 1448 | tf_op jit(solution)/shard_map/ppermute | solution.py:24
  50.7 6.9 %collective-permute-start = (s32[8,15]{1,0:T(8,128)}, s32[8,15]{1,0:T(8,128)S(1)}, u32[]{:S(2)}, u32[]{:S(2)}) collective-permute-start(s32[8,15]{1,0:T(8,128)} %param.8), channel_id=1, source_target_pairs={{0,8},{4,12},{8,0},{12,4},{1,9},{5,13},{9,1},{13,5},{2,10},{6,14},... | collective-permute-start | bytes 1448 | tf_op jit(solution)/shard_map/ppermute | solution.py:24
  53.3 7.5 %collective-permute-start.2 = (s32[8,15]{1,0:T(8,128)}, s32[8,15]{1,0:T(8,128)S(1)}, u32[]{:S(2)}, u32[]{:S(2)}) collective-permute-start(s32[8,15]{1,0:T(8,128)} %param.8), channel_id=1, source_target_pairs={{0,12},{4,8},{8,4},{12,0},{1,13},{5,9},{9,5},{13,1},{2,14},{6,10},... | collective-permute-start | bytes 1448 | tf_op jit(solution)/shard_map/ppermute | solution.py:24
  54.5 37.0 %collective-permute-start.4 = (bf16[2,1024,128]{2,1,0:T(8,128)(2,1)S(1)}, bf16[2,1024,128]{2,1,0:T(8,128)(2,1)S(1)}, u32[]{:S(2)}, u32[]{:S(2)}) collective-permute-start(bf16[2,1024,128]{2,1,0:T(8,128)(2,1)S(1)} %cut.6), channel_id=1, source_target_pairs={{0,8},{1,5},{2,10},{3,7},{4,12},{5,1},{6,14},{7,3},{8,0},{9,13},{1... | collective-permute-start | bytes 1572872 | tf_op jit(solution)/shard_map/ppermute | solution.py:34
  57.6 41.1 %collective-permute-start.5 = (bf16[2,1024,128]{2,1,0:T(8,128)(2,1)S(1)}, bf16[2,1024,128]{2,1,0:T(8,128)(2,1)}, u32[]{:S(2)}, u32[]{:S(2)}) collective-permute-start(bf16[2,1024,128]{2,1,0:T(8,128)(2,1)S(1)} %cut.7), channel_id=1, source_target_pairs={{0,12},{1,13},{2,14},{3,15},{4,8},{5,9},{6,10},{7,11},{8,4},{9,5},... | collective-permute-start | bytes 1572872 | tf_op jit(solution)/shard_map/ppermute | solution.py:34
  60.8 3.1 %copy-start.2 = (s32[8,15]{1,0:T(8,128)S(1)}, s32[8,15]{1,0:T(8,128)}, u32[]{:S(2)}) copy-start(s32[8,15]{1,0:T(8,128)} %param.8) | copy-start | bytes 1444
  60.8 49.2 %collective-permute-start.3 = (bf16[2,1024,128]{2,1,0:T(8,128)(2,1)S(1)}, bf16[2,1024,128]{2,1,0:T(8,128)(2,1)}, u32[]{:S(2)}, u32[]{:S(2)}) collective-permute-start(bf16[2,1024,128]{2,1,0:T(8,128)(2,1)S(1)} %cut.5), channel_id=1, source_target_pairs={{0,4},{1,9},{2,6},{3,11},{4,0},{5,13},{6,2},{7,15},{8,12},{9,1},{1... | collective-permute-start | bytes 1572872 | tf_op jit(solution)/shard_map/ppermute | solution.py:34
  63.1 0.8 copy-start
  91.4 20.6 %copy-start.1 = (bf16[2,1024,128]{2,1,0:T(8,128)(2,1)}, bf16[2,1024,128]{2,1,0:T(8,128)(2,1)S(1)}, u32[]{:S(2)}) copy-start(bf16[2,1024,128]{2,1,0:T(8,128)(2,1)S(1)} %collective-permute-done.4.refs_2_) | copy-start | bytes 1572868
  91.4 26.1 %collective-permute-start.6 = (bf16[1024,128]{1,0:T(8,128)(2,1)S(1)}, bf16[1024,128]{1,0:T(8,128)(2,1)S(1)}, u32[]{:S(2)}, u32[]{:S(2)}) collective-permute-start(bf16[1024,128]{1,0:T(8,128)(2,1)S(1)} %get-tuple-element.16), channel_id=1, source_target_pairs={{0,12},{4,8},{8,4},{12,0},{1,13},{5,9},{9,5},{13,1},{2,14},{6,10},... | collective-permute-start | bytes 786440 | tf_op jit(solution)/shard_map/ppermute | solution.py:24
  98.8 24.2 %collective-permute-start.7 = (bf16[1024,128]{1,0:T(8,128)(2,1)S(1)}, bf16[1024,128]{1,0:T(8,128)(2,1)S(1)}, u32[]{:S(2)}, u32[]{:S(2)}) collective-permute-start(bf16[1024,128]{1,0:T(8,128)(2,1)S(1)} %get-tuple-element.18), channel_id=1, source_target_pairs={{0,4},{4,0},{8,12},{12,8},{1,5},{5,1},{9,13},{13,9},{2,6},{6,2},{1... | collective-permute-start | bytes 786440 | tf_op jit(solution)/shard_map/ppermute | solution.py:24
  110.0 20.9 %collective-permute-start.8 = (bf16[1024,128]{1,0:T(8,128)(2,1)S(1)}, bf16[1024,128]{1,0:T(8,128)(2,1)S(1)}, u32[]{:S(2)}, u32[]{:S(2)}) collective-permute-start(bf16[1024,128]{1,0:T(8,128)(2,1)S(1)} %get-tuple-element.20), channel_id=1, source_target_pairs={{0,8},{4,12},{8,0},{12,4},{1,9},{5,13},{9,1},{13,5},{2,10},{6,14},... | collective-permute-start | bytes 786440 | tf_op jit(solution)/shard_map/ppermute | solution.py:24
  121.4 27.0 %collective-permute-start.19 = (bf16[1024,128]{1,0:T(8,128)(2,1)S(1)}, bf16[1024,128]{1,0:T(8,128)(2,1)S(1)}, u32[]{:S(2)}, u32[]{:S(2)}) collective-permute-start(bf16[1024,128]{1,0:T(8,128)(2,1)S(1)} %attend.5), channel_id=1, source_target_pairs={{0,12},{4,8},{8,4},{12,0},{1,13},{5,9},{9,5},{13,1},{2,14},{6,10},... | collective-permute-start | bytes 786440 | tf_op jit(solution)/shard_map/ppermute | solution.py:24
  135.0 5.3 %collective-permute-start.11 = (bf16[256,128]{1,0:T(8,128)(2,1)S(1)}, bf16[256,128]{1,0:T(8,128)(2,1)S(1)}, u32[]{:S(2)}, u32[]{:S(2)}) collective-permute-start(bf16[256,128]{1,0:T(8,128)(2,1)S(1)} %get-tuple-element.34), channel_id=1, source_target_pairs={{0,3},{1,2},{2,1},{3,0},{4,7},{5,6},{6,5},{7,4},{8,11},{9,10},{10,... | collective-permute-start | bytes 196616 | tf_op jit(solution)/shard_map/ppermute | solution.py:24
  138.3 4.3 %collective-permute-start.10 = (bf16[256,128]{1,0:T(8,128)(2,1)S(1)}, bf16[256,128]{1,0:T(8,128)(2,1)S(1)}, u32[]{:S(2)}, u32[]{:S(2)}) collective-permute-start(bf16[256,128]{1,0:T(8,128)(2,1)S(1)} %get-tuple-element.35), channel_id=1, source_target_pairs={{0,2},{1,3},{2,0},{3,1},{4,6},{5,7},{6,4},{7,5},{8,10},{9,11},{10,... | collective-permute-start | bytes 196616 | tf_op jit(solution)/shard_map/ppermute | solution.py:24
  140.3 2.3 %collective-permute-start.9 = (bf16[256,128]{1,0:T(8,128)(2,1)S(1)}, bf16[256,128]{1,0:T(8,128)(2,1)S(1)}, u32[]{:S(2)}, u32[]{:S(2)}) collective-permute-start(bf16[256,128]{1,0:T(8,128)(2,1)S(1)} %get-tuple-element.36), channel_id=1, source_target_pairs={{0,1},{1,0},{2,3},{3,2},{4,5},{5,4},{6,7},{7,6},{8,9},{9,8},{10,11... | collective-permute-start | bytes 196616 | tf_op jit(solution)/shard_map/ppermute | solution.py:24
  142.7 4.0 %collective-permute-start.25 = (bf16[256,128]{1,0:T(8,128)(2,1)S(1)}, bf16[256,128]{1,0:T(8,128)(2,1)S(1)}, u32[]{:S(2)}, u32[]{:S(2)}) collective-permute-start(bf16[256,128]{1,0:T(8,128)(2,1)S(1)} %get-tuple-element.22), channel_id=1, source_target_pairs={{0,3},{1,2},{2,1},{3,0},{4,7},{5,6},{6,5},{7,4},{8,11},{9,10},{10,... | collective-permute-start | bytes 196616 | tf_op jit(solution)/shard_map/ppermute | solution.py:24
  142.7 5.0 %collective-permute-start.24 = (bf16[256,128]{1,0:T(8,128)(2,1)S(1)}, bf16[256,128]{1,0:T(8,128)(2,1)S(1)}, u32[]{:S(2)}, u32[]{:S(2)}) collective-permute-start(bf16[256,128]{1,0:T(8,128)(2,1)S(1)} %get-tuple-element.23), channel_id=1, source_target_pairs={{0,2},{1,3},{2,0},{3,1},{4,6},{5,7},{6,4},{7,5},{8,10},{9,11},{10,... | collective-permute-start | bytes 196616 | tf_op jit(solution)/shard_map/ppermute | solution.py:24
  146.7 2.7 %collective-permute-start.23 = (bf16[256,128]{1,0:T(8,128)(2,1)S(1)}, bf16[256,128]{1,0:T(8,128)(2,1)S(1)}, u32[]{:S(2)}, u32[]{:S(2)}) collective-permute-start(bf16[256,128]{1,0:T(8,128)(2,1)S(1)} %get-tuple-element.24), channel_id=1, source_target_pairs={{0,1},{1,0},{2,3},{3,2},{4,5},{5,4},{6,7},{7,6},{8,9},{9,8},{10,11... | collective-permute-start | bytes 196616 | tf_op jit(solution)/shard_map/ppermute | solution.py:24
  147.6 4.1 %collective-permute-start.18 = (bf16[256,128]{1,0:T(8,128)(2,1)S(1)}, bf16[256,128]{1,0:T(8,128)(2,1)S(1)}, u32[]{:S(2)}, u32[]{:S(2)}) collective-permute-start(bf16[256,128]{1,0:T(8,128)(2,1)S(1)} %get-tuple-element.30), channel_id=1, source_target_pairs={{0,3},{1,2},{2,1},{3,0},{4,7},{5,6},{6,5},{7,4},{8,11},{9,10},{10,... | collective-permute-start | bytes 196616 | tf_op jit(solution)/shard_map/ppermute | solution.py:24
  148.5 5.0 %collective-permute-start.17 = (bf16[256,128]{1,0:T(8,128)(2,1)S(1)}, bf16[256,128]{1,0:T(8,128)(2,1)S(1)}, u32[]{:S(2)}, u32[]{:S(2)}) collective-permute-start(bf16[256,128]{1,0:T(8,128)(2,1)S(1)} %get-tuple-element.31), channel_id=1, source_target_pairs={{0,2},{1,3},{2,0},{3,1},{4,6},{5,7},{6,4},{7,5},{8,10},{9,11},{10,... | collective-permute-start | bytes 196616 | tf_op jit(solution)/shard_map/ppermute | solution.py:24
  149.4 5.2 %collective-permute-start.16 = (bf16[256,128]{1,0:T(8,128)(2,1)S(1)}, bf16[256,128]{1,0:T(8,128)(2,1)S(1)}, u32[]{:S(2)}, u32[]{:S(2)}) collective-permute-start(bf16[256,128]{1,0:T(8,128)(2,1)S(1)} %get-tuple-element.32), channel_id=1, source_target_pairs={{0,1},{1,0},{2,3},{3,2},{4,5},{5,4},{6,7},{7,6},{8,9},{9,8},{10,11... | collective-permute-start | bytes 196616 | tf_op jit(solution)/shard_map/ppermute | solution.py:24
  151.7 3.8 %collective-permute-start.22 = (bf16[256,128]{1,0:T(8,128)(2,1)S(1)}, bf16[256,128]{1,0:T(8,128)(2,1)S(1)}, u32[]{:S(2)}, u32[]{:S(2)}) collective-permute-start(bf16[256,128]{1,0:T(8,128)(2,1)S(1)} %get-tuple-element.26), channel_id=1, source_target_pairs={{0,3},{1,2},{2,1},{3,0},{4,7},{5,6},{6,5},{7,4},{8,11},{9,10},{10,... | collective-permute-start | bytes 196616 | tf_op jit(solution)/shard_map/ppermute | solution.py:24
  153.4 5.6 %collective-permute-start.21 = (bf16[256,128]{1,0:T(8,128)(2,1)S(1)}, bf16[256,128]{1,0:T(8,128)(2,1)S(1)}, u32[]{:S(2)}, u32[]{:S(2)}) collective-permute-start(bf16[256,128]{1,0:T(8,128)(2,1)S(1)} %get-tuple-element.27), channel_id=1, source_target_pairs={{0,2},{1,3},{2,0},{3,1},{4,6},{5,7},{6,4},{7,5},{8,10},{9,11},{10,... | collective-permute-start | bytes 196616 | tf_op jit(solution)/shard_map/ppermute | solution.py:24
  154.6 12.6 %collective-permute-start.26 = (bf16[4,256,128]{2,1,0:T(8,128)(2,1)S(1)}, bf16[4,256,128]{2,1,0:T(8,128)(2,1)S(1)}, u32[]{:S(2)}, u32[]{:S(2)}) collective-permute-start(bf16[4,256,128]{2,1,0:T(8,128)(2,1)S(1)} %pad_maximum_fusion.3), channel_id=1, source_target_pairs={{0,4},{4,0},{8,12},{12,8},{1,5},{5,1},{9,13},{13,9},{2,6},{6,2},{1... | collective-permute-start | bytes 786440 | tf_op jit(solution)/shard_map/ppermute | solution.py:24
  155.5 15.5 %collective-permute-start.12 = (bf16[4,256,128]{2,1,0:T(8,128)(2,1)S(1)}, bf16[4,256,128]{2,1,0:T(8,128)(2,1)S(1)}, u32[]{:S(2)}, u32[]{:S(2)}) collective-permute-start(bf16[4,256,128]{2,1,0:T(8,128)(2,1)S(1)} %pad_maximum_fusion), channel_id=1, source_target_pairs={{0,8},{4,12},{8,0},{12,4},{1,9},{5,13},{9,1},{13,5},{2,10},{6,14},... | collective-permute-start | bytes 786440 | tf_op jit(solution)/shard_map/ppermute | solution.py:24
  159.0 1.3 collective-permute-start.20

commit v2 on v1

--- a/solution.py
+++ b/solution.py
@@ -24,10 +24,10 @@
     return lax.ppermute(value, axis, [(i, i ^ mask) for i in range(count)])
 
 
-def swapped_by_parity(value, masks):
+def sent(value, masks, hop):
     seq, heads = lax.axis_size("seq"), lax.axis_size("head")
     moves = [
-        (s * heads + h, (s ^ masks[h % 2]) * heads + h)
+        (s * heads + h, (s ^ masks[h % 2]) * heads + (h ^ hop))
         for s in range(seq)
         for h in range(heads)
     ]
@@ -193,47 +193,49 @@
         scratch_shapes=[pltpu.SemaphoreType.DMA((count * (rows // width),))],
         compiler_params=pltpu.CompilerParams(vmem_limit_bytes=4 << 20),
         name="sheaf",
-    )(*[in_hbm(weight) for weight in weights])
-
-
-def product(left_ref, rights_ref, mask, columns):
-    count, _, width = left_ref.shape
+    )(*weights)
+
+
+def product(left_refs, rights_ref, mask, columns):
     origin = lax.axis_index("seq") ^ mask
-    depth = count * width
-    left = jnp.concatenate([left_ref[j] for j in range(count)], axis=1)
+    depth = len(left_refs) * left_refs[0].shape[1]
+    left = jnp.concatenate([ref[...] for ref in left_refs], axis=1)
     right = rights_ref[pl.ds(pl.multiple_of(origin * depth, depth), depth), columns]
     return jnp.dot(left, right, preferred_element_type=jnp.float32)
 
 
-def project_body(masks, tile, rights_ref, *refs):
+def project_body(masks, count, tile, rights_ref, *refs):
     lefts, o_ref = refs[:-1], refs[-1]
     for first in range(0, o_ref.shape[1], tile):
         columns = pl.ds(first, tile)
         total = None
-        for left_ref, mask in zip(lefts, masks):
-            term = product(left_ref, rights_ref, mask, columns)
+        for at, mask in enumerate(masks):
+            group = lefts[at * count : (at + 1) * count]
+            term = product(group, rights_ref, mask, columns)
             total = term if total is None else total + term
         o_ref[:, columns] = total
 
 
 def project(lefts, masks, rights):
-    rows, columns = lefts[0].shape[1], rights.shape[1]
+    count = len(lefts[0])
+    rows, columns = lefts[0][0].shape[0], rights.shape[1]
     inside = pl.BlockSpec(memory_space=pltpu.VMEM)
     return pl.pallas_call(
-        functools.partial(project_body, masks, math.gcd(512, columns)),
+        functools.partial(project_body, masks, count, math.gcd(512, columns)),
         out_shape=pltpu.VMEM((rows, columns), jnp.float32),
-        in_specs=[inside] * (1 + len(lefts)),
+        in_specs=[inside] * (1 + len(lefts) * count),
         out_specs=inside,
         compiler_params=pltpu.CompilerParams(vmem_limit_bytes=24 << 20),
         name="project",
-    )(rights, *lefts)
-
-
-def finish_body(mask, tile, left_ref, rights_ref, part_ref, o_ref, held, sems):
+    )(rights, *[block for group in lefts for block in group])
+
+
+def finish_body(mask, tile, rights_ref, part_ref, *refs):
+    lefts, (o_ref, held, sems) = refs[:-3], refs[-3:]
     copies = []
     for n in range(part_ref.shape[1] // tile):
         columns = pl.ds(n * tile, tile)
-        term = product(left_ref, rights_ref, mask, columns)
+        term = product(lefts, rights_ref, mask, columns)
         held[:, columns] = (part_ref[:, columns] + term).astype(held.dtype)
         copies.append(
             pltpu.make_async_copy(held.at[:, columns], o_ref.at[:, columns], sems.at[n])
@@ -243,13 +245,13 @@
         copy.wait()
 
 
-def finish(left, mask, rights, part, dtype):
+def finish(lefts, mask, rights, part, dtype):
     tile = math.gcd(512, part.shape[1])
     inside = pl.BlockSpec(memory_space=pltpu.VMEM)
     return pl.pallas_call(
         functools.partial(finish_body, mask, tile),
         out_shape=jax.ShapeDtypeStruct(part.shape, dtype),
-        in_specs=[inside] * 3,
+        in_specs=[inside] * (2 + len(lefts)),
         out_specs=pl.BlockSpec(memory_space=pl.ANY),
         scratch_shapes=[
             pltpu.VMEM(part.shape, dtype),
@@ -257,7 +259,7 @@
         ],
         compiler_params=pltpu.CompilerParams(vmem_limit_bytes=24 << 20),
         name="finish",
-    )(left, rights, part)
+    )(rights, part, *lefts)
 
 
 def rounds_of(seq):
@@ -292,7 +294,7 @@
     pairs = []
     for masks in rounds:
         (outgoing,) = cut(arrays, [((0, 1), masks)], width)
-        pairs.append(swapped_by_parity(outgoing, masks))
+        pairs.append(sent(outgoing, masks, 0))
     kept = [((0, 1), (0, 0)), ((2,), (0, 0))] + [((2,), (m, m)) for m in order]
     own_pair, own_queries, *queries_for = cut(arrays, kept, width)
     pairs = [own_pair] + pairs
@@ -314,12 +316,14 @@
             slot = jnp.where(apart == jnp.where(even, a, b), r + 1, slot)
         return slot * qblocks + ids % qblocks
 
-    def split(block):
+    def split(block, mask):
         got = []
         for hop in range(heads):
             mine = lax.dynamic_slice_in_dim(block, (head ^ hop) * share, share, axis=0)
-            got.append(swapped(mine, "head", hop) if hop else mine)
-        return jnp.stack(got)
+            if mask or hop:
+                mine = sent(mine, (mask, mask), hop)
+            got.append(mine)
+        return got
 
     ready, before = {}, None
     for mask in [0] + order:
@@ -327,12 +331,7 @@
         if before is not None:
             slots, before = chained(slots, before)
         mixed = before = attend(asked[mask], pooled, slots)
-        if mask and mask != 1 and mask != order[-1]:
-            ready[mask] = split(swapped(mixed, "seq", mask))
-        elif mask:
-            ready[mask] = swapped(split(mixed), "seq", mask)
-        else:
-            ready[mask] = split(mixed)
+        ready[mask] = split(mixed, mask)
     tail = order[-1]
     early = [mask for mask in [0] + order if mask != tail]
     rights = sheaf([weights[hop] for hop in range(heads)], width)

time: 173 us -> 171 us (0.988)
  waiting for transfers between devices: 93.7 us -> 90.9 us
  local copies, waits for them, and re-layouts: 0.88 us -> 2.99 us
    ppermute x3 -> x18, starting transfers between devices: 4.61 us -> 25.1 us  [sent(): return lax.ppermute(value, ('seq', 'head'), moves)]
    ppermute x24 -> x9, starting transfers between devices: 43.7 us -> 23.4 us  [swapped(): return lax.ppermute(value, axis, [(i, i ^ mask) for i in range(count)])]
    ppermute x24 -> x9, waiting for transfers between devices: 66.2 us -> 57.1 us  [swapped(): return lax.ppermute(value, axis, [(i, i ^ mask) for i in range(count)])]
    ppermute x3 -> x18, waiting for transfers between devices: 27.5 us -> 33.8 us  [sent(): return lax.ppermute(value, ('seq', 'head'), moves)]
    unnamed x6 -> x12, local copies, waits for them, and re-layouts: 0.8 us -> 2.91 us
  transfers between devices with their start and end apart: 27 -> 27, of which waited for: 13 -> 10; matrix products, arithmetic and copies ran while one was open for 0% -> 0% of each run, Pallas kernels for 16% -> 16%
where the time goes in v2:
time: 171 us
  waiting for transfers between devices  90.9 us (53%)
  starting transfers between devices  48.5 us (28%)
  Pallas kernels  28.1 us (16%)
  local copies, waits for them, and re-layouts  2.99 us (2%)
    ppermute x9, waiting for transfers between devices, swapped(): return lax.ppermute(value, axis, [(i, i ^ mask) for i in range(count)])  57.1 us
    ppermute x18, waiting for transfers between devices, sent(): return lax.ppermute(value, ('seq', 'head'), moves)  33.8 us
    ppermute x18, starting transfers between devices, sent(): return lax.ppermute(value, ('seq', 'head'), moves)  25.1 us
    ppermute x9, starting transfers between devices, swapped(): return lax.ppermute(value, axis, [(i, i ^ mask) for i in range(count)])  23.4 us
    pallas_call x4, Pallas kernels, attend(): pl.pallas_call(attend_body, out_shape=jax.ShapeDtypeStruct(queries.shape,...  15.1 us
    pallas_call x4, Pallas kernels, cut(): pl.pallas_call(functools.partial(cut_body, plan, width), out_shape=[pltpu...  5.88 us
  transfers between devices with their start and end apart: 27, of which 10 were waited for; matrix products, arithmetic and copies ran while one was open for 0% of the time, Pallas kernels for 16%

profile of v2, /device:TPU:0, one launch (start us, length us, event | category | flops | bytes accessed | tf_op | source)
XLA Modules:
  0.0 171.0 jit_solution(16450312577719852262)
XLA Ops:
  0.0 3.0 %collective-permute-start.1 = (bf16[512,2048]{1,0:T(8,128)(2,1)}, bf16[512,2048]{1,0:T(8,128)(2,1)S(1)}, u32[]{:S(2)}, u32[]{:S(2)}) collective-permute-start(bf16[512,2048]{1,0:T(8,128)(2,1)} %refs_0_.5), channel_id=1, source_target_pairs={{0,2},{1,3},{2,0},{3,1},{4,6},{5,7},{6,4},{7,5},{8,10},{9,11},{10,... | collective-permute-start | bytes 6291464 | tf_op jit(solution)/shard_map/ppermute | solution.py:24
  3.0 0.0 collective-permute-start
  3.0 45.8 %collective-permute-done.1.refs_2_ = bf16[512,2048]{1,0:T(8,128)(2,1)S(1)} collective-permute-done((bf16[512,2048]{1,0:T(8,128)(2,1)}, bf16[512,2048]{1,0:T(8,128)(2,1)S(1)}, u32[]{:S(2)}, u32[]{:S(2)}) %collective-permute-start.1) | collective-permute-done | bytes 2097184 | tf_op jit(solution)/shard_map/ppermute | solution.py:24
  48.8 0.0 collective-permute-start.2
  48.8 1.1 cut.5
  50.0 1.9 %collective-permute-start.3 = (bf16[2,1024,128]{2,1,0:T(8,128)(2,1)S(1)}, bf16[2,1024,128]{2,1,0:T(8,128)(2,1)}, u32[]{:S(2)}, u32[]{:S(2)}) collective-permute-start(bf16[2,1024,128]{2,1,0:T(8,128)(2,1)S(1)} %cut.5), channel_id=1, source_target_pairs={{0,4},{1,9},{2,6},{3,11},{4,0},{5,13},{6,2},{7,15},{8,12},{9,1},{1... | collective-permute-start | bytes 1572872 | tf_op jit(solution)/shard_map/ppermute | solution.py:34
  51.9 2.5 %collective-permute-start.9 = (s32[8,15]{1,0:T(8,128)S(1)}, s32[8,15]{1,0:T(8,128)S(1)}, u32[]{:S(2)}, u32[]{:S(2)}) collective-permute-start(s32[8,15]{1,0:T(8,128)S(1)} %copy-done.5), channel_id=1, source_target_pairs={{0,12},{4,8},{8,4},{12,0},{1,13},{5,9},{9,5},{13,1},{2,14},{6,10},... | collective-permute-start | bytes 1448 | tf_op jit(solution)/shard_map/ppermute | solution.py:24
  54.3 0.7 collective-permute-start.15
  55.0 1.1 cut.6
  56.2 10.5 %collective-permute-done.9 = s32[8,15]{1,0:T(8,128)S(1)} collective-permute-done((s32[8,15]{1,0:T(8,128)S(1)}, s32[8,15]{1,0:T(8,128)S(1)}, u32[]{:S(2)}, u32[]{:S(2)}) %collective-permute-start.9) | collective-permute-done | bytes 512 | tf_op jit(solution)/shard_map/ppermute | solution.py:24
  66.7 0.0 collective-permute-start.4
  66.7 1.9 %cut.7 = bf16[2,1024,128]{2,1,0:T(8,128)(2,1)} custom-call(bf16[1024,512]{1,0:T(8,128)(2,1)} %refs_0_.9, bf16[1024,512]{1,0:T(8,128)(2,1)} %refs_1_.7, bf16[1024,512]{1,0:T(8,128)(2,1)} %refs_2_.7), custom_call_target="tpu_custom_call" | custom-call | tf_op jit(solution)/shard_map/cut/pallas_call | solution.py:80
  68.6 0.0 collective-permute-done.15
  68.6 1.6 collective-permute-start.5
  70.2 1.6 cut.4
  71.8 0.0 copy-start.1
  71.9 0.8 copy-done.1
  72.6 0.7 copy-done.2
  73.3 0.7 copy-done.3
  74.1 0.7 copy-done.4
  74.8 0.0 collective-permute-done.3.refs_1_
  74.8 2.4 %collective-permute-start.10 = (bf16[1024,128]{1,0:T(8,128)(2,1)}, bf16[1024,128]{1,0:T(8,128)(2,1)S(1)}, u32[]{:S(2)}, u32[]{:S(2)}) collective-permute-start(bf16[1024,128]{1,0:T(8,128)(2,1)} %copy-done.4), channel_id=1, source_target_pairs={{0,12},{4,8},{8,4},{12,0},{1,13},{5,9},{9,5},{13,1},{2,14},{6,10},... | collective-permute-start | bytes 786440 | tf_op jit(solution)/shard_map/ppermute | solution.py:24
  77.2 26.4 %collective-permute-done.4.refs_2_ = bf16[2,1024,128]{2,1,0:T(8,128)(2,1)} collective-permute-done((bf16[2,1024,128]{2,1,0:T(8,128)(2,1)S(1)}, bf16[2,1024,128]{2,1,0:T(8,128)(2,1)}, u32[]{:S(2)}, u32[]{:S(2)}) %collective-permute-start.4) | collective-permute-done | bytes 524320 | tf_op jit(solution)/shard_map/ppermute | solution.py:34
  103.6 0.0 collective-permute-start.16
  103.6 0.0 collective-permute-done.5.refs_3_
  103.6 14.8 %collective-permute-start.22 = (bf16[1024,128]{1,0:T(8,128)(2,1)}, bf16[1024,128]{1,0:T(8,128)(2,1)S(1)}, u32[]{:S(2)}, u32[]{:S(2)}) collective-permute-start(bf16[1024,128]{1,0:T(8,128)(2,1)} %copy-done.2), channel_id=1, source_target_pairs={{0,8},{4,12},{8,0},{12,4},{1,9},{5,13},{9,1},{13,5},{2,10},{6,14},... | collective-permute-start | bytes 786440 | tf_op jit(solution)/shard_map/ppermute | solution.py:24
  118.4 1.6 pool.1.kv
  120.0 3.7 %attend.4 = bf16[1024,128]{1,0:T(8,128)(2,1)S(1)} custom-call(s32[8,15]{1,0:T(8,128)S(1)} %fusion.1.slots, bf16[1024,128]{1,0:T(8,128)(2,1)S(1)} %get-tuple-element.13.q_ref, bf16[2,4096,128]{2,1,0:T(8,128)(2,1)S(1)} %pool.1.kv), custom_call_target="tpu_custom_call" | custom-call | tf_op jit(solution)/shard_map/attend/pallas_call | solution.py:154
  123.7 0.0 collective-permute-done.10.q_ref
  123.7 0.1 collective-permute-start.21
  123.8 3.7 %attend.5 = bf16[1024,128]{1,0:T(8,128)(2,1)S(1)} custom-call(s32[8,15]{1,0:T(8,128)S(1)} %fusion.3.slots, bf16[1024,128]{1,0:T(8,128)(2,1)S(1)} %collective-permute-done.10.q_ref, bf16[2,4096,128]{2,1,0:T(8,128)(2,1)S(1)} %pool.1.kv), custom_call_target="tpu_custom_call" | custom-call | tf_op jit(solution)/shard_map/attend/pallas_call | solution.py:154
  127.6 0.7 collective-permute-done.21
  128.3 0.0 collective-permute-start.6
  128.3 0.0 collective-permute-done.16.q_ref
  128.3 1.6 collective-permute-start.7
  129.9 0.4 collective-permute-start.8
  130.2 2.2 %collective-permute-start.11 = (bf16[256,128]{1,0:T(8,128)(2,1)S(1)}, bf16[256,128]{1,0:T(8,128)(2,1)S(1)}, u32[]{:S(2)}, u32[]{:S(2)}) collective-permute-start(bf16[256,128]{1,0:T(8,128)(2,1)S(1)} %get-tuple-element.32), channel_id=1, source_target_pairs={{0,12},{1,13},{2,14},{3,15},{4,8},{5,9},{6,10},{7,11},{8,4},{9,5},... | collective-permute-start | bytes 196616 | tf_op jit(solution)/shard_map/ppermute | solution.py:34
  132.5 3.7 %attend.6 = bf16[1024,128]{1,0:T(8,128)(2,1)S(1)} custom-call(s32[8,15]{1,0:T(8,128)S(1)} %fusion.5.slots, bf16[1024,128]{1,0:T(8,128)(2,1)S(1)} %collective-permute-done.16.q_ref, bf16[2,4096,128]{2,1,0:T(8,128)(2,1)S(1)} %pool.1.kv), custom_call_target="tpu_custom_call" | custom-call | tf_op jit(solution)/shard_map/attend/pallas_call | solution.py:154
  136.2 0.0 copy-start
  136.2 3.9 %attend.7 = bf16[1024,128]{1,0:T(8,128)(2,1)S(1)} custom-call(s32[8,15]{1,0:T(8,128)S(1)} %fusion.7.slots, bf16[1024,128]{1,0:T(8,128)(2,1)S(1)} %collective-permute-done.22.q_ref, bf16[2,4096,128]{2,1,0:T(8,128)(2,1)S(1)} %pool.1.kv), custom_call_target="tpu_custom_call" | custom-call | tf_op jit(solution)/shard_map/attend/pallas_call | solution.py:154
  140.1 0.0 collective-permute-done.7.refs_2_
  140.1 1.3 collective-permute-start.12
  141.4 0.0 collective-permute-done.8.refs_3_
  141.4 3.1 %collective-permute-start.13 = (bf16[256,128]{1,0:T(8,128)(2,1)S(1)}, bf16[256,128]{1,0:T(8,128)(2,1)S(1)}, u32[]{:S(2)}, u32[]{:S(2)}) collective-permute-start(bf16[256,128]{1,0:T(8,128)(2,1)S(1)} %get-tuple-element.30), channel_id=1, source_target_pairs={{0,14},{1,15},{2,12},{3,13},{4,10},{5,11},{6,8},{7,9},{8,6},{9,7},... | collective-permute-start | bytes 196616 | tf_op jit(solution)/shard_map/ppermute | solution.py:34
  144.6 1.4 collective-permute-start.14
  146.0 0.3 collective-permute-done.12.refs_5_
  146.3 0.0 collective-permute-start.17
  146.3 2.5 %collective-permute-done.13.refs_6_ = bf16[256,128]{1,0:T(8,128)(2,1)S(1)} collective-permute-done((bf16[256,128]{1,0:T(8,128)(2,1)S(1)}, bf16[256,128]{1,0:T(8,128)(2,1)S(1)}, u32[]{:S(2)}, u32[]{:S(2)}) %collective-permute-start.13) | collective-permute-done | bytes 65568 | tf_op jit(solution)/shard_map/ppermute | solution.py:34
  148.8 1.0 collective-permute-start.18
  149.8 1.5 collective-permute-done.14.refs_7_
  151.4 2.1 %collective-permute-start.19 = (bf16[256,128]{1,0:T(8,128)(2,1)S(1)}, bf16[256,128]{1,0:T(8,128)(2,1)S(1)}, u32[]{:S(2)}, u32[]{:S(2)}) collective-permute-start(bf16[256,128]{1,0:T(8,128)(2,1)S(1)} %get-tuple-element.26), channel_id=1, source_target_pairs={{0,6},{1,7},{2,4},{3,5},{4,2},{5,3},{6,0},{7,1},{8,14},{9,15},{10,... | collective-permute-start | bytes 196616 | tf_op jit(solution)/shard_map/ppermute | solution.py:34
  153.5 0.8 collective-permute-start.20
  154.3 0.0 collective-permute-done.18.refs_9_
  154.3 2.0 %collective-permute-start.23 = (bf16[256,128]{1,0:T(8,128)(2,1)S(1)}, bf16[256,128]{1,0:T(8,128)(2,1)S(1)}, u32[]{:S(2)}, u32[]{:S(2)}) collective-permute-start(bf16[256,128]{1,0:T(8,128)(2,1)S(1)} %get-tuple-element.24), channel_id=1, source_target_pairs={{0,8},{1,9},{2,10},{3,11},{4,12},{5,13},{6,14},{7,15},{8,0},{9,1},... | collective-permute-start | bytes 196616 | tf_op jit(solution)/shard_map/ppermute | solution.py:34
  156.3 0.6 collective-permute-done.19.refs_10_
  156.8 0.6 collective-permute-start.24
  157.4 1.9 %collective-permute-start.25 = (bf16[256,128]{1,0:T(8,128)(2,1)S(1)}, bf16[256,128]{1,0:T(8,128)(2,1)S(1)}, u32[]{:S(2)}, u32[]{:S(2)}) collective-permute-start(bf16[256,128]{1,0:T(8,128)(2,1)S(1)} %get-tuple-element.22), channel_id=1, source_target_pairs={{0,10},{1,11},{2,8},{3,9},{4,14},{5,15},{6,12},{7,13},{8,2},{9,3},... | collective-permute-start | bytes 196616 | tf_op jit(solution)/shard_map/ppermute | solution.py:34
  159.3 3.4 %collective-permute-start.26 = (bf16[256,128]{1,0:T(8,128)(2,1)S(1)}, bf16[256,128]{1,0:T(8,128)(2,1)S(1)}, u32[]{:S(2)}, u32[]{:S(2)}) collective-permute-start(bf16[256,128]{1,0:T(8,128)(2,1)S(1)} %get-tuple-element.21), channel_id=1, source_target_pairs={{0,11},{1,10},{2,9},{3,8},{4,15},{5,14},{6,13},{7,12},{8,3},{9,2},... | collective-permute-start | bytes 196616 | tf_op jit(solution)/shard_map/ppermute | solution.py:34
  162.7 2.4 %sheaf.1.rights_ref = bf16[2048,2048]{1,0:T(8,128)(2,1)S(1)} custom-call(bf16[512,2048]{1,0:T(8,128)(2,1)S(1)} %copy-done, bf16[512,2048]{1,0:T(8,128)(2,1)} %collective-permute-done.refs_1_, bf16[512,2048]{1,0:T(8,128)(2,1)S(1)} %collective-permute-done.1.refs_2_, bf16[512,2048]{1,0:T(8,128)(2,1)} %collective-permute-done.2.refs_3_), custom_call_target="tpu_custom_call" | custom-call | tf_op jit(solution)/shard_map/sheaf/pallas_call | solution.py:188
  165.1 1.8 %project.1.part_ref = f32[256,2048]{1,0:T(8,128)S(1)} custom-call(bf16[2048,2048]{1,0:T(8,128)(2,1)S(1)} %sheaf.1.rights_ref, bf16[256,128]{1,0:T(8,128)(2,1)S(1)} %get-tuple-element.36.refs_0_, bf16[256,128]{1,0:T(8,128)(2,1)S(1)} %collective-permute-done.6.refs_1_, bf16[256,128]{1,0:T(8,128)(2,1)S(1)} %collective-permute-done.7.refs_2_, ...), custom_call_target="tpu_custom_call" | custom-call | tf_op jit(solution)/shard_map/project/pallas_call | solution.py:223
  166.9 0.0 collective-permute-done.23.refs_0_
  166.9 1.1 collective-permute-done.25.refs_2_
  168.0 1.4 collective-permute-done.26.refs_3_
  169.4 1.5 finish.1
  (22 shorter events, 0.2 us)
Async XLA Ops:
  0.0 51.9 %copy-start.5 = (s32[8,15]{1,0:T(8,128)S(1)}, s32[8,15]{1,0:T(8,128)}, u32[]{:S(2)}) copy-start(s32[8,15]{1,0:T(8,128)} %param.8) | copy-start | bytes 1444
  0.0 48.8 %collective-permute-start.1 = (bf16[512,2048]{1,0:T(8,128)(2,1)}, bf16[512,2048]{1,0:T(8,128)(2,1)S(1)}, u32[]{:S(2)}, u32[]{:S(2)}) collective-permute-start(bf16[512,2048]{1,0:T(8,128)(2,1)} %refs_0_.5), channel_id=1, source_target_pairs={{0,2},{1,3},{2,0},{3,1},{4,6},{5,7},{6,4},{7,5},{8,10},{9,11},{10,... | collective-permute-start | bytes 6291464 | tf_op jit(solution)/shard_map/ppermute | solution.py:24
  3.0 154.4 %collective-permute-start = (bf16[512,2048]{1,0:T(8,128)(2,1)}, bf16[512,2048]{1,0:T(8,128)(2,1)}, u32[]{:S(2)}, u32[]{:S(2)}) collective-permute-start(bf16[512,2048]{1,0:T(8,128)(2,1)} %refs_0_.5), channel_id=1, source_target_pairs={{0,1},{1,0},{2,3},{3,2},{4,5},{5,4},{6,7},{7,6},{8,9},{9,8},{10,11... | collective-permute-start | bytes 6291464 | tf_op jit(solution)/shard_map/ppermute | solution.py:24
  48.8 110.5 %collective-permute-start.2 = (bf16[512,2048]{1,0:T(8,128)(2,1)S(1)}, bf16[512,2048]{1,0:T(8,128)(2,1)}, u32[]{:S(2)}, u32[]{:S(2)}) collective-permute-start(bf16[512,2048]{1,0:T(8,128)(2,1)S(1)} %collective-permute-done.1.refs_2_), channel_id=1, source_target_pairs={{0,1},{1,0},{2,3},{3,2},{4,5},{5,4},{6,7},{7,6},{8,9},{9,8},{10,11... | collective-permute-start | bytes 6291464 | tf_op jit(solution)/shard_map/ppermute | solution.py:24
  50.0 24.8 %collective-permute-start.3 = (bf16[2,1024,128]{2,1,0:T(8,128)(2,1)S(1)}, bf16[2,1024,128]{2,1,0:T(8,128)(2,1)}, u32[]{:S(2)}, u32[]{:S(2)}) collective-permute-start(bf16[2,1024,128]{2,1,0:T(8,128)(2,1)S(1)} %cut.5), channel_id=1, source_target_pairs={{0,4},{1,9},{2,6},{3,11},{4,0},{5,13},{6,2},{7,15},{8,12},{9,1},{1... | collective-permute-start | bytes 1572872 | tf_op jit(solution)/shard_map/ppermute | solution.py:34
  51.9 14.8 %collective-permute-start.9 = (s32[8,15]{1,0:T(8,128)S(1)}, s32[8,15]{1,0:T(8,128)S(1)}, u32[]{:S(2)}, u32[]{:S(2)}) collective-permute-start(s32[8,15]{1,0:T(8,128)S(1)} %copy-done.5), channel_id=1, source_target_pairs={{0,12},{4,8},{8,4},{12,0},{1,13},{5,9},{9,5},{13,1},{2,14},{6,10},... | collective-permute-start | bytes 1448 | tf_op jit(solution)/shard_map/ppermute | solution.py:24
  54.3 14.3 %collective-permute-start.15 = (s32[8,15]{1,0:T(8,128)S(1)}, s32[8,15]{1,0:T(8,128)S(1)}, u32[]{:S(2)}, u32[]{:S(2)}) collective-permute-start(s32[8,15]{1,0:T(8,128)S(1)} %copy-done.5), channel_id=1, source_target_pairs={{0,4},{4,0},{8,12},{12,8},{1,5},{5,1},{9,13},{13,9},{2,6},{6,2},{1... | collective-permute-start | bytes 1448 | tf_op jit(solution)/shard_map/ppermute | solution.py:24
  66.7 36.9 %collective-permute-start.4 = (bf16[2,1024,128]{2,1,0:T(8,128)(2,1)S(1)}, bf16[2,1024,128]{2,1,0:T(8,128)(2,1)}, u32[]{:S(2)}, u32[]{:S(2)}) collective-permute-start(bf16[2,1024,128]{2,1,0:T(8,128)(2,1)S(1)} %cut.6), channel_id=1, source_target_pairs={{0,8},{1,5},{2,10},{3,7},{4,12},{5,1},{6,14},{7,3},{8,0},{9,13},{1... | collective-permute-start | bytes 1572872 | tf_op jit(solution)/shard_map/ppermute | solution.py:34
  68.6 35.0 %collective-permute-start.5 = (bf16[2,1024,128]{2,1,0:T(8,128)(2,1)}, bf16[2,1024,128]{2,1,0:T(8,128)(2,1)}, u32[]{:S(2)}, u32[]{:S(2)}) collective-permute-start(bf16[2,1024,128]{2,1,0:T(8,128)(2,1)} %cut.7), channel_id=1, source_target_pairs={{0,12},{1,13},{2,14},{3,15},{4,8},{5,9},{6,10},{7,11},{8,4},{9,5},... | collective-permute-start | bytes 1572872 | tf_op jit(solution)/shard_map/ppermute | solution.py:34
  71.8 0.8 copy-start.1
  72.6 0.7 copy-start.2
  73.3 0.7 copy-start.3
  74.0 0.7 copy-start.4
  74.8 48.9 %collective-permute-start.10 = (bf16[1024,128]{1,0:T(8,128)(2,1)}, bf16[1024,128]{1,0:T(8,128)(2,1)S(1)}, u32[]{:S(2)}, u32[]{:S(2)}) collective-permute-start(bf16[1024,128]{1,0:T(8,128)(2,1)} %copy-done.4), channel_id=1, source_target_pairs={{0,12},{4,8},{8,4},{12,0},{1,13},{5,9},{9,5},{13,1},{2,14},{6,10},... | collective-permute-start | bytes 786440 | tf_op jit(solution)/shard_map/ppermute | solution.py:24
  103.6 24.7 %collective-permute-start.16 = (bf16[1024,128]{1,0:T(8,128)(2,1)}, bf16[1024,128]{1,0:T(8,128)(2,1)S(1)}, u32[]{:S(2)}, u32[]{:S(2)}) collective-permute-start(bf16[1024,128]{1,0:T(8,128)(2,1)} %copy-done.3), channel_id=1, source_target_pairs={{0,4},{4,0},{8,12},{12,8},{1,5},{5,1},{9,13},{13,9},{2,6},{6,2},{1... | collective-permute-start | bytes 786440 | tf_op jit(solution)/shard_map/ppermute | solution.py:24
  103.6 26.3 %collective-permute-start.22 = (bf16[1024,128]{1,0:T(8,128)(2,1)}, bf16[1024,128]{1,0:T(8,128)(2,1)S(1)}, u32[]{:S(2)}, u32[]{:S(2)}) collective-permute-start(bf16[1024,128]{1,0:T(8,128)(2,1)} %copy-done.2), channel_id=1, source_target_pairs={{0,8},{4,12},{8,0},{12,4},{1,9},{5,13},{9,1},{13,5},{2,10},{6,14},... | collective-permute-start | bytes 786440 | tf_op jit(solution)/shard_map/ppermute | solution.py:24
  123.7 4.6 %collective-permute-start.21 = (s32[8,15]{1,0:T(8,128)S(1)}, s32[8,15]{1,0:T(8,128)S(1)}, u32[]{:S(2)}, u32[]{:S(2)}) collective-permute-start(s32[8,15]{1,0:T(8,128)S(1)} %copy-done.5), channel_id=1, source_target_pairs={{0,8},{4,12},{8,0},{12,4},{1,9},{5,13},{9,1},{13,5},{2,10},{6,14},... | collective-permute-start | bytes 1448 | tf_op jit(solution)/shard_map/ppermute | solution.py:24
  128.3 2.0 %collective-permute-start.6 = (bf16[256,128]{1,0:T(8,128)(2,1)S(1)}, bf16[256,128]{1,0:T(8,128)(2,1)S(1)}, u32[]{:S(2)}, u32[]{:S(2)}) collective-permute-start(bf16[256,128]{1,0:T(8,128)(2,1)S(1)} %get-tuple-element.35), channel_id=1, source_target_pairs={{0,1},{1,0},{2,3},{3,2},{4,5},{5,4},{6,7},{7,6},{8,9},{9,8},{10,11... | collective-permute-start | bytes 196616 | tf_op jit(solution)/shard_map/ppermute | solution.py:34
  128.3 11.8 %collective-permute-start.7 = (bf16[256,128]{1,0:T(8,128)(2,1)S(1)}, bf16[256,128]{1,0:T(8,128)(2,1)S(1)}, u32[]{:S(2)}, u32[]{:S(2)}) collective-permute-start(bf16[256,128]{1,0:T(8,128)(2,1)S(1)} %get-tuple-element.34), channel_id=1, source_target_pairs={{0,2},{1,3},{2,0},{3,1},{4,6},{5,7},{6,4},{7,5},{8,10},{9,11},{10,... | collective-permute-start | bytes 196616 | tf_op jit(solution)/shard_map/ppermute | solution.py:34
  129.9 11.6 %collective-permute-start.8 = (bf16[256,128]{1,0:T(8,128)(2,1)S(1)}, bf16[256,128]{1,0:T(8,128)(2,1)S(1)}, u32[]{:S(2)}, u32[]{:S(2)}) collective-permute-start(bf16[256,128]{1,0:T(8,128)(2,1)S(1)} %get-tuple-element.33), channel_id=1, source_target_pairs={{0,3},{1,2},{2,1},{3,0},{4,7},{5,6},{6,5},{7,4},{8,11},{9,10},{10,... | collective-permute-start | bytes 196616 | tf_op jit(solution)/shard_map/ppermute | solution.py:34
  130.2 14.3 %collective-permute-start.11 = (bf16[256,128]{1,0:T(8,128)(2,1)S(1)}, bf16[256,128]{1,0:T(8,128)(2,1)S(1)}, u32[]{:S(2)}, u32[]{:S(2)}) collective-permute-start(bf16[256,128]{1,0:T(8,128)(2,1)S(1)} %get-tuple-element.32), channel_id=1, source_target_pairs={{0,12},{1,13},{2,14},{3,15},{4,8},{5,9},{6,10},{7,11},{8,4},{9,5},... | collective-permute-start | bytes 196616 | tf_op jit(solution)/shard_map/ppermute | solution.py:34
  136.2 26.5 %copy-start = (bf16[512,2048]{1,0:T(8,128)(2,1)S(1)}, bf16[512,2048]{1,0:T(8,128)(2,1)}, u32[]{:S(2)}) copy-start(bf16[512,2048]{1,0:T(8,128)(2,1)} %refs_0_.5) | copy-start | bytes 6291460
  140.1 6.2 %collective-permute-start.12 = (bf16[256,128]{1,0:T(8,128)(2,1)S(1)}, bf16[256,128]{1,0:T(8,128)(2,1)S(1)}, u32[]{:S(2)}, u32[]{:S(2)}) collective-permute-start(bf16[256,128]{1,0:T(8,128)(2,1)S(1)} %get-tuple-element.31), channel_id=1, source_target_pairs={{0,13},{1,12},{2,15},{3,14},{4,9},{5,8},{6,11},{7,10},{8,5},{9,4},... | collective-permute-start | bytes 196616 | tf_op jit(solution)/shard_map/ppermute | solution.py:34
  141.4 7.4 %collective-permute-start.13 = (bf16[256,128]{1,0:T(8,128)(2,1)S(1)}, bf16[256,128]{1,0:T(8,128)(2,1)S(1)}, u32[]{:S(2)}, u32[]{:S(2)}) collective-permute-start(bf16[256,128]{1,0:T(8,128)(2,1)S(1)} %get-tuple-element.30), channel_id=1, source_target_pairs={{0,14},{1,15},{2,12},{3,13},{4,10},{5,11},{6,8},{7,9},{8,6},{9,7},... | collective-permute-start | bytes 196616 | tf_op jit(solution)/shard_map/ppermute | solution.py:34
  144.6 6.8 %collective-permute-start.14 = (bf16[256,128]{1,0:T(8,128)(2,1)S(1)}, bf16[256,128]{1,0:T(8,128)(2,1)S(1)}, u32[]{:S(2)}, u32[]{:S(2)}) collective-permute-start(bf16[256,128]{1,0:T(8,128)(2,1)S(1)} %get-tuple-element.29), channel_id=1, source_target_pairs={{0,15},{1,14},{2,13},{3,12},{4,11},{5,10},{6,9},{7,8},{8,7},{9,6},... | collective-permute-start | bytes 196616 | tf_op jit(solution)/shard_map/ppermute | solution.py:34
  146.3 7.1 %collective-permute-start.17 = (bf16[256,128]{1,0:T(8,128)(2,1)S(1)}, bf16[256,128]{1,0:T(8,128)(2,1)S(1)}, u32[]{:S(2)}, u32[]{:S(2)}) collective-permute-start(bf16[256,128]{1,0:T(8,128)(2,1)S(1)} %get-tuple-element.28), channel_id=1, source_target_pairs={{0,4},{1,5},{2,6},{3,7},{4,0},{5,1},{6,2},{7,3},{8,12},{9,13},{10,... | collective-permute-start | bytes 196616 | tf_op jit(solution)/shard_map/ppermute | solution.py:34
  148.8 5.5 %collective-permute-start.18 = (bf16[256,128]{1,0:T(8,128)(2,1)S(1)}, bf16[256,128]{1,0:T(8,128)(2,1)S(1)}, u32[]{:S(2)}, u32[]{:S(2)}) collective-permute-start(bf16[256,128]{1,0:T(8,128)(2,1)S(1)} %get-tuple-element.27), channel_id=1, source_target_pairs={{0,5},{1,4},{2,7},{3,6},{4,1},{5,0},{6,3},{7,2},{8,13},{9,12},{10,... | collective-permute-start | bytes 196616 | tf_op jit(solution)/shard_map/ppermute | solution.py:34
  151.4 5.5 %collective-permute-start.19 = (bf16[256,128]{1,0:T(8,128)(2,1)S(1)}, bf16[256,128]{1,0:T(8,128)(2,1)S(1)}, u32[]{:S(2)}, u32[]{:S(2)}) collective-permute-start(bf16[256,128]{1,0:T(8,128)(2,1)S(1)} %get-tuple-element.26), channel_id=1, source_target_pairs={{0,6},{1,7},{2,4},{3,5},{4,2},{5,3},{6,0},{7,1},{8,14},{9,15},{10,... | collective-permute-start | bytes 196616 | tf_op jit(solution)/shard_map/ppermute | solution.py:34
  153.5 11.6 %collective-permute-start.20 = (bf16[256,128]{1,0:T(8,128)(2,1)S(1)}, bf16[256,128]{1,0:T(8,128)(2,1)S(1)}, u32[]{:S(2)}, u32[]{:S(2)}) collective-permute-start(bf16[256,128]{1,0:T(8,128)(2,1)S(1)} %get-tuple-element.25), channel_id=1, source_target_pairs={{0,7},{1,6},{2,5},{3,4},{4,3},{5,2},{6,1},{7,0},{8,15},{9,14},{10,... | collective-permute-start | bytes 196616 | tf_op jit(solution)/shard_map/ppermute | solution.py:34
  154.3 12.6 %collective-permute-start.23 = (bf16[256,128]{1,0:T(8,128)(2,1)S(1)}, bf16[256,128]{1,0:T(8,128)(2,1)S(1)}, u32[]{:S(2)}, u32[]{:S(2)}) collective-permute-start(bf16[256,128]{1,0:T(8,128)(2,1)S(1)} %get-tuple-element.24), channel_id=1, source_target_pairs={{0,8},{1,9},{2,10},{3,11},{4,12},{5,13},{6,14},{7,15},{8,0},{9,1},... | collective-permute-start | bytes 196616 | tf_op jit(solution)/shard_map/ppermute | solution.py:34
  156.8 10.1 %collective-permute-start.24 = (bf16[256,128]{1,0:T(8,128)(2,1)S(1)}, bf16[256,128]{1,0:T(8,128)(2,1)S(1)}, u32[]{:S(2)}, u32[]{:S(2)}) collective-permute-start(bf16[256,128]{1,0:T(8,128)(2,1)S(1)} %get-tuple-element.23), channel_id=1, source_target_pairs={{0,9},{1,8},{2,11},{3,10},{4,13},{5,12},{6,15},{7,14},{8,1},{9,0},... | collective-permute-start | bytes 196616 | tf_op jit(solution)/shard_map/ppermute | solution.py:34
  157.4 10.5 %collective-permute-start.25 = (bf16[256,128]{1,0:T(8,128)(2,1)S(1)}, bf16[256,128]{1,0:T(8,128)(2,1)S(1)}, u32[]{:S(2)}, u32[]{:S(2)}) collective-permute-start(bf16[256,128]{1,0:T(8,128)(2,1)S(1)} %get-tuple-element.22), channel_id=1, source_target_pairs={{0,10},{1,11},{2,8},{3,9},{4,14},{5,15},{6,12},{7,13},{8,2},{9,3},... | collective-permute-start | bytes 196616 | tf_op jit(solution)/shard_map/ppermute | solution.py:34
  159.3 10.1 %collective-permute-start.26 = (bf16[256,128]{1,0:T(8,128)(2,1)S(1)}, bf16[256,128]{1,0:T(8,128)(2,1)S(1)}, u32[]{:S(2)}, u32[]{:S(2)}) collective-permute-start(bf16[256,128]{1,0:T(8,128)(2,1)S(1)} %get-tuple-element.21), channel_id=1, source_target_pairs={{0,11},{1,10},{2,9},{3,8},{4,15},{5,14},{6,13},{7,12},{8,3},{9,2},... | collective-permute-start | bytes 196616 | tf_op jit(solution)/shard_map/ppermute | solution.py:34

commit v3 on v2

--- a/solution.py
+++ b/solution.py
@@ -196,11 +196,16 @@
     )(*weights)
 
 
-def product(left_refs, rights_ref, mask, columns):
-    origin = lax.axis_index("seq") ^ mask
-    depth = len(left_refs) * left_refs[0].shape[1]
+def product(left_refs, rights_ref, masks, columns):
+    me, head = lax.axis_index("seq"), lax.axis_index("head")
+    count, width = len(left_refs), left_refs[0].shape[1]
+    rights = []
+    for hop in range(count):
+        origin = me ^ jnp.where((head + hop) % 2 == 0, masks[0], masks[1])
+        first = pl.multiple_of((origin * count + hop) * width, width)
+        rights.append(rights_ref[pl.ds(first, width), columns])
     left = jnp.concatenate([ref[...] for ref in left_refs], axis=1)
-    right = rights_ref[pl.ds(pl.multiple_of(origin * depth, depth), depth), columns]
+    right = jnp.concatenate(rights, axis=0)
     return jnp.dot(left, right, preferred_element_type=jnp.float32)
 
 
@@ -270,7 +275,9 @@
 
 def served_by(seq):
     far = list(range(seq - 1, 1, -1))
-    return far[:1] + [1] + far[1:]
+    even = far[:1] + [1] + far[1:]
+    odd = even[:1] + even[1:3][::-1] + even[3:]
+    return [(0, 0)] + list(zip(even, odd))
 
 
 def far_first(heads):
@@ -295,13 +302,13 @@
     for masks in rounds:
         (outgoing,) = cut(arrays, [((0, 1), masks)], width)
         pairs.append(sent(outgoing, masks, 0))
-    kept = [((0, 1), (0, 0)), ((2,), (0, 0))] + [((2,), (m, m)) for m in order]
-    own_pair, own_queries, *queries_for = cut(arrays, kept, width)
+    kept = [((0, 1), (0, 0))] + [((2,), masks) for masks in order]
+    own_pair, *queries_for = cut(arrays, kept, width)
     pairs = [own_pair] + pairs
-    patterns, asked = {0: pattern}, {0: own_queries}
-    for at, mask in enumerate(order):
-        patterns[mask] = swapped(pattern, "seq", mask)
-        asked[mask] = swapped(queries_for[at], "seq", mask)
+    patterns, asked = [pattern], [queries_for[0]]
+    for at, masks in enumerate(order[1:], 1):
+        patterns.append(sent(pattern, masks, 0))
+        asked.append(sent(queries_for[at], masks, 0))
     weights = {0: out_weight}
     for hop in far_first(heads):
         for other in list(weights):
@@ -316,27 +323,25 @@
             slot = jnp.where(apart == jnp.where(even, a, b), r + 1, slot)
         return slot * qblocks + ids % qblocks
 
-    def split(block, mask):
+    def split(block, at):
         got = []
         for hop in range(heads):
             mine = lax.dynamic_slice_in_dim(block, (head ^ hop) * share, share, axis=0)
-            if mask or hop:
-                mine = sent(mine, (mask, mask), hop)
+            if at or hop:
+                mine = sent(mine, order[at], hop)
             got.append(mine)
         return got
 
-    ready, before = {}, None
-    for mask in [0] + order:
-        slots = slots_of(patterns[mask])
+    ready, before = [], None
+    for at in range(len(order)):
+        slots = slots_of(patterns[at])
         if before is not None:
             slots, before = chained(slots, before)
-        mixed = before = attend(asked[mask], pooled, slots)
-        ready[mask] = split(mixed, mask)
-    tail = order[-1]
-    early = [mask for mask in [0] + order if mask != tail]
+        mixed = before = attend(asked[at], pooled, slots)
+        ready.append(split(mixed, at))
     rights = sheaf([weights[hop] for hop in range(heads)], width)
-    part = project([ready[mask] for mask in early], early, rights)
-    return finish(ready[tail], tail, rights, part, queries.dtype)
+    part = project(ready[:-1], order[:-1], rights)
+    return finish(ready[-1], order[-1], rights, part, queries.dtype)
 
 
 def by_rows(queries, keys, values, pattern, out_weight):

time: 171 us -> 169 us (0.988)
  starting transfers between devices: 48.5 us -> 46.2 us
    ppermute x9 -> x3, starting transfers between devices: 23.4 us -> 2.97 us  [swapped(): return lax.ppermute(value, axis, [(i, i ^ mask) for i in range(count)])]
    ppermute x18 -> x24, starting transfers between devices: 25.1 us -> 43.2 us  [sent(): return lax.ppermute(value, ('seq', 'head'), moves)]
    ppermute x9 -> x3, waiting for transfers between devices: 57.1 us -> 45.8 us  [swapped(): return lax.ppermute(value, axis, [(i, i ^ mask) for i in range(count)])]
    ppermute x18 -> x24, waiting for transfers between devices: 33.8 us -> 44.9 us  [sent(): return lax.ppermute(value, ('seq', 'head'), moves)]
  transfers between devices with their start and end apart: 27 -> 27, of which waited for: 10 -> 7; matrix products, arithmetic and copies ran while one was open for 0% -> 0% of each run, Pallas kernels for 16% -> 16%
where the time goes in v3:
time: 169 us; the launch traced here: 168 us
  waiting for transfers between devices  90.7 us (54%)
  starting transfers between devices  46.2 us (27%)
  Pallas kernels  28.1 us (17%)
  local copies, waits for them, and re-layouts  2.99 us (2%)
    ppermute x3, waiting for transfers between devices, swapped(): return lax.ppermute(value, axis, [(i, i ^ mask) for i in range(count)])  45.8 us
    ppermute x24, waiting for transfers between devices, sent(): return lax.ppermute(value, ('seq', 'head'), moves)  44.9 us
    ppermute x24, starting transfers between devices, sent(): return lax.ppermute(value, ('seq', 'head'), moves)  43.2 us
    pallas_call x4, Pallas kernels, attend(): pl.pallas_call(attend_body, out_shape=jax.ShapeDtypeStruct(queries.shape,...  15.1 us
    pallas_call x4, Pallas kernels, cut(): pl.pallas_call(functools.partial(cut_body, plan, width), out_shape=[pltpu...  5.88 us
  transfers between devices with their start and end apart: 27, of which 7 were waited for; matrix products, arithmetic and copies ran while one was open for 0% of the time, Pallas kernels for 16%

profile of v3, /device:TPU:0, one launch (start us, length us, event | category | flops | bytes accessed | tf_op | source)
XLA Modules:
  0.0 168.4 jit_solution(9482041838708624283)
XLA Ops:
  0.0 3.0 %collective-permute-start.1 = (bf16[512,2048]{1,0:T(8,128)(2,1)}, bf16[512,2048]{1,0:T(8,128)(2,1)S(1)}, u32[]{:S(2)}, u32[]{:S(2)}) collective-permute-start(bf16[512,2048]{1,0:T(8,128)(2,1)} %refs_0_.5), channel_id=1, source_target_pairs={{0,2},{1,3},{2,0},{3,1},{4,6},{5,7},{6,4},{7,5},{8,10},{9,11},{10,... | collective-permute-start | bytes 6291464 | tf_op jit(solution)/shard_map/ppermute | solution.py:24
  3.0 0.0 collective-permute-start
  3.0 45.8 %collective-permute-done.1.refs_2_ = bf16[512,2048]{1,0:T(8,128)(2,1)S(1)} collective-permute-done((bf16[512,2048]{1,0:T(8,128)(2,1)}, bf16[512,2048]{1,0:T(8,128)(2,1)S(1)}, u32[]{:S(2)}, u32[]{:S(2)}) %collective-permute-start.1) | collective-permute-done | bytes 2097184 | tf_op jit(solution)/shard_map/ppermute | solution.py:24
  48.8 0.0 collective-permute-start.2
  48.8 1.1 cut.5
  50.0 1.9 %collective-permute-start.3 = (bf16[2,1024,128]{2,1,0:T(8,128)(2,1)S(1)}, bf16[2,1024,128]{2,1,0:T(8,128)(2,1)}, u32[]{:S(2)}, u32[]{:S(2)}) collective-permute-start(bf16[2,1024,128]{2,1,0:T(8,128)(2,1)S(1)} %cut.5), channel_id=1, source_target_pairs={{0,4},{1,9},{2,6},{3,11},{4,0},{5,13},{6,2},{7,15},{8,12},{9,1},{1... | collective-permute-start | bytes 1572872 | tf_op jit(solution)/shard_map/ppermute | solution.py:34
  51.9 2.5 %collective-permute-start.9 = (s32[8,15]{1,0:T(8,128)S(1)}, s32[8,15]{1,0:T(8,128)S(1)}, u32[]{:S(2)}, u32[]{:S(2)}) collective-permute-start(s32[8,15]{1,0:T(8,128)S(1)} %copy-done.5), channel_id=1, source_target_pairs={{0,12},{1,13},{2,14},{3,15},{4,8},{5,9},{6,10},{7,11},{8,4},{9,5},... | collective-permute-start | bytes 1448 | tf_op jit(solution)/shard_map/ppermute | solution.py:34
  54.3 0.7 collective-permute-start.15
  55.0 1.1 cut.6
  56.2 10.5 %collective-permute-done.9 = s32[8,15]{1,0:T(8,128)S(1)} collective-permute-done((s32[8,15]{1,0:T(8,128)S(1)}, s32[8,15]{1,0:T(8,128)S(1)}, u32[]{:S(2)}, u32[]{:S(2)}) %collective-permute-start.9) | collective-permute-done | bytes 512 | tf_op jit(solution)/shard_map/ppermute | solution.py:34
  66.7 0.0 collective-permute-start.4
  66.7 1.9 %cut.7 = bf16[2,1024,128]{2,1,0:T(8,128)(2,1)} custom-call(bf16[1024,512]{1,0:T(8,128)(2,1)} %refs_0_.9, bf16[1024,512]{1,0:T(8,128)(2,1)} %refs_1_.7, bf16[1024,512]{1,0:T(8,128)(2,1)} %refs_2_.7), custom_call_target="tpu_custom_call" | custom-call | tf_op jit(solution)/shard_map/cut/pallas_call | solution.py:80
  68.6 0.0 collective-permute-done.15
  68.6 1.6 collective-permute-start.5
  70.2 1.6 cut.4
  71.8 0.0 copy-start.1
  71.9 0.8 copy-done.1
  72.6 0.7 copy-done.2
  73.3 0.7 copy-done.3
  74.1 0.7 copy-done.4
  74.8 2.4 %collective-permute-start.10 = (bf16[1024,128]{1,0:T(8,128)(2,1)}, bf16[1024,128]{1,0:T(8,128)(2,1)S(1)}, u32[]{:S(2)}, u32[]{:S(2)}) collective-permute-start(bf16[1024,128]{1,0:T(8,128)(2,1)} %copy-done.4), channel_id=1, source_target_pairs={{0,12},{1,13},{2,14},{3,15},{4,8},{5,9},{6,10},{7,11},{8,4},{9,5},... | collective-permute-start | bytes 786440 | tf_op jit(solution)/shard_map/ppermute | solution.py:34
  77.2 29.2 %collective-permute-done.4.refs_2_ = bf16[2,1024,128]{2,1,0:T(8,128)(2,1)} collective-permute-done((bf16[2,1024,128]{2,1,0:T(8,128)(2,1)S(1)}, bf16[2,1024,128]{2,1,0:T(8,128)(2,1)}, u32[]{:S(2)}, u32[]{:S(2)}) %collective-permute-start.4) | collective-permute-done | bytes 524320 | tf_op jit(solution)/shard_map/ppermute | solution.py:34
  106.4 12.0 %collective-permute-start.22 = (bf16[1024,128]{1,0:T(8,128)(2,1)}, bf16[1024,128]{1,0:T(8,128)(2,1)S(1)}, u32[]{:S(2)}, u32[]{:S(2)}) collective-permute-start(bf16[1024,128]{1,0:T(8,128)(2,1)} %copy-done.2), channel_id=1, source_target_pairs={{0,8},{1,5},{2,10},{3,7},{4,12},{5,1},{6,14},{7,3},{8,0},{9,13},{1... | collective-permute-start | bytes 786440 | tf_op jit(solution)/shard_map/ppermute | solution.py:34
  118.4 1.6 pool.1.kv
  119.9 3.7 %attend.4 = bf16[1024,128]{1,0:T(8,128)(2,1)S(1)} custom-call(s32[8,15]{1,0:T(8,128)S(1)} %fusion.1.slots, bf16[1024,128]{1,0:T(8,128)(2,1)S(1)} %get-tuple-element.13.q_ref, bf16[2,4096,128]{2,1,0:T(8,128)(2,1)S(1)} %pool.1.kv), custom_call_target="tpu_custom_call" | custom-call | tf_op jit(solution)/shard_map/attend/pallas_call | solution.py:154
  123.7 0.1 collective-permute-start.21
  123.8 3.7 %attend.5 = bf16[1024,128]{1,0:T(8,128)(2,1)S(1)} custom-call(s32[8,15]{1,0:T(8,128)S(1)} %fusion.3.slots, bf16[1024,128]{1,0:T(8,128)(2,1)S(1)} %collective-permute-done.10.q_ref, bf16[2,4096,128]{2,1,0:T(8,128)(2,1)S(1)} %pool.1.kv), custom_call_target="tpu_custom_call" | custom-call | tf_op jit(solution)/shard_map/attend/pallas_call | solution.py:154
  127.5 0.7 collective-permute-done.21
  128.2 0.0 collective-permute-start.6
  128.3 1.6 collective-permute-start.7
  129.8 0.4 collective-permute-start.8
  130.2 0.0 collective-permute-done.6.refs_1_
  130.2 2.2 %collective-permute-start.11 = (bf16[256,128]{1,0:T(8,128)(2,1)S(1)}, bf16[256,128]{1,0:T(8,128)(2,1)S(1)}, u32[]{:S(2)}, u32[]{:S(2)}) collective-permute-start(bf16[256,128]{1,0:T(8,128)(2,1)S(1)} %get-tuple-element.32), channel_id=1, source_target_pairs={{0,12},{1,13},{2,14},{3,15},{4,8},{5,9},{6,10},{7,11},{8,4},{9,5},... | collective-permute-start | bytes 196616 | tf_op jit(solution)/shard_map/ppermute | solution.py:34
  132.4 3.7 %attend.6 = bf16[1024,128]{1,0:T(8,128)(2,1)S(1)} custom-call(s32[8,15]{1,0:T(8,128)S(1)} %fusion.5.slots, bf16[1024,128]{1,0:T(8,128)(2,1)S(1)} %collective-permute-done.16.q_ref, bf16[2,4096,128]{2,1,0:T(8,128)(2,1)S(1)} %pool.1.kv), custom_call_target="tpu_custom_call" | custom-call | tf_op jit(solution)/shard_map/attend/pallas_call | solution.py:154
  136.1 0.0 copy-start
  136.1 3.9 %attend.7 = bf16[1024,128]{1,0:T(8,128)(2,1)S(1)} custom-call(s32[8,15]{1,0:T(8,128)S(1)} %fusion.7.slots, bf16[1024,128]{1,0:T(8,128)(2,1)S(1)} %collective-permute-done.22.q_ref, bf16[2,4096,128]{2,1,0:T(8,128)(2,1)S(1)} %pool.1.kv), custom_call_target="tpu_custom_call" | custom-call | tf_op jit(solution)/shard_map/attend/pallas_call | solution.py:154
  140.1 0.0 collective-permute-done.7.refs_2_
  140.1 1.3 collective-permute-start.12
  141.4 0.0 collective-permute-done.8.refs_3_
  141.4 3.1 %collective-permute-start.13 = (bf16[256,128]{1,0:T(8,128)(2,1)S(1)}, bf16[256,128]{1,0:T(8,128)(2,1)S(1)}, u32[]{:S(2)}, u32[]{:S(2)}) collective-permute-start(bf16[256,128]{1,0:T(8,128)(2,1)S(1)} %get-tuple-element.30), channel_id=1, source_target_pairs={{0,14},{1,15},{2,12},{3,13},{4,10},{5,11},{6,8},{7,9},{8,6},{9,7},... | collective-permute-start | bytes 196616 | tf_op jit(solution)/shard_map/ppermute | solution.py:34
  144.5 0.0 collective-permute-done.11.refs_4_
  144.5 1.4 collective-permute-start.14
  146.0 0.3 collective-permute-done.12.refs_5_
  146.2 0.0 collective-permute-start.17
  146.2 2.5 %collective-permute-done.13.refs_6_ = bf16[256,128]{1,0:T(8,128)(2,1)S(1)} collective-permute-done((bf16[256,128]{1,0:T(8,128)(2,1)S(1)}, bf16[256,128]{1,0:T(8,128)(2,1)S(1)}, u32[]{:S(2)}, u32[]{:S(2)}) %collective-permute-start.13) | collective-permute-done | bytes 65568 | tf_op jit(solution)/shard_map/ppermute | solution.py:34
  148.8 1.0 collective-permute-start.18
  149.8 1.6 collective-permute-done.14.refs_7_
  151.4 2.7 %collective-permute-start.19 = (bf16[256,128]{1,0:T(8,128)(2,1)S(1)}, bf16[256,128]{1,0:T(8,128)(2,1)S(1)}, u32[]{:S(2)}, u32[]{:S(2)}) collective-permute-start(bf16[256,128]{1,0:T(8,128)(2,1)S(1)} %get-tuple-element.26), channel_id=1, source_target_pairs={{0,6},{1,11},{2,4},{3,9},{4,2},{5,15},{6,0},{7,13},{8,14},{9,3},{1... | collective-permute-start | bytes 196616 | tf_op jit(solution)/shard_map/ppermute | solution.py:34
  154.1 0.0 collective-permute-done.17.refs_8_
  154.1 0.3 collective-permute-start.20
  154.4 0.0 collective-permute-done.18.refs_9_
  154.4 3.5 %collective-permute-start.23 = (bf16[256,128]{1,0:T(8,128)(2,1)S(1)}, bf16[256,128]{1,0:T(8,128)(2,1)S(1)}, u32[]{:S(2)}, u32[]{:S(2)}) collective-permute-start(bf16[256,128]{1,0:T(8,128)(2,1)S(1)} %get-tuple-element.24), channel_id=1, source_target_pairs={{0,8},{1,5},{2,10},{3,7},{4,12},{5,1},{6,14},{7,3},{8,0},{9,13},{1... | collective-permute-start | bytes 196616 | tf_op jit(solution)/shard_map/ppermute | solution.py:34
  157.8 0.0 collective-permute-done.19.refs_10_
  157.8 1.9 %collective-permute-start.24 = (bf16[256,128]{1,0:T(8,128)(2,1)S(1)}, bf16[256,128]{1,0:T(8,128)(2,1)S(1)}, u32[]{:S(2)}, u32[]{:S(2)}) collective-permute-start(bf16[256,128]{1,0:T(8,128)(2,1)S(1)} %get-tuple-element.23), channel_id=1, source_target_pairs={{0,9},{1,4},{2,11},{3,6},{4,13},{5,0},{6,15},{7,2},{8,1},{9,12},{1... | collective-permute-start | bytes 196616 | tf_op jit(solution)/shard_map/ppermute | solution.py:34
  159.8 1.5 collective-permute-start.25
  161.3 0.0 collective-permute-done.2.refs_3_
  161.3 1.3 collective-permute-start.26
  162.6 2.4 %sheaf.1.rights_ref = bf16[2048,2048]{1,0:T(8,128)(2,1)S(1)} custom-call(bf16[512,2048]{1,0:T(8,128)(2,1)S(1)} %copy-done, bf16[512,2048]{1,0:T(8,128)(2,1)} %collective-permute-done.refs_1_, bf16[512,2048]{1,0:T(8,128)(2,1)S(1)} %collective-permute-done.1.refs_2_, bf16[512,2048]{1,0:T(8,128)(2,1)} %collective-permute-done.2.refs_3_), custom_call_target="tpu_custom_call" | custom-call | tf_op jit(solution)/shard_map/sheaf/pallas_call | solution.py:188
  164.9 0.0 collective-permute-done.20.refs_11_
  165.0 1.8 %project.1.part_ref = f32[256,2048]{1,0:T(8,128)S(1)} custom-call(bf16[2048,2048]{1,0:T(8,128)(2,1)S(1)} %sheaf.1.rights_ref, bf16[256,128]{1,0:T(8,128)(2,1)S(1)} %get-tuple-element.36.refs_0_, bf16[256,128]{1,0:T(8,128)(2,1)S(1)} %collective-permute-done.6.refs_1_, bf16[256,128]{1,0:T(8,128)(2,1)S(1)} %collective-permute-done.7.refs_2_, ...), custom_call_target="tpu_custom_call" | custom-call | tf_op jit(solution)/shard_map/project/pallas_call | solution.py:228
  166.8 0.0 collective-permute-done.23.refs_0_
  166.8 0.0 collective-permute-done.24.refs_1_
  166.8 0.0 collective-permute-done.26.refs_3_
  166.8 1.5 finish.1
  (22 shorter events, 0.2 us)
Async XLA Ops:
  0.0 51.9 %copy-start.5 = (s32[8,15]{1,0:T(8,128)S(1)}, s32[8,15]{1,0:T(8,128)}, u32[]{:S(2)}) copy-start(s32[8,15]{1,0:T(8,128)} %param.8) | copy-start | bytes 1444
  0.0 48.8 %collective-permute-start.1 = (bf16[512,2048]{1,0:T(8,128)(2,1)}, bf16[512,2048]{1,0:T(8,128)(2,1)S(1)}, u32[]{:S(2)}, u32[]{:S(2)}) collective-permute-start(bf16[512,2048]{1,0:T(8,128)(2,1)} %refs_0_.5), channel_id=1, source_target_pairs={{0,2},{1,3},{2,0},{3,1},{4,6},{5,7},{6,4},{7,5},{8,10},{9,11},{10,... | collective-permute-start | bytes 6291464 | tf_op jit(solution)/shard_map/ppermute | solution.py:24
  3.0 156.8 %collective-permute-start = (bf16[512,2048]{1,0:T(8,128)(2,1)}, bf16[512,2048]{1,0:T(8,128)(2,1)}, u32[]{:S(2)}, u32[]{:S(2)}) collective-permute-start(bf16[512,2048]{1,0:T(8,128)(2,1)} %refs_0_.5), channel_id=1, source_target_pairs={{0,1},{1,0},{2,3},{3,2},{4,5},{5,4},{6,7},{7,6},{8,9},{9,8},{10,11... | collective-permute-start | bytes 6291464 | tf_op jit(solution)/shard_map/ppermute | solution.py:24
  48.8 112.5 %collective-permute-start.2 = (bf16[512,2048]{1,0:T(8,128)(2,1)S(1)}, bf16[512,2048]{1,0:T(8,128)(2,1)}, u32[]{:S(2)}, u32[]{:S(2)}) collective-permute-start(bf16[512,2048]{1,0:T(8,128)(2,1)S(1)} %collective-permute-done.1.refs_2_), channel_id=1, source_target_pairs={{0,1},{1,0},{2,3},{3,2},{4,5},{5,4},{6,7},{7,6},{8,9},{9,8},{10,11... | collective-permute-start | bytes 6291464 | tf_op jit(solution)/shard_map/ppermute | solution.py:24
  50.0 24.8 %collective-permute-start.3 = (bf16[2,1024,128]{2,1,0:T(8,128)(2,1)S(1)}, bf16[2,1024,128]{2,1,0:T(8,128)(2,1)}, u32[]{:S(2)}, u32[]{:S(2)}) collective-permute-start(bf16[2,1024,128]{2,1,0:T(8,128)(2,1)S(1)} %cut.5), channel_id=1, source_target_pairs={{0,4},{1,9},{2,6},{3,11},{4,0},{5,13},{6,2},{7,15},{8,12},{9,1},{1... | collective-permute-start | bytes 1572872 | tf_op jit(solution)/shard_map/ppermute | solution.py:34
  51.9 14.8 %collective-permute-start.9 = (s32[8,15]{1,0:T(8,128)S(1)}, s32[8,15]{1,0:T(8,128)S(1)}, u32[]{:S(2)}, u32[]{:S(2)}) collective-permute-start(s32[8,15]{1,0:T(8,128)S(1)} %copy-done.5), channel_id=1, source_target_pairs={{0,12},{1,13},{2,14},{3,15},{4,8},{5,9},{6,10},{7,11},{8,4},{9,5},... | collective-permute-start | bytes 1448 | tf_op jit(solution)/shard_map/ppermute | solution.py:34
  54.3 14.3 %collective-permute-start.15 = (s32[8,15]{1,0:T(8,128)S(1)}, s32[8,15]{1,0:T(8,128)S(1)}, u32[]{:S(2)}, u32[]{:S(2)}) collective-permute-start(s32[8,15]{1,0:T(8,128)S(1)} %copy-done.5), channel_id=1, source_target_pairs={{0,4},{1,9},{2,6},{3,11},{4,0},{5,13},{6,2},{7,15},{8,12},{9,1},{1... | collective-permute-start | bytes 1448 | tf_op jit(solution)/shard_map/ppermute | solution.py:34
  66.7 39.7 %collective-permute-start.4 = (bf16[2,1024,128]{2,1,0:T(8,128)(2,1)S(1)}, bf16[2,1024,128]{2,1,0:T(8,128)(2,1)}, u32[]{:S(2)}, u32[]{:S(2)}) collective-permute-start(bf16[2,1024,128]{2,1,0:T(8,128)(2,1)S(1)} %cut.6), channel_id=1, source_target_pairs={{0,8},{1,5},{2,10},{3,7},{4,12},{5,1},{6,14},{7,3},{8,0},{9,13},{1... | collective-permute-start | bytes 1572872 | tf_op jit(solution)/shard_map/ppermute | solution.py:34
  68.6 37.8 %collective-permute-start.5 = (bf16[2,1024,128]{2,1,0:T(8,128)(2,1)}, bf16[2,1024,128]{2,1,0:T(8,128)(2,1)}, u32[]{:S(2)}, u32[]{:S(2)}) collective-permute-start(bf16[2,1024,128]{2,1,0:T(8,128)(2,1)} %cut.7), channel_id=1, source_target_pairs={{0,12},{1,13},{2,14},{3,15},{4,8},{5,9},{6,10},{7,11},{8,4},{9,5},... | collective-permute-start | bytes 1572872 | tf_op jit(solution)/shard_map/ppermute | solution.py:34
  71.8 0.8 copy-start.1
  72.6 0.7 copy-start.2
  73.3 0.7 copy-start.3
  74.1 0.7 copy-start.4
  74.8 48.9 %collective-permute-start.10 = (bf16[1024,128]{1,0:T(8,128)(2,1)}, bf16[1024,128]{1,0:T(8,128)(2,1)S(1)}, u32[]{:S(2)}, u32[]{:S(2)}) collective-permute-start(bf16[1024,128]{1,0:T(8,128)(2,1)} %copy-done.4), channel_id=1, source_target_pairs={{0,12},{1,13},{2,14},{3,15},{4,8},{5,9},{6,10},{7,11},{8,4},{9,5},... | collective-permute-start | bytes 786440 | tf_op jit(solution)/shard_map/ppermute | solution.py:34
  106.4 21.9 %collective-permute-start.16 = (bf16[1024,128]{1,0:T(8,128)(2,1)}, bf16[1024,128]{1,0:T(8,128)(2,1)S(1)}, u32[]{:S(2)}, u32[]{:S(2)}) collective-permute-start(bf16[1024,128]{1,0:T(8,128)(2,1)} %copy-done.3), channel_id=1, source_target_pairs={{0,4},{1,9},{2,6},{3,11},{4,0},{5,13},{6,2},{7,15},{8,12},{9,1},{1... | collective-permute-start | bytes 786440 | tf_op jit(solution)/shard_map/ppermute | solution.py:34
  106.4 23.4 %collective-permute-start.22 = (bf16[1024,128]{1,0:T(8,128)(2,1)}, bf16[1024,128]{1,0:T(8,128)(2,1)S(1)}, u32[]{:S(2)}, u32[]{:S(2)}) collective-permute-start(bf16[1024,128]{1,0:T(8,128)(2,1)} %copy-done.2), channel_id=1, source_target_pairs={{0,8},{1,5},{2,10},{3,7},{4,12},{5,1},{6,14},{7,3},{8,0},{9,13},{1... | collective-permute-start | bytes 786440 | tf_op jit(solution)/shard_map/ppermute | solution.py:34
  123.7 4.6 %collective-permute-start.21 = (s32[8,15]{1,0:T(8,128)S(1)}, s32[8,15]{1,0:T(8,128)S(1)}, u32[]{:S(2)}, u32[]{:S(2)}) collective-permute-start(s32[8,15]{1,0:T(8,128)S(1)} %copy-done.5), channel_id=1, source_target_pairs={{0,8},{1,5},{2,10},{3,7},{4,12},{5,1},{6,14},{7,3},{8,0},{9,13},{1... | collective-permute-start | bytes 1448 | tf_op jit(solution)/shard_map/ppermute | solution.py:34
  128.2 2.0 %collective-permute-start.6 = (bf16[256,128]{1,0:T(8,128)(2,1)S(1)}, bf16[256,128]{1,0:T(8,128)(2,1)S(1)}, u32[]{:S(2)}, u32[]{:S(2)}) collective-permute-start(bf16[256,128]{1,0:T(8,128)(2,1)S(1)} %get-tuple-element.35), channel_id=1, source_target_pairs={{0,1},{1,0},{2,3},{3,2},{4,5},{5,4},{6,7},{7,6},{8,9},{9,8},{10,11... | collective-permute-start | bytes 196616 | tf_op jit(solution)/shard_map/ppermute | solution.py:34
  128.3 11.8 %collective-permute-start.7 = (bf16[256,128]{1,0:T(8,128)(2,1)S(1)}, bf16[256,128]{1,0:T(8,128)(2,1)S(1)}, u32[]{:S(2)}, u32[]{:S(2)}) collective-permute-start(bf16[256,128]{1,0:T(8,128)(2,1)S(1)} %get-tuple-element.34), channel_id=1, source_target_pairs={{0,2},{1,3},{2,0},{3,1},{4,6},{5,7},{6,4},{7,5},{8,10},{9,11},{10,... | collective-permute-start | bytes 196616 | tf_op jit(solution)/shard_map/ppermute | solution.py:34
  129.8 11.6 %collective-permute-start.8 = (bf16[256,128]{1,0:T(8,128)(2,1)S(1)}, bf16[256,128]{1,0:T(8,128)(2,1)S(1)}, u32[]{:S(2)}, u32[]{:S(2)}) collective-permute-start(bf16[256,128]{1,0:T(8,128)(2,1)S(1)} %get-tuple-element.33), channel_id=1, source_target_pairs={{0,3},{1,2},{2,1},{3,0},{4,7},{5,6},{6,5},{7,4},{8,11},{9,10},{10,... | collective-permute-start | bytes 196616 | tf_op jit(solution)/shard_map/ppermute | solution.py:34
  130.2 14.3 %collective-permute-start.11 = (bf16[256,128]{1,0:T(8,128)(2,1)S(1)}, bf16[256,128]{1,0:T(8,128)(2,1)S(1)}, u32[]{:S(2)}, u32[]{:S(2)}) collective-permute-start(bf16[256,128]{1,0:T(8,128)(2,1)S(1)} %get-tuple-element.32), channel_id=1, source_target_pairs={{0,12},{1,13},{2,14},{3,15},{4,8},{5,9},{6,10},{7,11},{8,4},{9,5},... | collective-permute-start | bytes 196616 | tf_op jit(solution)/shard_map/ppermute | solution.py:34
  136.1 26.4 %copy-start = (bf16[512,2048]{1,0:T(8,128)(2,1)S(1)}, bf16[512,2048]{1,0:T(8,128)(2,1)}, u32[]{:S(2)}) copy-start(bf16[512,2048]{1,0:T(8,128)(2,1)} %refs_0_.5) | copy-start | bytes 6291460
  140.1 6.2 %collective-permute-start.12 = (bf16[256,128]{1,0:T(8,128)(2,1)S(1)}, bf16[256,128]{1,0:T(8,128)(2,1)S(1)}, u32[]{:S(2)}, u32[]{:S(2)}) collective-permute-start(bf16[256,128]{1,0:T(8,128)(2,1)S(1)} %get-tuple-element.31), channel_id=1, source_target_pairs={{0,13},{1,12},{2,15},{3,14},{4,9},{5,8},{6,11},{7,10},{8,5},{9,4},... | collective-permute-start | bytes 196616 | tf_op jit(solution)/shard_map/ppermute | solution.py:34
  141.4 7.4 %collective-permute-start.13 = (bf16[256,128]{1,0:T(8,128)(2,1)S(1)}, bf16[256,128]{1,0:T(8,128)(2,1)S(1)}, u32[]{:S(2)}, u32[]{:S(2)}) collective-permute-start(bf16[256,128]{1,0:T(8,128)(2,1)S(1)} %get-tuple-element.30), channel_id=1, source_target_pairs={{0,14},{1,15},{2,12},{3,13},{4,10},{5,11},{6,8},{7,9},{8,6},{9,7},... | collective-permute-start | bytes 196616 | tf_op jit(solution)/shard_map/ppermute | solution.py:34
  144.5 6.8 %collective-permute-start.14 = (bf16[256,128]{1,0:T(8,128)(2,1)S(1)}, bf16[256,128]{1,0:T(8,128)(2,1)S(1)}, u32[]{:S(2)}, u32[]{:S(2)}) collective-permute-start(bf16[256,128]{1,0:T(8,128)(2,1)S(1)} %get-tuple-element.29), channel_id=1, source_target_pairs={{0,15},{1,14},{2,13},{3,12},{4,11},{5,10},{6,9},{7,8},{8,7},{9,6},... | collective-permute-start | bytes 196616 | tf_op jit(solution)/shard_map/ppermute | solution.py:34
  146.2 7.9 %collective-permute-start.17 = (bf16[256,128]{1,0:T(8,128)(2,1)S(1)}, bf16[256,128]{1,0:T(8,128)(2,1)S(1)}, u32[]{:S(2)}, u32[]{:S(2)}) collective-permute-start(bf16[256,128]{1,0:T(8,128)(2,1)S(1)} %get-tuple-element.28), channel_id=1, source_target_pairs={{0,4},{1,9},{2,6},{3,11},{4,0},{5,13},{6,2},{7,15},{8,12},{9,1},{1... | collective-permute-start | bytes 196616 | tf_op jit(solution)/shard_map/ppermute | solution.py:34
  148.8 5.6 %collective-permute-start.18 = (bf16[256,128]{1,0:T(8,128)(2,1)S(1)}, bf16[256,128]{1,0:T(8,128)(2,1)S(1)}, u32[]{:S(2)}, u32[]{:S(2)}) collective-permute-start(bf16[256,128]{1,0:T(8,128)(2,1)S(1)} %get-tuple-element.27), channel_id=1, source_target_pairs={{0,5},{1,8},{2,7},{3,10},{4,1},{5,12},{6,3},{7,14},{8,13},{9,0},{1... | collective-permute-start | bytes 196616 | tf_op jit(solution)/shard_map/ppermute | solution.py:34
  151.4 6.5 %collective-permute-start.19 = (bf16[256,128]{1,0:T(8,128)(2,1)S(1)}, bf16[256,128]{1,0:T(8,128)(2,1)S(1)}, u32[]{:S(2)}, u32[]{:S(2)}) collective-permute-start(bf16[256,128]{1,0:T(8,128)(2,1)S(1)} %get-tuple-element.26), channel_id=1, source_target_pairs={{0,6},{1,11},{2,4},{3,9},{4,2},{5,15},{6,0},{7,13},{8,14},{9,3},{1... | collective-permute-start | bytes 196616 | tf_op jit(solution)/shard_map/ppermute | solution.py:34
  154.1 10.8 %collective-permute-start.20 = (bf16[256,128]{1,0:T(8,128)(2,1)S(1)}, bf16[256,128]{1,0:T(8,128)(2,1)S(1)}, u32[]{:S(2)}, u32[]{:S(2)}) collective-permute-start(bf16[256,128]{1,0:T(8,128)(2,1)S(1)} %get-tuple-element.25), channel_id=1, source_target_pairs={{0,7},{1,10},{2,5},{3,8},{4,3},{5,14},{6,1},{7,12},{8,15},{9,2},{1... | collective-permute-start | bytes 196616 | tf_op jit(solution)/shard_map/ppermute | solution.py:34
  154.4 12.4 %collective-permute-start.23 = (bf16[256,128]{1,0:T(8,128)(2,1)S(1)}, bf16[256,128]{1,0:T(8,128)(2,1)S(1)}, u32[]{:S(2)}, u32[]{:S(2)}) collective-permute-start(bf16[256,128]{1,0:T(8,128)(2,1)S(1)} %get-tuple-element.24), channel_id=1, source_target_pairs={{0,8},{1,5},{2,10},{3,7},{4,12},{5,1},{6,14},{7,3},{8,0},{9,13},{1... | collective-permute-start | bytes 196616 | tf_op jit(solution)/shard_map/ppermute | solution.py:34
  157.8 8.9 %collective-permute-start.24 = (bf16[256,128]{1,0:T(8,128)(2,1)S(1)}, bf16[256,128]{1,0:T(8,128)(2,1)S(1)}, u32[]{:S(2)}, u32[]{:S(2)}) collective-permute-start(bf16[256,128]{1,0:T(8,128)(2,1)S(1)} %get-tuple-element.23), channel_id=1, source_target_pairs={{0,9},{1,4},{2,11},{3,6},{4,13},{5,0},{6,15},{7,2},{8,1},{9,12},{1... | collective-permute-start | bytes 196616 | tf_op jit(solution)/shard_map/ppermute | solution.py:34
  159.8 7.0 %collective-permute-start.25 = (bf16[256,128]{1,0:T(8,128)(2,1)S(1)}, bf16[256,128]{1,0:T(8,128)(2,1)S(1)}, u32[]{:S(2)}, u32[]{:S(2)}) collective-permute-start(bf16[256,128]{1,0:T(8,128)(2,1)S(1)} %get-tuple-element.22), channel_id=1, source_target_pairs={{0,10},{1,7},{2,8},{3,5},{4,14},{5,3},{6,12},{7,1},{8,2},{9,15},{1... | collective-permute-start | bytes 196616 | tf_op jit(solution)/shard_map/ppermute | solution.py:34
  161.3 5.5 %collective-permute-start.26 = (bf16[256,128]{1,0:T(8,128)(2,1)S(1)}, bf16[256,128]{1,0:T(8,128)(2,1)S(1)}, u32[]{:S(2)}, u32[]{:S(2)}) collective-permute-start(bf16[256,128]{1,0:T(8,128)(2,1)S(1)} %get-tuple-element.21), channel_id=1, source_target_pairs={{0,11},{1,6},{2,9},{3,4},{4,15},{5,2},{6,13},{7,0},{8,3},{9,14},{1... | collective-permute-start | bytes 196616 | tf_op jit(solution)/shard_map/ppermute | solution.py:34

commit v4 on v3

--- a/solution.py
+++ b/solution.py
@@ -276,7 +276,7 @@
 def served_by(seq):
     far = list(range(seq - 1, 1, -1))
     even = far[:1] + [1] + far[1:]
-    odd = even[:1] + even[1:3][::-1] + even[3:]
+    odd = even[2:3] + even[:2] + even[3:]
     return [(0, 0)] + list(zip(even, odd))
 
 
@@ -298,10 +298,12 @@
     even = head % 2 == 0
     arrays = tuple(in_hbm(array) for array in (keys, values, queries))
 
-    pairs = []
-    for masks in rounds:
-        (outgoing,) = cut(arrays, [((0, 1), masks)], width)
-        pairs.append(sent(outgoing, masks, 0))
+    first = cut(arrays, [((0, 1), rounds[0])], width)
+    more = cut(arrays, [((0, 1), masks) for masks in rounds[1:]], width)
+    pairs = [
+        sent(outgoing, masks, 0)
+        for outgoing, masks in zip([*first, *more], rounds)
+    ]
     kept = [((0, 1), (0, 0))] + [((2,), masks) for masks in order]
     own_pair, *queries_for = cut(arrays, kept, width)
     pairs = [own_pair] + pairs

time: 169 us -> 170 us (level)
  waiting for transfers between devices: 90.7 us -> 97.2 us
  starting transfers between devices: 46.2 us -> 40.9 us
    ppermute x24, waiting for transfers between devices: 44.9 us -> 51.4 us  [sent(): return lax.ppermute(value, ('seq', 'head'), moves)]
    ppermute x24, starting transfers between devices: 43.2 us -> 38 us  [sent(): return lax.ppermute(value, ('seq', 'head'), moves)]
    pallas_call x4 -> x3, Pallas kernels: 5.88 us -> 5.01 us  [cut(): pl.pallas_call(functools.partial(cut_body, plan, width), out_shape=[pltpu...]
  transfers between devices with their start and end apart: 27 -> 27, of which waited for: 7 -> 8; matrix products, arithmetic and copies ran while one was open for 0% -> 0% of each run, Pallas kernels for 16% -> 15%
where the time goes in v4:
time: 170 us; the launch traced here: 169 us
  waiting for transfers between devices  97.2 us (57%)
  starting transfers between devices  40.9 us (24%)
  Pallas kernels  27.3 us (16%)
  local copies, waits for them, and re-layouts  2.99 us (2%)
    ppermute x24, waiting for transfers between devices, sent(): return lax.ppermute(value, ('seq', 'head'), moves)  51.4 us
    ppermute x3, waiting for transfers between devices, swapped(): return lax.ppermute(value, axis, [(i, i ^ mask) for i in range(count)])  45.8 us
    ppermute x24, starting transfers between devices, sent(): return lax.ppermute(value, ('seq', 'head'), moves)  38 us
    pallas_call x4, Pallas kernels, attend(): pl.pallas_call(attend_body, out_shape=jax.ShapeDtypeStruct(queries.shape,...  15.1 us
    pallas_call x3, Pallas kernels, cut(): pl.pallas_call(functools.partial(cut_body, plan, width), out_shape=[pltpu...  5.01 us
  transfers between devices with their start and end apart: 27, of which 8 were waited for; matrix products, arithmetic and copies ran while one was open for 0% of the time, Pallas kernels for 15%

profile of v4, /device:TPU:0, one launch (start us, length us, event | category | flops | bytes accessed | tf_op | source)
XLA Modules:
  0.0 168.9 jit_solution(2834824006361206056)
XLA Ops:
  0.0 3.0 %collective-permute-start.1 = (bf16[512,2048]{1,0:T(8,128)(2,1)}, bf16[512,2048]{1,0:T(8,128)(2,1)S(1)}, u32[]{:S(2)}, u32[]{:S(2)}) collective-permute-start(bf16[512,2048]{1,0:T(8,128)(2,1)} %refs_0_.4), channel_id=1, source_target_pairs={{0,2},{1,3},{2,0},{3,1},{4,6},{5,7},{6,4},{7,5},{8,10},{9,11},{10,... | collective-permute-start | bytes 6291464 | tf_op jit(solution)/shard_map/ppermute | solution.py:24
  3.0 0.0 collective-permute-start
  3.0 45.8 %collective-permute-done.1.refs_2_ = bf16[512,2048]{1,0:T(8,128)(2,1)S(1)} collective-permute-done((bf16[512,2048]{1,0:T(8,128)(2,1)}, bf16[512,2048]{1,0:T(8,128)(2,1)S(1)}, u32[]{:S(2)}, u32[]{:S(2)}) %collective-permute-start.1) | collective-permute-done | bytes 2097184 | tf_op jit(solution)/shard_map/ppermute | solution.py:24
  48.8 0.0 collective-permute-start.2
  48.8 1.1 cut.4
  50.0 1.9 %collective-permute-start.3 = (bf16[2,1024,128]{2,1,0:T(8,128)(2,1)S(1)}, bf16[2,1024,128]{2,1,0:T(8,128)(2,1)}, u32[]{:S(2)}, u32[]{:S(2)}) collective-permute-start(bf16[2,1024,128]{2,1,0:T(8,128)(2,1)S(1)} %cut.4), channel_id=1, source_target_pairs={{0,4},{1,9},{2,6},{3,11},{4,0},{5,13},{6,2},{7,15},{8,12},{9,1},{1... | collective-permute-start | bytes 1572872 | tf_op jit(solution)/shard_map/ppermute | solution.py:34
  51.9 2.5 %collective-permute-start.9 = (s32[8,15]{1,0:T(8,128)S(1)}, s32[8,15]{1,0:T(8,128)S(1)}, u32[]{:S(2)}, u32[]{:S(2)}) collective-permute-start(s32[8,15]{1,0:T(8,128)S(1)} %copy-done.5), channel_id=1, source_target_pairs={{0,12},{1,9},{2,14},{3,11},{4,8},{5,13},{6,10},{7,15},{8,4},{9,1},... | collective-permute-start | bytes 1448 | tf_op jit(solution)/shard_map/ppermute | solution.py:34
  54.3 0.7 collective-permute-start.15
  55.0 2.2 %cut.5 = (bf16[2,1024,128]{2,1,0:T(8,128)(2,1)}, bf16[2,1024,128]{2,1,0:T(8,128)(2,1)S(1)}) custom-call(bf16[1024,512]{1,0:T(8,128)(2,1)} %refs_0_.7, bf16[1024,512]{1,0:T(8,128)(2,1)} %refs_1_.5, bf16[1024,512]{1,0:T(8,128)(2,1)} %refs_2_.5), custom_call_target="tpu_custom_call" | custom-call | tf_op jit(solution)/shard_map/cut/pallas_call | solution.py:80
  57.2 9.4 %collective-permute-done.9 = s32[8,15]{1,0:T(8,128)S(1)} collective-permute-done((s32[8,15]{1,0:T(8,128)S(1)}, s32[8,15]{1,0:T(8,128)S(1)}, u32[]{:S(2)}, u32[]{:S(2)}) %collective-permute-start.9) | collective-permute-done | bytes 512 | tf_op jit(solution)/shard_map/ppermute | solution.py:34
  66.7 0.0 collective-permute-start.4
  66.7 0.0 collective-permute-done.15
  66.7 1.6 collective-permute-start.5
  68.3 1.6 cut.3
  69.9 0.0 copy-start.1
  69.9 0.8 copy-done.1
  70.7 0.7 copy-done.2
  71.4 0.7 copy-done.3
  72.1 0.7 copy-done.4
  72.9 0.0 collective-permute-done.3.refs_1_
  72.9 2.3 %collective-permute-start.10 = (bf16[1024,128]{1,0:T(8,128)(2,1)}, bf16[1024,128]{1,0:T(8,128)(2,1)S(1)}, u32[]{:S(2)}, u32[]{:S(2)}) collective-permute-start(bf16[1024,128]{1,0:T(8,128)(2,1)} %copy-done.4), channel_id=1, source_target_pairs={{0,12},{1,9},{2,14},{3,11},{4,8},{5,13},{6,10},{7,15},{8,4},{9,1},... | collective-permute-start | bytes 786440 | tf_op jit(solution)/shard_map/ppermute | solution.py:34
  75.2 31.9 %collective-permute-done.4.refs_2_ = bf16[2,1024,128]{2,1,0:T(8,128)(2,1)} collective-permute-done((bf16[2,1024,128]{2,1,0:T(8,128)(2,1)}, bf16[2,1024,128]{2,1,0:T(8,128)(2,1)}, u32[]{:S(2)}, u32[]{:S(2)}) %collective-permute-start.4) | collective-permute-done | bytes 524320 | tf_op jit(solution)/shard_map/ppermute | solution.py:34
  107.1 12.3 %collective-permute-start.22 = (bf16[1024,128]{1,0:T(8,128)(2,1)}, bf16[1024,128]{1,0:T(8,128)(2,1)S(1)}, u32[]{:S(2)}, u32[]{:S(2)}) collective-permute-start(bf16[1024,128]{1,0:T(8,128)(2,1)} %copy-done.2), channel_id=1, source_target_pairs={{0,8},{1,5},{2,10},{3,7},{4,12},{5,1},{6,14},{7,3},{8,0},{9,13},{1... | collective-permute-start | bytes 786440 | tf_op jit(solution)/shard_map/ppermute | solution.py:34
  119.4 1.6 pool.1.kv
  121.0 3.7 %attend.4 = bf16[1024,128]{1,0:T(8,128)(2,1)S(1)} custom-call(s32[8,15]{1,0:T(8,128)S(1)} %fusion.1.slots, bf16[1024,128]{1,0:T(8,128)(2,1)S(1)} %get-tuple-element.15.q_ref, bf16[2,4096,128]{2,1,0:T(8,128)(2,1)S(1)} %pool.1.kv), custom_call_target="tpu_custom_call" | custom-call | tf_op jit(solution)/shard_map/attend/pallas_call | solution.py:154
  124.7 0.0 collective-permute-done.10.q_ref
  124.7 0.1 collective-permute-start.21
  124.9 3.7 %attend.5 = bf16[1024,128]{1,0:T(8,128)(2,1)S(1)} custom-call(s32[8,15]{1,0:T(8,128)S(1)} %fusion.3.slots, bf16[1024,128]{1,0:T(8,128)(2,1)S(1)} %collective-permute-done.10.q_ref, bf16[2,4096,128]{2,1,0:T(8,128)(2,1)S(1)} %pool.1.kv), custom_call_target="tpu_custom_call" | custom-call | tf_op jit(solution)/shard_map/attend/pallas_call | solution.py:154
  128.6 0.7 collective-permute-done.21
  129.3 0.0 collective-permute-start.6
  129.3 1.6 collective-permute-start.7
  130.9 0.0 collective-permute-done.22.q_ref
  130.9 0.4 collective-permute-start.8
  131.3 0.0 collective-permute-done.6.refs_1_
  131.3 1.3 collective-permute-start.11
  132.6 3.7 %attend.6 = bf16[1024,128]{1,0:T(8,128)(2,1)S(1)} custom-call(s32[8,15]{1,0:T(8,128)S(1)} %fusion.5.slots, bf16[1024,128]{1,0:T(8,128)(2,1)S(1)} %collective-permute-done.16.q_ref, bf16[2,4096,128]{2,1,0:T(8,128)(2,1)S(1)} %pool.1.kv), custom_call_target="tpu_custom_call" | custom-call | tf_op jit(solution)/shard_map/attend/pallas_call | solution.py:154
  136.3 0.0 copy-start
  136.3 3.9 %attend.7 = bf16[1024,128]{1,0:T(8,128)(2,1)S(1)} custom-call(s32[8,15]{1,0:T(8,128)S(1)} %fusion.7.slots, bf16[1024,128]{1,0:T(8,128)(2,1)S(1)} %collective-permute-done.22.q_ref, bf16[2,4096,128]{2,1,0:T(8,128)(2,1)S(1)} %pool.1.kv), custom_call_target="tpu_custom_call" | custom-call | tf_op jit(solution)/shard_map/attend/pallas_call | solution.py:154
  140.3 0.0 collective-permute-done.7.refs_2_
  140.3 1.9 %collective-permute-start.12 = (bf16[256,128]{1,0:T(8,128)(2,1)S(1)}, bf16[256,128]{1,0:T(8,128)(2,1)S(1)}, u32[]{:S(2)}, u32[]{:S(2)}) collective-permute-start(bf16[256,128]{1,0:T(8,128)(2,1)S(1)} %get-tuple-element.35), channel_id=1, source_target_pairs={{0,13},{1,8},{2,15},{3,10},{4,9},{5,12},{6,11},{7,14},{8,5},{9,0},... | collective-permute-start | bytes 196616 | tf_op jit(solution)/shard_map/ppermute | solution.py:34
  142.2 0.0 collective-permute-done.8.refs_3_
  142.2 3.5 %collective-permute-start.13 = (bf16[256,128]{1,0:T(8,128)(2,1)S(1)}, bf16[256,128]{1,0:T(8,128)(2,1)S(1)}, u32[]{:S(2)}, u32[]{:S(2)}) collective-permute-start(bf16[256,128]{1,0:T(8,128)(2,1)S(1)} %get-tuple-element.34), channel_id=1, source_target_pairs={{0,14},{1,11},{2,12},{3,9},{4,10},{5,15},{6,8},{7,13},{8,6},{9,3},... | collective-permute-start | bytes 196616 | tf_op jit(solution)/shard_map/ppermute | solution.py:34
  145.6 0.0 collective-permute-done.11.refs_4_
  145.7 0.5 collective-permute-start.14
  146.1 0.0 collective-permute-done.12.refs_5_
  146.1 0.3 collective-permute-start.17
  146.4 3.5 %collective-permute-done.13.refs_6_ = bf16[256,128]{1,0:T(8,128)(2,1)S(1)} collective-permute-done((bf16[256,128]{1,0:T(8,128)(2,1)S(1)}, bf16[256,128]{1,0:T(8,128)(2,1)S(1)}, u32[]{:S(2)}, u32[]{:S(2)}) %collective-permute-start.13) | collective-permute-done | bytes 65568 | tf_op jit(solution)/shard_map/ppermute | solution.py:34
  149.9 1.2 collective-permute-start.18
  151.0 2.7 %collective-permute-done.14.refs_7_ = bf16[256,128]{1,0:T(8,128)(2,1)S(1)} collective-permute-done((bf16[256,128]{1,0:T(8,128)(2,1)S(1)}, bf16[256,128]{1,0:T(8,128)(2,1)S(1)}, u32[]{:S(2)}, u32[]{:S(2)}) %collective-permute-start.14) | collective-permute-done | bytes 65568 | tf_op jit(solution)/shard_map/ppermute | solution.py:34
  153.8 0.0 collective-permute-done.17.refs_8_
  153.8 1.6 collective-permute-start.20
  155.3 1.3 collective-permute-done.18.refs_9_
  156.6 0.5 collective-permute-start.23
  157.1 1.8 %collective-permute-done.19.refs_10_ = bf16[256,128]{1,0:T(8,128)(2,1)S(1)} collective-permute-done((bf16[256,128]{1,0:T(8,128)(2,1)S(1)}, bf16[256,128]{1,0:T(8,128)(2,1)S(1)}, u32[]{:S(2)}, u32[]{:S(2)}) %collective-permute-start.19) | collective-permute-done | bytes 65568 | tf_op jit(solution)/shard_map/ppermute | solution.py:34
  158.9 0.0 collective-permute-start.24
  158.9 2.4 %collective-permute-start.25 = (bf16[256,128]{1,0:T(8,128)(2,1)S(1)}, bf16[256,128]{1,0:T(8,128)(2,1)S(1)}, u32[]{:S(2)}, u32[]{:S(2)}) collective-permute-start(bf16[256,128]{1,0:T(8,128)(2,1)S(1)} %get-tuple-element.26), channel_id=1, source_target_pairs={{0,10},{1,7},{2,8},{3,5},{4,14},{5,3},{6,12},{7,1},{8,2},{9,15},{1... | collective-permute-start | bytes 196616 | tf_op jit(solution)/shard_map/ppermute | solution.py:34
  161.3 0.0 collective-permute-done.2.refs_3_
  161.3 1.7 %collective-permute-start.26 = (bf16[256,128]{1,0:T(8,128)(2,1)S(1)}, bf16[256,128]{1,0:T(8,128)(2,1)S(1)}, u32[]{:S(2)}, u32[]{:S(2)}) collective-permute-start(bf16[256,128]{1,0:T(8,128)(2,1)S(1)} %get-tuple-element.25), channel_id=1, source_target_pairs={{0,11},{1,6},{2,9},{3,4},{4,15},{5,2},{6,13},{7,0},{8,3},{9,14},{1... | collective-permute-start | bytes 196616 | tf_op jit(solution)/shard_map/ppermute | solution.py:34
  163.0 2.4 %sheaf.1.rights_ref = bf16[2048,2048]{1,0:T(8,128)(2,1)S(1)} custom-call(bf16[512,2048]{1,0:T(8,128)(2,1)S(1)} %copy-done, bf16[512,2048]{1,0:T(8,128)(2,1)} %collective-permute-done.refs_1_, bf16[512,2048]{1,0:T(8,128)(2,1)S(1)} %collective-permute-done.1.refs_2_, bf16[512,2048]{1,0:T(8,128)(2,1)} %collective-permute-done.2.refs_3_), custom_call_target="tpu_custom_call" | custom-call | tf_op jit(solution)/shard_map/sheaf/pallas_call | solution.py:188
  165.4 0.0 collective-permute-done.20.refs_11_
  165.4 1.8 %project.1.part_ref = f32[256,2048]{1,0:T(8,128)S(1)} custom-call(bf16[2048,2048]{1,0:T(8,128)(2,1)S(1)} %sheaf.1.rights_ref, bf16[256,128]{1,0:T(8,128)(2,1)S(1)} %get-tuple-element.40.refs_0_, bf16[256,128]{1,0:T(8,128)(2,1)S(1)} %collective-permute-done.6.refs_1_, bf16[256,128]{1,0:T(8,128)(2,1)S(1)} %collective-permute-done.7.refs_2_, ...), custom_call_target="tpu_custom_call" | custom-call | tf_op jit(solution)/shard_map/project/pallas_call | solution.py:228
  167.2 0.0 collective-permute-done.23.refs_0_
  167.2 0.0 collective-permute-done.24.refs_1_
  167.2 1.5 finish.1
  (21 shorter events, 0.2 us)
Async XLA Ops:
  0.0 51.9 %copy-start.5 = (s32[8,15]{1,0:T(8,128)S(1)}, s32[8,15]{1,0:T(8,128)}, u32[]{:S(2)}) copy-start(s32[8,15]{1,0:T(8,128)} %param.8) | copy-start | bytes 1444
  0.0 48.8 %collective-permute-start.1 = (bf16[512,2048]{1,0:T(8,128)(2,1)}, bf16[512,2048]{1,0:T(8,128)(2,1)S(1)}, u32[]{:S(2)}, u32[]{:S(2)}) collective-permute-start(bf16[512,2048]{1,0:T(8,128)(2,1)} %refs_0_.4), channel_id=1, source_target_pairs={{0,2},{1,3},{2,0},{3,1},{4,6},{5,7},{6,4},{7,5},{8,10},{9,11},{10,... | collective-permute-start | bytes 6291464 | tf_op jit(solution)/shard_map/ppermute | solution.py:24
  3.0 155.9 %collective-permute-start = (bf16[512,2048]{1,0:T(8,128)(2,1)}, bf16[512,2048]{1,0:T(8,128)(2,1)}, u32[]{:S(2)}, u32[]{:S(2)}) collective-permute-start(bf16[512,2048]{1,0:T(8,128)(2,1)} %refs_0_.4), channel_id=1, source_target_pairs={{0,1},{1,0},{2,3},{3,2},{4,5},{5,4},{6,7},{7,6},{8,9},{9,8},{10,11... | collective-permute-start | bytes 6291464 | tf_op jit(solution)/shard_map/ppermute | solution.py:24
  48.8 112.5 %collective-permute-start.2 = (bf16[512,2048]{1,0:T(8,128)(2,1)S(1)}, bf16[512,2048]{1,0:T(8,128)(2,1)}, u32[]{:S(2)}, u32[]{:S(2)}) collective-permute-start(bf16[512,2048]{1,0:T(8,128)(2,1)S(1)} %collective-permute-done.1.refs_2_), channel_id=1, source_target_pairs={{0,1},{1,0},{2,3},{3,2},{4,5},{5,4},{6,7},{7,6},{8,9},{9,8},{10,11... | collective-permute-start | bytes 6291464 | tf_op jit(solution)/shard_map/ppermute | solution.py:24
  50.0 22.9 %collective-permute-start.3 = (bf16[2,1024,128]{2,1,0:T(8,128)(2,1)S(1)}, bf16[2,1024,128]{2,1,0:T(8,128)(2,1)}, u32[]{:S(2)}, u32[]{:S(2)}) collective-permute-start(bf16[2,1024,128]{2,1,0:T(8,128)(2,1)S(1)} %cut.4), channel_id=1, source_target_pairs={{0,4},{1,9},{2,6},{3,11},{4,0},{5,13},{6,2},{7,15},{8,12},{9,1},{1... | collective-permute-start | bytes 1572872 | tf_op jit(solution)/shard_map/ppermute | solution.py:34
  51.9 14.8 %collective-permute-start.9 = (s32[8,15]{1,0:T(8,128)S(1)}, s32[8,15]{1,0:T(8,128)S(1)}, u32[]{:S(2)}, u32[]{:S(2)}) collective-permute-start(s32[8,15]{1,0:T(8,128)S(1)} %copy-done.5), channel_id=1, source_target_pairs={{0,12},{1,9},{2,14},{3,11},{4,8},{5,13},{6,10},{7,15},{8,4},{9,1},... | collective-permute-start | bytes 1448 | tf_op jit(solution)/shard_map/ppermute | solution.py:34
  54.3 12.3 %collective-permute-start.15 = (s32[8,15]{1,0:T(8,128)S(1)}, s32[8,15]{1,0:T(8,128)S(1)}, u32[]{:S(2)}, u32[]{:S(2)}) collective-permute-start(s32[8,15]{1,0:T(8,128)S(1)} %copy-done.5), channel_id=1, source_target_pairs={{0,4},{1,13},{2,6},{3,15},{4,0},{5,9},{6,2},{7,11},{8,12},{9,5},{1... | collective-permute-start | bytes 1448 | tf_op jit(solution)/shard_map/ppermute | solution.py:34
  66.7 40.4 %collective-permute-start.4 = (bf16[2,1024,128]{2,1,0:T(8,128)(2,1)}, bf16[2,1024,128]{2,1,0:T(8,128)(2,1)}, u32[]{:S(2)}, u32[]{:S(2)}) collective-permute-start(bf16[2,1024,128]{2,1,0:T(8,128)(2,1)} %get-tuple-element.17), channel_id=1, source_target_pairs={{0,8},{1,5},{2,10},{3,7},{4,12},{5,1},{6,14},{7,3},{8,0},{9,13},{1... | collective-permute-start | bytes 1572872 | tf_op jit(solution)/shard_map/ppermute | solution.py:34
  66.7 40.4 %collective-permute-start.5 = (bf16[2,1024,128]{2,1,0:T(8,128)(2,1)S(1)}, bf16[2,1024,128]{2,1,0:T(8,128)(2,1)}, u32[]{:S(2)}, u32[]{:S(2)}) collective-permute-start(bf16[2,1024,128]{2,1,0:T(8,128)(2,1)S(1)} %get-tuple-element.18), channel_id=1, source_target_pairs={{0,12},{1,13},{2,14},{3,15},{4,8},{5,9},{6,10},{7,11},{8,4},{9,5},... | collective-permute-start | bytes 1572872 | tf_op jit(solution)/shard_map/ppermute | solution.py:34
  69.9 0.8 copy-start.1
  70.7 0.7 copy-start.2
  71.4 0.7 copy-start.3
  72.1 0.7 copy-start.4
  72.9 51.9 %collective-permute-start.10 = (bf16[1024,128]{1,0:T(8,128)(2,1)}, bf16[1024,128]{1,0:T(8,128)(2,1)S(1)}, u32[]{:S(2)}, u32[]{:S(2)}) collective-permute-start(bf16[1024,128]{1,0:T(8,128)(2,1)} %copy-done.4), channel_id=1, source_target_pairs={{0,12},{1,9},{2,14},{3,11},{4,8},{5,13},{6,10},{7,15},{8,4},{9,1},... | collective-permute-start | bytes 786440 | tf_op jit(solution)/shard_map/ppermute | solution.py:34
  107.1 22.3 %collective-permute-start.16 = (bf16[1024,128]{1,0:T(8,128)(2,1)}, bf16[1024,128]{1,0:T(8,128)(2,1)S(1)}, u32[]{:S(2)}, u32[]{:S(2)}) collective-permute-start(bf16[1024,128]{1,0:T(8,128)(2,1)} %copy-done.3), channel_id=1, source_target_pairs={{0,4},{1,13},{2,6},{3,15},{4,0},{5,9},{6,2},{7,11},{8,12},{9,5},{1... | collective-permute-start | bytes 786440 | tf_op jit(solution)/shard_map/ppermute | solution.py:34
  107.1 23.8 %collective-permute-start.22 = (bf16[1024,128]{1,0:T(8,128)(2,1)}, bf16[1024,128]{1,0:T(8,128)(2,1)S(1)}, u32[]{:S(2)}, u32[]{:S(2)}) collective-permute-start(bf16[1024,128]{1,0:T(8,128)(2,1)} %copy-done.2), channel_id=1, source_target_pairs={{0,8},{1,5},{2,10},{3,7},{4,12},{5,1},{6,14},{7,3},{8,0},{9,13},{1... | collective-permute-start | bytes 786440 | tf_op jit(solution)/shard_map/ppermute | solution.py:34
  124.7 4.6 %collective-permute-start.21 = (s32[8,15]{1,0:T(8,128)S(1)}, s32[8,15]{1,0:T(8,128)S(1)}, u32[]{:S(2)}, u32[]{:S(2)}) collective-permute-start(s32[8,15]{1,0:T(8,128)S(1)} %copy-done.5), channel_id=1, source_target_pairs={{0,8},{1,5},{2,10},{3,7},{4,12},{5,1},{6,14},{7,3},{8,0},{9,13},{1... | collective-permute-start | bytes 1448 | tf_op jit(solution)/shard_map/ppermute | solution.py:34
  129.3 2.0 %collective-permute-start.6 = (bf16[256,128]{1,0:T(8,128)(2,1)S(1)}, bf16[256,128]{1,0:T(8,128)(2,1)S(1)}, u32[]{:S(2)}, u32[]{:S(2)}) collective-permute-start(bf16[256,128]{1,0:T(8,128)(2,1)S(1)} %get-tuple-element.39), channel_id=1, source_target_pairs={{0,1},{1,0},{2,3},{3,2},{4,5},{5,4},{6,7},{7,6},{8,9},{9,8},{10,11... | collective-permute-start | bytes 196616 | tf_op jit(solution)/shard_map/ppermute | solution.py:34
  129.3 10.9 %collective-permute-start.7 = (bf16[256,128]{1,0:T(8,128)(2,1)S(1)}, bf16[256,128]{1,0:T(8,128)(2,1)S(1)}, u32[]{:S(2)}, u32[]{:S(2)}) collective-permute-start(bf16[256,128]{1,0:T(8,128)(2,1)S(1)} %get-tuple-element.38), channel_id=1, source_target_pairs={{0,2},{1,3},{2,0},{3,1},{4,6},{5,7},{6,4},{7,5},{8,10},{9,11},{10,... | collective-permute-start | bytes 196616 | tf_op jit(solution)/shard_map/ppermute | solution.py:34
  130.9 11.3 %collective-permute-start.8 = (bf16[256,128]{1,0:T(8,128)(2,1)S(1)}, bf16[256,128]{1,0:T(8,128)(2,1)S(1)}, u32[]{:S(2)}, u32[]{:S(2)}) collective-permute-start(bf16[256,128]{1,0:T(8,128)(2,1)S(1)} %get-tuple-element.37), channel_id=1, source_target_pairs={{0,3},{1,2},{2,1},{3,0},{4,7},{5,6},{6,5},{7,4},{8,11},{9,10},{10,... | collective-permute-start | bytes 196616 | tf_op jit(solution)/shard_map/ppermute | solution.py:34
  131.3 14.4 %collective-permute-start.11 = (bf16[256,128]{1,0:T(8,128)(2,1)S(1)}, bf16[256,128]{1,0:T(8,128)(2,1)S(1)}, u32[]{:S(2)}, u32[]{:S(2)}) collective-permute-start(bf16[256,128]{1,0:T(8,128)(2,1)S(1)} %get-tuple-element.36), channel_id=1, source_target_pairs={{0,12},{1,9},{2,14},{3,11},{4,8},{5,13},{6,10},{7,15},{8,4},{9,1},... | collective-permute-start | bytes 196616 | tf_op jit(solution)/shard_map/ppermute | solution.py:34
  136.3 26.7 %copy-start = (bf16[512,2048]{1,0:T(8,128)(2,1)S(1)}, bf16[512,2048]{1,0:T(8,128)(2,1)}, u32[]{:S(2)}) copy-start(bf16[512,2048]{1,0:T(8,128)(2,1)} %refs_0_.4) | copy-start | bytes 6291460
  140.3 5.9 %collective-permute-start.12 = (bf16[256,128]{1,0:T(8,128)(2,1)S(1)}, bf16[256,128]{1,0:T(8,128)(2,1)S(1)}, u32[]{:S(2)}, u32[]{:S(2)}) collective-permute-start(bf16[256,128]{1,0:T(8,128)(2,1)S(1)} %get-tuple-element.35), channel_id=1, source_target_pairs={{0,13},{1,8},{2,15},{3,10},{4,9},{5,12},{6,11},{7,14},{8,5},{9,0},... | collective-permute-start | bytes 196616 | tf_op jit(solution)/shard_map/ppermute | solution.py:34
  142.2 7.7 %collective-permute-start.13 = (bf16[256,128]{1,0:T(8,128)(2,1)S(1)}, bf16[256,128]{1,0:T(8,128)(2,1)S(1)}, u32[]{:S(2)}, u32[]{:S(2)}) collective-permute-start(bf16[256,128]{1,0:T(8,128)(2,1)S(1)} %get-tuple-element.34), channel_id=1, source_target_pairs={{0,14},{1,11},{2,12},{3,9},{4,10},{5,15},{6,8},{7,13},{8,6},{9,3},... | collective-permute-start | bytes 196616 | tf_op jit(solution)/shard_map/ppermute | solution.py:34
  145.7 8.1 %collective-permute-start.14 = (bf16[256,128]{1,0:T(8,128)(2,1)S(1)}, bf16[256,128]{1,0:T(8,128)(2,1)S(1)}, u32[]{:S(2)}, u32[]{:S(2)}) collective-permute-start(bf16[256,128]{1,0:T(8,128)(2,1)S(1)} %get-tuple-element.33), channel_id=1, source_target_pairs={{0,15},{1,10},{2,13},{3,8},{4,11},{5,14},{6,9},{7,12},{8,7},{9,2},... | collective-permute-start | bytes 196616 | tf_op jit(solution)/shard_map/ppermute | solution.py:34
  146.1 7.6 %collective-permute-start.17 = (bf16[256,128]{1,0:T(8,128)(2,1)S(1)}, bf16[256,128]{1,0:T(8,128)(2,1)S(1)}, u32[]{:S(2)}, u32[]{:S(2)}) collective-permute-start(bf16[256,128]{1,0:T(8,128)(2,1)S(1)} %get-tuple-element.32), channel_id=1, source_target_pairs={{0,4},{1,13},{2,6},{3,15},{4,0},{5,9},{6,2},{7,11},{8,12},{9,5},{1... | collective-permute-start | bytes 196616 | tf_op jit(solution)/shard_map/ppermute | solution.py:34
  149.9 6.7 %collective-permute-start.18 = (bf16[256,128]{1,0:T(8,128)(2,1)S(1)}, bf16[256,128]{1,0:T(8,128)(2,1)S(1)}, u32[]{:S(2)}, u32[]{:S(2)}) collective-permute-start(bf16[256,128]{1,0:T(8,128)(2,1)S(1)} %get-tuple-element.31), channel_id=1, source_target_pairs={{0,5},{1,12},{2,7},{3,14},{4,1},{5,8},{6,3},{7,10},{8,13},{9,4},{1... | collective-permute-start | bytes 196616 | tf_op jit(solution)/shard_map/ppermute | solution.py:34
  153.7 5.2 %collective-permute-start.19 = (bf16[256,128]{1,0:T(8,128)(2,1)S(1)}, bf16[256,128]{1,0:T(8,128)(2,1)S(1)}, u32[]{:S(2)}, u32[]{:S(2)}) collective-permute-start(bf16[256,128]{1,0:T(8,128)(2,1)S(1)} %get-tuple-element.30), channel_id=1, source_target_pairs={{0,6},{1,15},{2,4},{3,13},{4,2},{5,11},{6,0},{7,9},{8,14},{9,7},{1... | collective-permute-start | bytes 196616 | tf_op jit(solution)/shard_map/ppermute | solution.py:34
  153.8 11.6 %collective-permute-start.20 = (bf16[256,128]{1,0:T(8,128)(2,1)S(1)}, bf16[256,128]{1,0:T(8,128)(2,1)S(1)}, u32[]{:S(2)}, u32[]{:S(2)}) collective-permute-start(bf16[256,128]{1,0:T(8,128)(2,1)S(1)} %get-tuple-element.29), channel_id=1, source_target_pairs={{0,7},{1,14},{2,5},{3,12},{4,3},{5,10},{6,1},{7,8},{8,15},{9,6},{1... | collective-permute-start | bytes 196616 | tf_op jit(solution)/shard_map/ppermute | solution.py:34
  156.6 10.6 %collective-permute-start.23 = (bf16[256,128]{1,0:T(8,128)(2,1)S(1)}, bf16[256,128]{1,0:T(8,128)(2,1)S(1)}, u32[]{:S(2)}, u32[]{:S(2)}) collective-permute-start(bf16[256,128]{1,0:T(8,128)(2,1)S(1)} %get-tuple-element.28), channel_id=1, source_target_pairs={{0,8},{1,5},{2,10},{3,7},{4,12},{5,1},{6,14},{7,3},{8,0},{9,13},{1... | collective-permute-start | bytes 196616 | tf_op jit(solution)/shard_map/ppermute | solution.py:34
  158.9 8.3 %collective-permute-start.24 = (bf16[256,128]{1,0:T(8,128)(2,1)S(1)}, bf16[256,128]{1,0:T(8,128)(2,1)S(1)}, u32[]{:S(2)}, u32[]{:S(2)}) collective-permute-start(bf16[256,128]{1,0:T(8,128)(2,1)S(1)} %get-tuple-element.27), channel_id=1, source_target_pairs={{0,9},{1,4},{2,11},{3,6},{4,13},{5,0},{6,15},{7,2},{8,1},{9,12},{1... | collective-permute-start | bytes 196616 | tf_op jit(solution)/shard_map/ppermute | solution.py:34
  158.9 8.3 %collective-permute-start.25 = (bf16[256,128]{1,0:T(8,128)(2,1)S(1)}, bf16[256,128]{1,0:T(8,128)(2,1)S(1)}, u32[]{:S(2)}, u32[]{:S(2)}) collective-permute-start(bf16[256,128]{1,0:T(8,128)(2,1)S(1)} %get-tuple-element.26), channel_id=1, source_target_pairs={{0,10},{1,7},{2,8},{3,5},{4,14},{5,3},{6,12},{7,1},{8,2},{9,15},{1... | collective-permute-start | bytes 196616 | tf_op jit(solution)/shard_map/ppermute | solution.py:34
  161.3 6.0 %collective-permute-start.26 = (bf16[256,128]{1,0:T(8,128)(2,1)S(1)}, bf16[256,128]{1,0:T(8,128)(2,1)S(1)}, u32[]{:S(2)}, u32[]{:S(2)}) collective-permute-start(bf16[256,128]{1,0:T(8,128)(2,1)S(1)} %get-tuple-element.25), channel_id=1, source_target_pairs={{0,11},{1,6},{2,9},{3,4},{4,15},{5,2},{6,13},{7,0},{8,3},{9,14},{1... | collective-permute-start | bytes 196616 | tf_op jit(solution)/shard_map/ppermute | solution.py:34
